TPU v7x, 256 devices: a whole 4x4x8 slice. The times are simulated.
256 devices in a mesh: dp: 8 (over y, x_hi), proto: 16 (over z, core), crop: 2 (over x_lo).
Axes of the slice: x: 4 (x_hi: 2, x_lo: 2; x = x_hi * 2 + x_lo), y: 4, z: 8, core: 2. Of those that a mesh axis runs over, the one named last changes fastest.
Arguments:
- embeddings: bfloat16 [2048, 2, 4, 256], P(('dp', 'proto'), 'crop'), may hold values from -2 to 2
- codes: bfloat16 [2048, 2, 65536], P('dp', 'crop', 'proto'), may hold values from 0 to 1, as said below
- prototypes: bfloat16 [16, 4096, 256], P('proto', ('dp', 'crop')), may hold values from -2 to 2
Outputs:
- grad_emb: float32 [2048, 2, 4, 256], P(('dp', 'proto'), 'crop')
- grad_proto: float32 [16, 4096, 256], P('proto', ('dp', 'crop'))
Inputs may be any that keep to these rules, and one draw needn't show every extreme that they name: `codes`: each image's code is a distribution over the prototypes: nonnegative entries that sum to about one over all 65536.
All inputs are finite; a program needn't handle non-finite values.
Results may differ from a plain program's by a relative error of at most 0.0031.
Values may be sent and summed in bfloat16 or wider, within the bound.
No kernel may reach another device: no remote copies, remote signals or barrier semaphores. Data moves between devices by JAX's collectives and lax.ppermute only.
A program may use at most 64 MiB of HBM per device.

v0:
```python
import functools

import jax
import jax.numpy as jnp
from jax import lax
from jax.experimental import pallas as pl
from jax.experimental.pallas import tpu as pltpu
from jax.sharding import PartitionSpec as P


sharpness = 10.0
epsilon = 1e-06
grad_scale = 8.0
tile = 512
side = 4
arrivals = (2, 1, 3)
f16, bf16, f32 = jnp.float16, jnp.bfloat16, jnp.float32
owners = ("dp", "crop")


def swapped(value):
    return lax.ppermute(value, "crop", [(0, 1), (1, 0)])


def exchange(value, along, mask):
    step = mask * (side if along == "y" else 1)
    return lax.ppermute(value, owners, [(owner, owner ^ step) for owner in range(side * side)])


def normalize_rows(values):
    floats = values.astype(f32)
    lengths = jnp.sqrt(jnp.sum(floats * floats, axis=-1, keepdims=True) + epsilon)
    return floats / lengths, lengths


def dot(left, right, left_dim, right_dim):
    return lax.dot_general(
        left, right, (((left_dim,), (right_dim,)), ((), ())), preferred_element_type=f32
    )


def row_weights(totals_ref, crops, own_images):
    totals = jnp.sum(totals_ref[...], axis=0)
    flat = jnp.concatenate([totals[r : r + 1] for r in range(totals.shape[0])], axis=1)
    lane = lax.broadcasted_iota(jnp.int32, flat.shape, 1)
    views = jnp.where((lane // own_images) % crops == 0, 1.0, 2.0).astype(f32)
    return views / flat


def code_columns(code_ref, columns_ref, group, index, unit):
    per_tile = tile // unit
    parts = []
    for j in range(per_tile):
        owner = columns_ref[group * side + index * per_tile + j]
        parts.append(code_ref[:, pl.ds(pl.multiple_of(owner * unit, unit), unit)])
    return jnp.concatenate(parts, axis=1)


def embeddings_kernel(raw_ref, z_t_ref, local_ref, outgoing_ref):
    z = normalize_rows(raw_ref[...])[0].astype(bf16).astype(f32)
    features = z.shape[-1]
    local = z[:, 1]
    for crop in range(2, z.shape[1]):
        local = local + z[:, crop]
    local_ref[...] = local.reshape(-1, features)
    outgoing_ref[...] = (z[:, 0] + local).reshape(-1, features)
    z_t_ref[...] = z.reshape(-1, features).T.astype(bf16)


def scores_kernel(*refs, group, unit, first, last):
    columns_ref, z_t_ref, code_ref = refs[:3]
    before = () if first else refs[3:6]
    raw_ref, exp_ref, soft_ref, own_ref, total_ref, acc_ref = refs[3 + len(before) :]
    rows = z_t_ref.shape[1]
    for ref, held in zip((soft_ref, own_ref, acc_ref), before or (None,) * 3):
        ref[...] = jnp.zeros_like(ref) if first else held[...]

    @pl.loop(0, raw_ref.shape[0] // tile)
    def _(index):
        here = pl.ds(pl.multiple_of(index * tile, tile), tile)
        c = normalize_rows(raw_ref[here])[0].astype(bf16)
        exponent = jnp.exp(dot(c, z_t_ref[...], 1, 0) * sharpness)
        acc_ref[...] += jnp.sum(exponent.reshape(-1, 8, rows), axis=0)
        exponent = exponent.astype(bf16)
        exp_ref[here] = exponent
        soft_ref[...] += dot(c, exponent, 0, 0)
        own_ref[...] += dot(code_columns(code_ref, columns_ref, group, index, unit), c, 1, 0)

    if last:
        totals = jnp.sum(acc_ref[...], axis=0, keepdims=True)
        for r in range(rows // 128):
            lanes = jnp.broadcast_to(totals[:, r * 128 : (r + 1) * 128], (total_ref.shape[0], 128))
            total_ref[:, r] = lanes
    else:
        total_ref[...] = acc_ref[...]


def prototypes_kernel(
    columns_ref, totals_ref, z_t_ref, local_ref, incoming_ref, code_ref, exp_ref, out_ref, zw_ref,
    *, group, unit, crops, own_images
):
    weights = row_weights(totals_ref, crops, own_images)
    zw_ref[...] = (z_t_ref[...].astype(f32) * weights).astype(bf16)
    target = (local_ref[...] + incoming_ref[...]).astype(bf16)

    @pl.loop(0, exp_ref.shape[0] // tile)
    def _(index):
        here = pl.ds(pl.multiple_of(index * tile, tile), tile)
        code = code_columns(code_ref, columns_ref, group, index, unit)
        grads = dot(exp_ref[here], zw_ref[...], 1, 1) - dot(code, target, 0, 0)
        out_ref[here] = grads * grad_scale


def rows_kernel(totals_ref, soft_ref, own_ref, out_ref, *, crops, own_images):
    weights = row_weights(totals_ref, crops, own_images)
    own_rows = crops * own_images
    n_proto = out_ref.shape[0]
    features = out_ref.shape[2]
    soft = (soft_ref[...] * weights).T
    out_ref[:, :own_rows] = soft.reshape(n_proto, own_rows, features)
    out_ref[:, own_rows:] = own_ref[...].reshape(n_proto, own_images, features)


def finish_kernel(total_ref, raw_ref, out_ref):
    unit_proto, length = normalize_rows(raw_ref[...])
    grad = total_ref[...] * (1.0 / grad_scale)
    along = jnp.sum(unit_proto * grad, axis=-1, keepdims=True)
    out_ref[...] = (grad - unit_proto * along) / length


def shape(*dims, dtype=f32):
    return jax.ShapeDtypeStruct(dims, dtype)


def call(kernel, out_shape, operands, mib=12, scalars=False, scratch=()):
    kept = pl.BlockSpec(memory_space=pltpu.VMEM)
    specs = [kept] * len(operands)
    if scalars:
        specs[0] = pl.BlockSpec(memory_space=pltpu.SMEM)
    return pl.pallas_call(
        kernel,
        out_shape=out_shape,
        in_specs=specs,
        out_specs=jax.tree.map(lambda _: kept, out_shape),
        scratch_shapes=scratch,
        compiler_params=pltpu.CompilerParams(vmem_limit_bytes=mib << 20),
    )(*operands)


def on_device(embeddings, codes, prototypes):
    n_proto = lax.axis_size("proto")
    own_images, _, crops, features = embeddings.shape
    images = own_images * n_proto
    rows = images * crops
    own_rows = own_images * crops
    code = codes[:, 0]
    unit = prototypes.shape[1]

    place = lax.axis_index(owners)
    near, far = jnp.arange(side), jnp.arange(side)[:, None]
    columns = (place ^ (near * side) ^ far).reshape(-1).astype(jnp.int32)

    column = {0: prototypes[0]}
    for j in (1, 3, 2):
        column[j] = exchange(prototypes[0], "y", j)

    by_crop = jnp.swapaxes(embeddings[:, 0], 0, 1)
    own_emb = by_crop.reshape(1, own_rows, features)
    raw_emb = lax.all_to_all(
        jnp.broadcast_to(own_emb, (n_proto, own_rows, features)), "proto", 0, 0
    )

    gathered = {0: jnp.concatenate([column[j] for j in range(side)])}
    for d in arrivals:
        gathered[d] = exchange(gathered[0], "x", d)

    z_t, local_sum, outgoing = call(
        embeddings_kernel,
        (shape(features, rows, dtype=bf16), shape(images, features), shape(images, features)),
        (raw_emb.reshape(n_proto, crops, own_images, features),),
    )

    exponents = {}
    state = ()
    for d in (0, *arrivals):
        last = d == arrivals[-1]
        total_dims = (n_proto, rows // 128, 128) if last else (8, rows)
        exponents[d], *state = call(
            functools.partial(scores_kernel, group=d, unit=unit, first=not state, last=last),
            [
                shape(side * unit, rows, dtype=bf16),
                shape(features, rows),
                shape(images, features),
                shape(*total_dims),
            ],
            (columns, z_t, code, *state, gathered[d]),
            scalars=True,
            scratch=[pltpu.VMEM((8, rows), f32)],
        )
    soft, own_term, totals, outgoing = lax.optimization_barrier((*state, outgoing))
    totals = lax.all_to_all(totals, "proto", 0, 0)
    incoming = swapped(outgoing)

    parts = {}
    for d in (*arrivals, 0):
        if d == 0:
            row_parts = call(
                functools.partial(rows_kernel, crops=crops, own_images=own_images),
                shape(n_proto, own_rows + own_images, features),
                (totals, soft, own_term),
            )
            row_parts = row_parts.astype(f16)
        parts[d] = call(
            functools.partial(
                prototypes_kernel, group=d, unit=unit, crops=crops, own_images=own_images
            ),
            shape(side * unit, features),
            (columns, totals, z_t, local_sum, incoming, code, exponents[d]),
            scalars=True,
            scratch=[pltpu.VMEM((features, rows), bf16)],
        )
        if d:
            parts[d] = parts[d].astype(f16)

    row_parts = lax.all_to_all(row_parts, "proto", 0, 0)

    column_sum = parts[0]
    for d in arrivals:
        column_sum = column_sum + exchange(parts[d], "x", d).astype(f32)
    column_sum = column_sum.reshape(side, unit, features)
    proto_sum = column_sum[0]
    for j in (1, 3, 2):
        part = exchange(column_sum[j].astype(f16), "y", j)
        proto_sum = proto_sum + part.astype(f32)

    row_sums = jnp.sum(row_parts.astype(f32), axis=0)
    own_code_term = row_sums[own_rows:]
    other_code_term = swapped(own_code_term)
    both = own_code_term + other_code_term
    assigned = jnp.stack([other_code_term] + [both] * (crops - 1))
    unit_emb, emb_norm = normalize_rows(by_crop)
    score_grad = (row_sums[:own_rows].reshape(crops, own_images, features) - assigned) * sharpness
    grad_emb = (
        score_grad - unit_emb * jnp.sum(unit_emb * score_grad, axis=-1, keepdims=True)
    ) / emb_norm
    grad_emb = jnp.swapaxes(grad_emb, 0, 1)[:, None]

    grad_proto = call(
        finish_kernel,
        shape(*prototypes.shape[1:]),
        (proto_sum, prototypes[0]),
    )
    return (grad_emb, grad_proto[None])


def solution(mesh):
    return jax.shard_map(
        on_device,
        mesh=mesh,
        in_specs=(
            P(("dp", "proto"), "crop", None, None),
            P("dp", "crop", "proto"),
            P("proto", ("dp", "crop"), None),
        ),
        out_specs=(P(("dp", "proto"), "crop", None, None), P("proto", ("dp", "crop"), None)),
        check_vma=False,
    )
```

profile of v0, /device:TPU:32, one launch (start us, length us, event | category | flops | bytes accessed | tf_op | source)
XLA Modules:
  0.0 124.3 jit_solution(7379292483587991986)
XLA Ops:
  2.4 8.6 %all-to-all-start = ((bf16[16,64,256]{2,1,0:T(8,128)(2,1)}), bf16[16,64,256]{2,1,0:T(8,128)(2,1)S(1)}, u32[]{:S(2)}, u32[]{:S(2)}) async-start(bf16[16,64,256]{2,1,0:T(8,128)(2,1)} %broadcast_in_dim.18), calls=%async_computation | async-start | bytes 1048576 | tf_op jit(solution)/shard_map/all_to_all | solution.py:169
  12.6 2.9 %collective-permute-start.1 = (bf16[256,256]{1,0:T(8,128)(2,1)}, bf16[256,256]{1,0:T(8,128)(2,1)S(1)}, u32[]{:S(2)}, u32[]{:S(2)}) collective-permute-start(bf16[256,256]{1,0:T(8,128)(2,1)} %bitcast.33), channel_id=1, source_target_pairs={{0,128},{1,129},{32,160},{33,161},{64,192},{65,193},{96,224},{97,2... | collective-permute-start | bytes 393224 | tf_op jit(solution)/shard_map/ppermute | solution.py:27
  17.2 4.9 %collective-permute-done.1 = bf16[256,256]{1,0:T(8,128)(2,1)S(1)} collective-permute-done((bf16[256,256]{1,0:T(8,128)(2,1)}, bf16[256,256]{1,0:T(8,128)(2,1)S(1)}, u32[]{:S(2)}, u32[]{:S(2)}) %collective-permute-start.1) | collective-permute-done | bytes 131104 | tf_op jit(solution)/shard_map/ppermute | solution.py:27
  22.1 2.2 %collective-permute-done.2 = bf16[256,256]{1,0:T(8,128)(2,1)S(1)} collective-permute-done((bf16[256,256]{1,0:T(8,128)(2,1)}, bf16[256,256]{1,0:T(8,128)(2,1)S(1)}, u32[]{:S(2)}, u32[]{:S(2)}) %collective-permute-start.2) | collective-permute-done | bytes 131104 | tf_op jit(solution)/shard_map/ppermute | solution.py:27
  24.3 1.7 %pad_maximum_fusion.refs_3_ = bf16[1024,256]{1,0:T(8,128)(2,1)} fusion(bf16[256,256]{1,0:T(8,128)(2,1)S(1)} %collective-permute-done.2, bf16[256,256]{1,0:T(8,128)(2,1)S(1)} %collective-permute-done.1, bf16[256,256]{1,0:T(8,128)(2,1)S(1)} %collective-permute-done, bf16[256,256]{1,0:T(8,128)(2,1)} %bitcast.35), kind=kLoop, calls=%fused_computation.7 | loop fusion | flops 2097152 | bytes 1048576 | tf_op jit(solution)/shard_map/concatenate | solution.py:173
  26.0 3.0 %collective-permute-start.3 = (bf16[1024,256]{1,0:T(8,128)(2,1)}, bf16[1024,256]{1,0:T(8,128)(2,1)}, u32[]{:S(2)}, u32[]{:S(2)}) collective-permute-start(bf16[1024,256]{1,0:T(8,128)(2,1)} %pad_maximum_fusion.refs_3_), channel_id=1, source_target_pairs={{0,32},{1,33},{32,0},{33,1},{64,96},{65,97},{96,64},{97,65},{128,1... | collective-permute-start | bytes 1572872 | tf_op jit(solution)/shard_map/ppermute | solution.py:27
  31.6 3.0 %shard_map.51 = (bf16[1024,1024]{1,0:T(8,128)(2,1)S(1)}, f32[256,1024]{1,0:T(8,128)S(1)}, f32[256,256]{1,0:T(8,128)S(1)}, f32[8,1024]{1,0:T(8,128)S(1)}) custom-call(s32[16]{0:T(128)S(1)} %xor.32.refs_0_.columns_ref, bf16[256,1024]{1,0:T(8,128)(2,1)S(1)} %get-tuple-element.25.refs_1_.z_t_ref, bf16[256,4096]{1,0:T(8,128)(2,1)S(1)} %bitcast.23, ...), custom_call_target="tpu_custom_call" | custom-call | tf_op jit(solution)/shard_map/pallas_call | solution.py:140
  34.6 8.1 %collective-permute-done.3.refs_6_ = bf16[1024,256]{1,0:T(8,128)(2,1)} collective-permute-done((bf16[1024,256]{1,0:T(8,128)(2,1)}, bf16[1024,256]{1,0:T(8,128)(2,1)}, u32[]{:S(2)}, u32[]{:S(2)}) %collective-permute-start.3) | collective-permute-done | bytes 524320 | tf_op jit(solution)/shard_map/ppermute | solution.py:27
  42.7 3.0 %shard_map.52 = (bf16[1024,1024]{1,0:T(8,128)(2,1)S(1)}, f32[256,1024]{1,0:T(8,128)S(1)}, f32[256,256]{1,0:T(8,128)S(1)}, f32[8,1024]{1,0:T(8,128)S(1)}) custom-call(s32[16]{0:T(128)S(1)} %xor.32.refs_0_.columns_ref, bf16[256,1024]{1,0:T(8,128)(2,1)S(1)} %get-tuple-element.25.refs_1_.z_t_ref, bf16[256,4096]{1,0:T(8,128)(2,1)S(1)} %bitcast.24, ...), custom_call_target="tpu_custom_call" | custom-call | tf_op jit(solution)/shard_map/pallas_call | solution.py:140
  47.0 5.6 %collective-permute-done.4.refs_6_ = bf16[1024,256]{1,0:T(8,128)(2,1)} collective-permute-done((bf16[1024,256]{1,0:T(8,128)(2,1)}, bf16[1024,256]{1,0:T(8,128)(2,1)}, u32[]{:S(2)}, u32[]{:S(2)}) %collective-permute-start.4) | collective-permute-done | bytes 524320 | tf_op jit(solution)/shard_map/ppermute | solution.py:27
  52.6 3.0 %shard_map.53 = (bf16[1024,1024]{1,0:T(8,128)(2,1)S(1)}, f32[256,1024]{1,0:T(8,128)S(1)}, f32[256,256]{1,0:T(8,128)S(1)}, f32[8,1024]{1,0:T(8,128)S(1)}) custom-call(s32[16]{0:T(128)S(1)} %xor.32.refs_0_.columns_ref, bf16[256,1024]{1,0:T(8,128)(2,1)S(1)} %get-tuple-element.25.refs_1_.z_t_ref, bf16[256,4096]{1,0:T(8,128)(2,1)S(1)} %bitcast.25, ...), custom_call_target="tpu_custom_call" | custom-call | tf_op jit(solution)/shard_map/pallas_call | solution.py:140
  55.6 3.4 %shard_map.54 = (bf16[1024,1024]{1,0:T(8,128)(2,1)S(1)}, f32[256,1024]{1,0:T(8,128)S(1)}, f32[256,256]{1,0:T(8,128)S(1)}, f32[16,8,128]{2,1,0:T(8,128)S(1)}) custom-call(s32[16]{0:T(128)S(1)} %xor.32.refs_0_.columns_ref, bf16[256,1024]{1,0:T(8,128)(2,1)S(1)} %get-tuple-element.25.refs_1_.z_t_ref, bf16[256,4096]{1,0:T(8,128)(2,1)S(1)} %bitcast.26, ...), custom_call_target="tpu_custom_call" | custom-call | tf_op jit(solution)/shard_map/pallas_call | solution.py:140
  61.9 13.5 %all_to_all.15.totals_ref = f32[16,8,128]{2,1,0:T(8,128)S(1)} all-to-all(f32[16,8,128]{2,1,0:T(8,128)S(1)} %get-tuple-element.39), channel_id=1, replica_groups=mesh['dp'=8,'proto'=16,'crop'=2] {'proto'}, dimensions={0} | all-to-all | bytes 131072 | tf_op jit(solution)/shard_map/all_to_all | solution.py:201
  76.7 5.4 %all-to-all-start.2 = ((f16[16,80,256]{2,1,0:T(8,128)(2,1)}), f16[16,80,256]{2,1,0:T(8,128)(2,1)}, u32[]{:S(2)}, u32[]{:S(2)}) async-start(f16[16,80,256]{2,1,0:T(8,128)(2,1)} %convert_element_type.39), calls=%async_computation.2 | async-start | bytes 1310720 | tf_op jit(solution)/shard_map/all_to_all | solution.py:225
  83.7 1.8 %shard_map.57 = f32[1024,256]{1,0:T(8,128)S(1)} custom-call(s32[16]{0:T(128)S(1)} %xor.32.refs_0_.columns_ref, f32[16,8,128]{2,1,0:T(8,128)S(1)} %all_to_all.15.totals_ref, bf16[256,1024]{1,0:T(8,128)(2,1)S(1)} %get-tuple-element.25.refs_1_.z_t_ref, f32[256,256]{1,0:T(8,128)S(1)} %get-tuple-element.42.local_ref, ...), custom_call_target="tpu_custom_call" | custom-call | tf_op jit(solution)/shard_map/pallas_call | solution.py:140
  86.2 1.8 %shard_map.58 = f32[1024,256]{1,0:T(8,128)S(1)} custom-call(s32[16]{0:T(128)S(1)} %xor.32.refs_0_.columns_ref, f32[16,8,128]{2,1,0:T(8,128)S(1)} %all_to_all.15.totals_ref, bf16[256,1024]{1,0:T(8,128)(2,1)S(1)} %get-tuple-element.25.refs_1_.z_t_ref, f32[256,256]{1,0:T(8,128)S(1)} %get-tuple-element.42.local_ref, ...), custom_call_target="tpu_custom_call" | custom-call | tf_op jit(solution)/shard_map/pallas_call | solution.py:140
  88.1 1.7 %collective-permute-start.9 = (f16[1024,256]{1,0:T(8,128)(2,1)S(1)}, f16[1024,256]{1,0:T(8,128)(2,1)S(1)}, u32[]{:S(2)}, u32[]{:S(2)}) collective-permute-start(f16[1024,256]{1,0:T(8,128)(2,1)S(1)} %convert_element_type.44), channel_id=1, source_target_pairs={{0,1},{1,0},{32,33},{33,32},{64,65},{65,64},{96,97},{97,96},{128,1... | collective-permute-start | bytes 1572872 | tf_op jit(solution)/shard_map/ppermute | solution.py:27
  89.8 1.8 %shard_map.59 = f32[1024,256]{1,0:T(8,128)S(1)} custom-call(s32[16]{0:T(128)S(1)} %xor.32.refs_0_.columns_ref, f32[16,8,128]{2,1,0:T(8,128)S(1)} %all_to_all.15.totals_ref, bf16[256,1024]{1,0:T(8,128)(2,1)S(1)} %get-tuple-element.25.refs_1_.z_t_ref, f32[256,256]{1,0:T(8,128)S(1)} %get-tuple-element.42.local_ref, ...), custom_call_target="tpu_custom_call" | custom-call | tf_op jit(solution)/shard_map/pallas_call | solution.py:140
  91.7 2.2 %collective-permute-start.10 = (f16[1024,256]{1,0:T(8,128)(2,1)S(1)}, f16[1024,256]{1,0:T(8,128)(2,1)S(1)}, u32[]{:S(2)}, u32[]{:S(2)}) collective-permute-start(f16[1024,256]{1,0:T(8,128)(2,1)S(1)} %convert_element_type.46), channel_id=1, source_target_pairs={{0,33},{1,32},{32,1},{33,0},{64,97},{65,96},{96,65},{97,64},{128,1... | collective-permute-start | bytes 1572872 | tf_op jit(solution)/shard_map/ppermute | solution.py:27
  94.0 1.8 %shard_map.56 = f32[1024,256]{1,0:T(8,128)S(1)} custom-call(s32[16]{0:T(128)S(1)} %xor.32.refs_0_.columns_ref, f32[16,8,128]{2,1,0:T(8,128)S(1)} %all_to_all.15.totals_ref, bf16[256,1024]{1,0:T(8,128)(2,1)S(1)} %get-tuple-element.25.refs_1_.z_t_ref, f32[256,256]{1,0:T(8,128)S(1)} %get-tuple-element.42.local_ref, ...), custom_call_target="tpu_custom_call" | custom-call | tf_op jit(solution)/shard_map/pallas_call | solution.py:140
  95.7 6.3 %collective-permute-done.8 = f16[1024,256]{1,0:T(8,128)(2,1)S(1)} collective-permute-done((f16[1024,256]{1,0:T(8,128)(2,1)S(1)}, f16[1024,256]{1,0:T(8,128)(2,1)S(1)}, u32[]{:S(2)}, u32[]{:S(2)}) %collective-permute-start.8) | collective-permute-done | bytes 524320 | tf_op jit(solution)/shard_map/ppermute | solution.py:27
  102.0 8.9 %collective-permute-done.9 = f16[1024,256]{1,0:T(8,128)(2,1)S(1)} collective-permute-done((f16[1024,256]{1,0:T(8,128)(2,1)S(1)}, f16[1024,256]{1,0:T(8,128)(2,1)S(1)}, u32[]{:S(2)}, u32[]{:S(2)}) %collective-permute-start.9) | collective-permute-done | bytes 524320 | tf_op jit(solution)/shard_map/ppermute | solution.py:27
  113.6 3.3 %collective-permute-start.13 = (f16[256,256]{1,0:T(8,128)(2,1)S(1)}, f16[256,256]{1,0:T(8,128)(2,1)S(1)}, u32[]{:S(2)}, u32[]{:S(2)}) collective-permute-start(f16[256,256]{1,0:T(8,128)(2,1)S(1)} %get-tuple-element.53), channel_id=1, source_target_pairs={{0,128},{1,129},{32,160},{33,161},{64,192},{65,193},{96,224},{97,2... | collective-permute-start | bytes 393224 | tf_op jit(solution)/shard_map/ppermute | solution.py:27
  119.2 3.2 %collective-permute-done.12 = f16[256,256]{1,0:T(8,128)(2,1)S(1)} collective-permute-done((f16[256,256]{1,0:T(8,128)(2,1)S(1)}, f16[256,256]{1,0:T(8,128)(2,1)S(1)}, u32[]{:S(2)}, u32[]{:S(2)}) %collective-permute-start.12) | collective-permute-done | bytes 131104 | tf_op jit(solution)/shard_map/ppermute | solution.py:27
  (63 shorter events, 22.5 us)
Async XLA Ops:
  0.6 30.9 %copy-start = (bf16[256,1,4096]{2,0,1:T(8,128)(2,1)S(1)}, bf16[256,1,4096]{2,0,1:T(8,128)(2,1)}, u32[]{:S(2)}) copy-start(bf16[256,1,4096]{2,0,1:T(8,128)(2,1)} %param.4) | copy-start | bytes 6291460
  2.4 27.9 %all-to-all-start = ((bf16[16,64,256]{2,1,0:T(8,128)(2,1)}), bf16[16,64,256]{2,1,0:T(8,128)(2,1)S(1)}, u32[]{:S(2)}, u32[]{:S(2)}) async-start(bf16[16,64,256]{2,1,0:T(8,128)(2,1)} %broadcast_in_dim.18), calls=%async_computation | async-start | bytes 1048576 | tf_op jit(solution)/shard_map/all_to_all | solution.py:169
  11.0 6.2 %collective-permute-start = (bf16[256,256]{1,0:T(8,128)(2,1)}, bf16[256,256]{1,0:T(8,128)(2,1)S(1)}, u32[]{:S(2)}, u32[]{:S(2)}) collective-permute-start(bf16[256,256]{1,0:T(8,128)(2,1)} %bitcast.32), channel_id=1, source_target_pairs={{0,64},{1,65},{32,96},{33,97},{64,0},{65,1},{96,32},{97,33},{128,1... | collective-permute-start | bytes 393224 | tf_op jit(solution)/shard_map/ppermute | solution.py:27
  12.6 9.5 %collective-permute-start.1 = (bf16[256,256]{1,0:T(8,128)(2,1)}, bf16[256,256]{1,0:T(8,128)(2,1)S(1)}, u32[]{:S(2)}, u32[]{:S(2)}) collective-permute-start(bf16[256,256]{1,0:T(8,128)(2,1)} %bitcast.33), channel_id=1, source_target_pairs={{0,128},{1,129},{32,160},{33,161},{64,192},{65,193},{96,224},{97,2... | collective-permute-start | bytes 393224 | tf_op jit(solution)/shard_map/ppermute | solution.py:27
  15.5 8.8 %collective-permute-start.2 = (bf16[256,256]{1,0:T(8,128)(2,1)}, bf16[256,256]{1,0:T(8,128)(2,1)S(1)}, u32[]{:S(2)}, u32[]{:S(2)}) collective-permute-start(bf16[256,256]{1,0:T(8,128)(2,1)} %bitcast.34), channel_id=1, source_target_pairs={{0,192},{1,193},{32,224},{33,225},{64,128},{65,129},{96,160},{97,1... | collective-permute-start | bytes 393224 | tf_op jit(solution)/shard_map/ppermute | solution.py:27
  26.0 16.7 %collective-permute-start.3 = (bf16[1024,256]{1,0:T(8,128)(2,1)}, bf16[1024,256]{1,0:T(8,128)(2,1)}, u32[]{:S(2)}, u32[]{:S(2)}) collective-permute-start(bf16[1024,256]{1,0:T(8,128)(2,1)} %pad_maximum_fusion.refs_3_), channel_id=1, source_target_pairs={{0,32},{1,33},{32,0},{33,1},{64,96},{65,97},{96,64},{97,65},{128,1... | collective-permute-start | bytes 1572872 | tf_op jit(solution)/shard_map/ppermute | solution.py:27
  29.1 23.5 %collective-permute-start.4 = (bf16[1024,256]{1,0:T(8,128)(2,1)}, bf16[1024,256]{1,0:T(8,128)(2,1)}, u32[]{:S(2)}, u32[]{:S(2)}) collective-permute-start(bf16[1024,256]{1,0:T(8,128)(2,1)} %pad_maximum_fusion.refs_3_), channel_id=1, source_target_pairs={{0,1},{1,0},{32,33},{33,32},{64,65},{65,64},{96,97},{97,96},{128,1... | collective-permute-start | bytes 1572872 | tf_op jit(solution)/shard_map/ppermute | solution.py:27
  29.7 26.0 %collective-permute-start.5 = (bf16[1024,256]{1,0:T(8,128)(2,1)}, bf16[1024,256]{1,0:T(8,128)(2,1)}, u32[]{:S(2)}, u32[]{:S(2)}) collective-permute-start(bf16[1024,256]{1,0:T(8,128)(2,1)} %pad_maximum_fusion.refs_3_), channel_id=1, source_target_pairs={{0,33},{1,32},{32,1},{33,0},{64,97},{65,96},{96,65},{97,64},{128,1... | collective-permute-start | bytes 1572872 | tf_op jit(solution)/shard_map/ppermute | solution.py:27
  34.6 11.2 %copy-start.1 = (bf16[1024,1024]{1,0:T(8,128)(2,1)}, bf16[1024,1024]{1,0:T(8,128)(2,1)S(1)}, u32[]{:S(2)}) copy-start(bf16[1024,1024]{1,0:T(8,128)(2,1)S(1)} %get-tuple-element.44.exp_ref) | copy-start | bytes 6291460
  55.6 3.5 %copy-start.5 = (bf16[1024,1024]{1,0:T(8,128)(2,1)}, bf16[1024,1024]{1,0:T(8,128)(2,1)S(1)}, u32[]{:S(2)}) copy-start(bf16[1024,1024]{1,0:T(8,128)(2,1)S(1)} %get-tuple-element.46.exp_ref) | copy-start | bytes 6291460
  60.5 21.6 %collective-permute-start.7 = (f32[256,256]{1,0:T(8,128)}, f32[256,256]{1,0:T(8,128)S(1)}, u32[]{:S(2)}, u32[]{:S(2)}) collective-permute-start(f32[256,256]{1,0:T(8,128)} %get-tuple-element.43), channel_id=1, source_target_pairs={{0,1},{1,0},{2,3},{3,2},{4,5},{5,4},{6,7},{7,6},{8,9},{9,8},{10,11... | collective-permute-start | bytes 786440 | tf_op jit(solution)/shard_map/ppermute | solution.py:22
  76.7 40.2 %all-to-all-start.2 = ((f16[16,80,256]{2,1,0:T(8,128)(2,1)}), f16[16,80,256]{2,1,0:T(8,128)(2,1)}, u32[]{:S(2)}, u32[]{:S(2)}) async-start(f16[16,80,256]{2,1,0:T(8,128)(2,1)} %convert_element_type.39), calls=%async_computation.2 | async-start | bytes 1310720 | tf_op jit(solution)/shard_map/all_to_all | solution.py:225
  83.7 2.5 %copy-start.6 = (bf16[1024,1024]{1,0:T(8,128)(2,1)S(1)}, bf16[1024,1024]{1,0:T(8,128)(2,1)}, u32[]{:S(2)}) copy-start(bf16[1024,1024]{1,0:T(8,128)(2,1)} %copy-done.5) | copy-start | bytes 6291460
  85.6 16.4 %collective-permute-start.8 = (f16[1024,256]{1,0:T(8,128)(2,1)S(1)}, f16[1024,256]{1,0:T(8,128)(2,1)S(1)}, u32[]{:S(2)}, u32[]{:S(2)}) collective-permute-start(f16[1024,256]{1,0:T(8,128)(2,1)S(1)} %convert_element_type.42), channel_id=1, source_target_pairs={{0,32},{1,33},{32,0},{33,1},{64,96},{65,97},{96,64},{97,65},{128,1... | collective-permute-start | bytes 1572872 | tf_op jit(solution)/shard_map/ppermute | solution.py:27
  86.2 3.6 %copy-start.8 = (bf16[1024,1024]{1,0:T(8,128)(2,1)S(1)}, bf16[1024,1024]{1,0:T(8,128)(2,1)}, u32[]{:S(2)}) copy-start(bf16[1024,1024]{1,0:T(8,128)(2,1)} %copy-done.7) | copy-start | bytes 6291460
  88.1 22.8 %collective-permute-start.9 = (f16[1024,256]{1,0:T(8,128)(2,1)S(1)}, f16[1024,256]{1,0:T(8,128)(2,1)S(1)}, u32[]{:S(2)}, u32[]{:S(2)}) collective-permute-start(f16[1024,256]{1,0:T(8,128)(2,1)S(1)} %convert_element_type.44), channel_id=1, source_target_pairs={{0,1},{1,0},{32,33},{33,32},{64,65},{65,64},{96,97},{97,96},{128,1... | collective-permute-start | bytes 1572872 | tf_op jit(solution)/shard_map/ppermute | solution.py:27
  89.8 4.1 %copy-start.10 = (bf16[16,1,4,256]{3,2,1,0:T(4,128)(2,1)S(1)}, bf16[16,1,4,256]{3,2,1,0:T(4,128)(2,1)}, u32[]{:S(2)}) copy-start(bf16[16,1,4,256]{3,2,1,0:T(4,128)(2,1)} %param.3) | copy-start | bytes 98308
  89.8 4.2 %copy-start.2 = (bf16[1024,1024]{1,0:T(8,128)(2,1)S(1)}, bf16[1024,1024]{1,0:T(8,128)(2,1)}, u32[]{:S(2)}) copy-start(bf16[1024,1024]{1,0:T(8,128)(2,1)} %copy-done.1) | copy-start | bytes 6291460
  91.7 20.7 %collective-permute-start.10 = (f16[1024,256]{1,0:T(8,128)(2,1)S(1)}, f16[1024,256]{1,0:T(8,128)(2,1)S(1)}, u32[]{:S(2)}, u32[]{:S(2)}) collective-permute-start(f16[1024,256]{1,0:T(8,128)(2,1)S(1)} %convert_element_type.46), channel_id=1, source_target_pairs={{0,33},{1,32},{32,1},{33,0},{64,97},{65,96},{96,65},{97,64},{128,1... | collective-permute-start | bytes 1572872 | tf_op jit(solution)/shard_map/ppermute | solution.py:27
  112.6 9.8 %copy-start.9 = (bf16[1,256,256]{2,1,0:T(8,128)(2,1)S(1)}, bf16[1,256,256]{2,1,0:T(8,128)(2,1)}, u32[]{:S(2)}) copy-start(bf16[1,256,256]{2,1,0:T(8,128)(2,1)} %param.5) | copy-start | bytes 393220
  112.7 6.4 %collective-permute-start.11 = (f16[256,256]{1,0:T(8,128)(2,1)S(1)}, f16[256,256]{1,0:T(8,128)(2,1)S(1)}, u32[]{:S(2)}, u32[]{:S(2)}) collective-permute-start(f16[256,256]{1,0:T(8,128)(2,1)S(1)} %get-tuple-element.52), channel_id=1, source_target_pairs={{0,64},{1,65},{32,96},{33,97},{64,0},{65,1},{96,32},{97,33},{128,1... | collective-permute-start | bytes 393224 | tf_op jit(solution)/shard_map/ppermute | solution.py:27
  112.8 9.5 %collective-permute-start.12 = (f16[256,256]{1,0:T(8,128)(2,1)S(1)}, f16[256,256]{1,0:T(8,128)(2,1)S(1)}, u32[]{:S(2)}, u32[]{:S(2)}) collective-permute-start(f16[256,256]{1,0:T(8,128)(2,1)S(1)} %get-tuple-element.54), channel_id=1, source_target_pairs={{0,192},{1,193},{32,224},{33,225},{64,128},{65,129},{96,160},{97,1... | collective-permute-start | bytes 393224 | tf_op jit(solution)/shard_map/ppermute | solution.py:27
  113.6 8.8 %collective-permute-start.13 = (f16[256,256]{1,0:T(8,128)(2,1)S(1)}, f16[256,256]{1,0:T(8,128)(2,1)S(1)}, u32[]{:S(2)}, u32[]{:S(2)}) collective-permute-start(f16[256,256]{1,0:T(8,128)(2,1)S(1)} %get-tuple-element.53), channel_id=1, source_target_pairs={{0,128},{1,129},{32,160},{33,161},{64,192},{65,193},{96,224},{97,2... | collective-permute-start | bytes 393224 | tf_op jit(solution)/shard_map/ppermute | solution.py:27
  118.1 5.3 %collective-permute-start.6 = (f32[16,256]{1,0:T(8,128)S(1)}, f32[16,256]{1,0:T(8,128)S(1)}, u32[]{:S(2)}, u32[]{:S(2)}) collective-permute-start(f32[16,256]{1,0:T(8,128)S(1)} %slice.32), channel_id=1, source_target_pairs={{0,1},{1,0},{2,3},{3,2},{4,5},{5,4},{6,7},{7,6},{8,9},{9,8},{10,11... | collective-permute-start | bytes 49160 | tf_op jit(solution)/shard_map/ppermute | solution.py:22
  (3 other events, 4.3 us)
where the time goes:
time: 126 us; the launch traced here: 124 us
  waiting for transfers between devices  42.5 us (34%)
  starting transfers between devices  33.7 us (27%)
  Pallas kernels  22 us (17%)
  blocking collectives  13.5 us (11%)
  local copies, waits for them, and re-layouts  6.92 us (5%)
  other arithmetic  4.78 us (4%)
    ppermute x12, waiting for transfers between devices, exchange(): lax.ppermute(value, owners, [(owner, owner ^ step) for owner in range(sid...  42.5 us
    pallas_call x11, Pallas kernels, call(): pl.pallas_call(kernel, out_shape=out_shape, in_specs=specs, out_specs=jax...  22 us
    ppermute x12, starting transfers between devices, exchange(): lax.ppermute(value, owners, [(owner, owner ^ step) for owner in range(sid...  17.6 us
    all_to_all x1, blocking collectives, on_device(): totals = lax.all_to_all(totals, 'proto', 0, 0)  13.5 us
    all_to_all x1, starting transfers between devices, on_device(): lax.all_to_all(jnp.broadcast_to(own_emb, (n_proto, own_rows, features)),...  8.59 us
    unnamed x24, local copies, waits for them, and re-layouts  5.89 us
    all_to_all x1, starting transfers between devices, on_device(): row_parts = lax.all_to_all(row_parts, 'proto', 0, 0)  5.39 us
  transfers between devices with their start and end apart: 16, of which 10 were waited for; matrix products, arithmetic and copies ran while one was open for 4% of the time, Pallas kernels for 15%

commit v1 on v0

v1 whole, which is shorter than its diff:
```python
import functools

import jax
import jax.numpy as jnp
from jax import lax
from jax.experimental import pallas as pl
from jax.experimental.pallas import tpu as pltpu
from jax.sharding import PartitionSpec as P


sharpness = 10.0
epsilon = 1e-06
side = 4
near = (0, 1, 3, 2)
arrivals = (2, 1, 3)
kinds = (0, 1)
bf16, f32 = jnp.bfloat16, jnp.float32
owners = ("dp", "crop")


def swapped(value):
    return lax.ppermute(value, "crop", [(0, 1), (1, 0)])


def mask_of(axis, distance):
    return distance * side if axis == 0 else distance


def exchange(value, axis, distance):
    mask = mask_of(axis, distance)
    return lax.ppermute(value, owners, [(owner, owner ^ mask) for owner in range(side * side)])


def normalize_rows(values):
    floats = values.astype(f32)
    lengths = jnp.sqrt(jnp.sum(floats * floats, axis=-1, keepdims=True) + epsilon)
    return floats / lengths, lengths


def dot(left, right, left_dim, right_dim):
    return lax.dot_general(
        left, right, (((left_dim,), (right_dim,)), ((), ())), preferred_element_type=f32
    )


def row_weights(totals_ref, crops, own_images):
    totals = jnp.sum(totals_ref[...], axis=0)
    flat = jnp.concatenate([totals[r : r + 1] for r in range(totals.shape[0])], axis=1)
    lane = lax.broadcasted_iota(jnp.int32, flat.shape, 1)
    views = jnp.where((lane // own_images) % crops == 0, 1.0, 2.0).astype(f32)
    return views / flat


def code_columns(code_ref, kind, distance):
    place = lax.axis_index(owners)
    half = code_ref.shape[1] // (2 * side * side)
    parts = []
    for j in near:
        owner = place ^ (mask_of(kind, j) + mask_of(1 - kind, distance))
        first = pl.multiple_of((owner * 2 + kind) * half, half)
        parts.append(code_ref[:, pl.ds(first, half)])
    return jnp.concatenate(parts, axis=1)


def embeddings_kernel(raw_ref, z_t_ref, local_ref, outgoing_ref):
    z = normalize_rows(raw_ref[...])[0].astype(bf16).astype(f32)
    features = z.shape[-1]
    local = z[:, 1]
    for crop in range(2, z.shape[1]):
        local = local + z[:, crop]
    local_ref[...] = local.reshape(-1, features)
    outgoing_ref[...] = (z[:, 0] + local).reshape(-1, features)
    z_t_ref[...] = z.reshape(-1, features).T.astype(bf16)


def scores_kernel(*refs, distance, first, last):
    z_t_ref, code_ref = refs[:2]
    before = () if first else refs[2:5]
    refs = refs[2 + len(before) :]
    raw_refs, exp_refs, (soft_ref, own_ref, total_ref) = refs[:2], refs[2:4], refs[4:]
    rows = z_t_ref.shape[1]
    soft, own, acc = (None, None, None) if first else (ref[...] for ref in before)
    add = lambda a, b: b if a is None else a + b
    for kind in kinds:
        c = normalize_rows(raw_refs[kind][...])[0].astype(bf16)
        exponent = jnp.exp(dot(c, z_t_ref[...], 1, 0) * sharpness)
        acc = add(acc, jnp.sum(exponent.reshape(-1, 8, rows), axis=0))
        exponent = exponent.astype(bf16)
        exp_refs[kind][...] = exponent
        soft = add(soft, dot(c, exponent, 0, 0))
        own = add(own, dot(code_columns(code_ref, kind, distance), c, 1, 0))
    soft_ref[...] = soft
    own_ref[...] = own
    if last:
        totals = jnp.sum(acc, axis=0, keepdims=True)
        for r in range(rows // 128):
            lanes = jnp.broadcast_to(totals[:, r * 128 : (r + 1) * 128], (total_ref.shape[0], 128))
            total_ref[:, r] = lanes
    else:
        total_ref[...] = acc


def prototypes_kernel(
    totals_ref, z_t_ref, local_ref, incoming_ref, code_ref, exp_a_ref, exp_b_ref, *out_refs,
    distance, crops, own_images
):
    weights = row_weights(totals_ref, crops, own_images)
    zw = (z_t_ref[...].astype(f32) * weights).astype(bf16)
    target = (local_ref[...] + incoming_ref[...]).astype(bf16)
    for kind, exp_ref, out_ref in zip(kinds, (exp_a_ref, exp_b_ref), out_refs):
        code = code_columns(code_ref, kind, distance)
        grads = dot(exp_ref[...], zw, 1, 1) - dot(code, target, 0, 0)
        out_ref[...] = grads.astype(out_ref.dtype)


def rows_kernel(totals_ref, soft_ref, own_ref, other_ref, out_ref, *, crops, own_images):
    weights = row_weights(totals_ref, crops, own_images)
    n_proto = out_ref.shape[0]
    features = out_ref.shape[3]
    soft = (soft_ref[...] * weights).T.reshape(n_proto, crops, own_images, features)
    own = own_ref[...].reshape(n_proto, own_images, features)
    other = other_ref[...].reshape(n_proto, own_images, features)
    for crop in range(crops):
        assigned = other if crop == 0 else own + other
        out_ref[:, crop] = ((soft[:, crop] - assigned) * sharpness).astype(bf16)


def finish_rows_kernel(parts_ref, raw_ref, out_ref):
    score_grad = jnp.sum(parts_ref[...].astype(f32), axis=0)
    unit, length = normalize_rows(raw_ref[...])
    grad = (score_grad - unit * jnp.sum(unit * score_grad, axis=-1, keepdims=True)) / length
    for crop in range(grad.shape[0]):
        out_ref[:, crop] = grad[crop]


def far_sum_kernel(held_ref, *refs):
    parts, (keep_ref, send_ref) = refs[:-2], refs[-2:]
    total = held_ref[...]
    for part in parts:
        total = total + part[...].astype(f32)
    half = total.shape[0] // 2
    keep_ref[...] = total[:half]
    send_ref[...] = total[half:].astype(bf16)


def near_sum_kernel(held_ref, part_ref, keep_ref, send_ref):
    total = held_ref[...] + part_ref[...].astype(f32)
    half = total.shape[0] // 2
    keep_ref[...] = total[:half]
    send_ref[...] = total[half:].astype(bf16)


def finish_kernel(held_a_ref, part_a_ref, held_b_ref, part_b_ref, raw_ref, out_ref):
    half = held_a_ref.shape[0]
    for kind, held, part in ((0, held_a_ref, part_a_ref), (1, held_b_ref, part_b_ref)):
        here = pl.ds(kind * half, half)
        grad = held[...] + part[...].astype(f32)
        unit, length = normalize_rows(raw_ref[here])
        along = jnp.sum(unit * grad, axis=-1, keepdims=True)
        out_ref[here] = (grad - unit * along) / length


def shape(*dims, dtype=f32):
    return jax.ShapeDtypeStruct(dims, dtype)


def call(kernel, out_shape, *operands, mib=12):
    kept = pl.BlockSpec(memory_space=pltpu.VMEM)
    return pl.pallas_call(
        kernel,
        out_shape=out_shape,
        in_specs=[kept] * len(operands),
        out_specs=jax.tree.map(lambda _: kept, out_shape),
        compiler_params=pltpu.CompilerParams(vmem_limit_bytes=mib << 20),
    )(*operands)


def on_device(embeddings, codes, prototypes):
    n_proto = lax.axis_size("proto")
    own_images, _, crops, features = embeddings.shape
    images = own_images * n_proto
    rows = images * crops
    own_rows = own_images * crops
    code = codes[:, 0]
    half = prototypes.shape[1] // 2

    by_crop = jnp.swapaxes(embeddings[:, 0], 0, 1)
    halves = [prototypes[0, :half], prototypes[0, half:]]
    for step, distance in enumerate((1, 3)):
        moved = []
        for kind in kinds:
            moved.append(exchange(halves[kind], kind, distance))
        halves = [jnp.concatenate(pair) for pair in zip(halves, moved)]
        if step == 0:
            own_emb = by_crop.reshape(1, own_rows, features)
            raw_emb = lax.all_to_all(
                jnp.broadcast_to(own_emb, (n_proto, own_rows, features)), "proto", 0, 0
            )
    gathered = {0: halves}
    for d in arrivals:
        gathered[d] = []
        for kind in kinds:
            gathered[d].append(exchange(halves[kind], 1 - kind, d))

    z_t, local_sum, outgoing = call(
        embeddings_kernel,
        (shape(features, rows, dtype=bf16), shape(images, features), shape(images, features)),
        raw_emb.reshape(n_proto, crops, own_images, features),
    )

    exponents = {}
    state = ()
    for d in (0, *arrivals):
        last = d == arrivals[-1]
        total_dims = (n_proto, rows // 128, 128) if last else (8, rows)
        *exponents[d], soft, own_term, totals = call(
            functools.partial(scores_kernel, distance=d, first=not state, last=last),
            [shape(side * half, rows, dtype=bf16)] * 2
            + [shape(features, rows), shape(images, features), shape(*total_dims)],
            z_t, code, *state, *gathered[d],
        )
        state = (soft, own_term, totals)
    totals, outgoing = lax.optimization_barrier((totals, outgoing))
    incoming = swapped(outgoing)
    totals = lax.all_to_all(totals, "proto", 0, 0)
    own_term, totals = lax.optimization_barrier((own_term, totals))
    other_term = swapped(own_term)

    arrived = [[], []]
    for d in (*arrivals, 0):
        parts = call(
            functools.partial(prototypes_kernel, distance=d, crops=crops, own_images=own_images),
            [shape(side * half, features, dtype=bf16 if d else f32)] * 2,
            totals, z_t, local_sum, incoming, code, *exponents[d],
        )
        for kind in kinds:
            if d:
                arrived[kind].append(exchange(parts[kind], 1 - kind, d))
            else:
                arrived[kind].insert(0, parts[kind])

    row_parts = call(
        functools.partial(rows_kernel, crops=crops, own_images=own_images),
        shape(n_proto, crops, own_images, features, dtype=bf16),
        totals, soft, own_term, other_term,
    )
    row_parts = lax.all_to_all(row_parts, "proto", 0, 0)

    held = []
    for kind in kinds:
        keep, send = call(
            far_sum_kernel,
            [shape(2 * half, features), shape(2 * half, features, dtype=bf16)],
            *arrived[kind],
        )
        held.append((keep, exchange(send, kind, 3)))
    operands = []
    for kind, (keep, part) in zip(kinds, held):
        keep, send = call(
            near_sum_kernel,
            [shape(half, features), shape(half, features, dtype=bf16)],
            keep, part,
        )
        operands += [keep, exchange(send, kind, 1)]
    grad_proto = call(finish_kernel, shape(*prototypes.shape[1:]), *operands, prototypes[0])

    grad_emb = call(finish_rows_kernel, shape(own_images, crops, features), row_parts, by_crop)
    return (grad_emb[:, None], grad_proto[None])


def solution(mesh):
    return jax.shard_map(
        on_device,
        mesh=mesh,
        in_specs=(
            P(("dp", "proto"), "crop", None, None),
            P("dp", "crop", "proto"),
            P("proto", ("dp", "crop"), None),
        ),
        out_specs=(P(("dp", "proto"), "crop", None, None), P("proto", ("dp", "crop"), None)),
        check_vma=False,
    )
```

time: 126 us -> 130 us (1.032); the launches traced: 124 us -> 130 us
  starting transfers between devices: 33.7 us -> 46.2 us
  waiting for transfers between devices: 42.5 us -> 34.2 us
  local copies, waits for them, and re-layouts: 6.92 us -> 13.9 us
  other arithmetic: 4.78 us -> 1.45 us
  Pallas kernels: 22 us -> 19.5 us
    ppermute x12 -> x20, waiting for transfers between devices: 42.5 us -> 27.1 us  [exchange(): lax.ppermute(value, owners, [(owner, owner ^ mask) for owner in range(sid...]
    ppermute x12 -> x20, starting transfers between devices: 17.6 us -> 30.3 us  [exchange(): lax.ppermute(value, owners, [(owner, owner ^ mask) for owner in range(sid...]
    ppermute x2, waiting for transfers between devices: 0.01 us -> 7.15 us  [swapped(): return lax.ppermute(value, 'crop', [(0, 1), (1, 0)])]
    unnamed x24 -> x43, local copies, waits for them, and re-layouts: 5.89 us -> 12 us
    pallas_call x11 -> x16, Pallas kernels: 22 us -> 19.5 us  [call(): pl.pallas_call(kernel, out_shape=out_shape, in_specs=[kept] * len(operand...]
  transfers between devices with their start and end apart: 16 -> 24, of which waited for: 10 -> 10; matrix products, arithmetic and copies ran while one was open for 4% -> 2% of each run, Pallas kernels for 15% -> 11%
where the time goes in v1:
time: 130 us
  starting transfers between devices  46.2 us (36%)
  waiting for transfers between devices  34.2 us (26%)
  Pallas kernels  19.5 us (15%)
  local copies, waits for them, and re-layouts  13.9 us (11%)
  blocking collectives  13.5 us (10%)
  other arithmetic  1.45 us (1%)
    ppermute x20, starting transfers between devices, exchange(): lax.ppermute(value, owners, [(owner, owner ^ mask) for owner in range(sid...  30.3 us
    ppermute x20, waiting for transfers between devices, exchange(): lax.ppermute(value, owners, [(owner, owner ^ mask) for owner in range(sid...  27.1 us
    pallas_call x16, Pallas kernels, call(): pl.pallas_call(kernel, out_shape=out_shape, in_specs=[kept] * len(operand...  19.5 us
    all_to_all x1, blocking collectives, on_device(): totals = lax.all_to_all(totals, 'proto', 0, 0)  13.5 us
    unnamed x43, local copies, waits for them, and re-layouts  12 us
    all_to_all x1, starting transfers between devices, on_device(): lax.all_to_all(jnp.broadcast_to(own_emb, (n_proto, own_rows, features)),...  8.59 us
    ppermute x2, waiting for transfers between devices, swapped(): return lax.ppermute(value, 'crop', [(0, 1), (1, 0)])  7.15 us
    all_to_all x1, starting transfers between devices, on_device(): row_parts = lax.all_to_all(row_parts, 'proto', 0, 0)  5.37 us
  transfers between devices with their start and end apart: 24, of which 10 were waited for; matrix products, arithmetic and copies ran while one was open for 2% of the time, Pallas kernels for 11%

profile of v1, /device:TPU:32, one launch (start us, length us, event | category | flops | bytes accessed | tf_op | source)
XLA Modules:
  0.0 129.7 jit_solution(5764055717702709477)
XLA Ops:
  5.0 8.6 %all-to-all-start = ((bf16[16,64,256]{2,1,0:T(8,128)(2,1)}), bf16[16,64,256]{2,1,0:T(8,128)(2,1)S(1)}, u32[]{:S(2)}, u32[]{:S(2)}) async-start(bf16[16,64,256]{2,1,0:T(8,128)(2,1)} %broadcast_in_dim.14), calls=%async_computation | async-start | bytes 1048576 | tf_op jit(solution)/shard_map/all_to_all | solution.py:196
  13.6 2.3 %collective-permute-start.1 = (bf16[256,256]{1,0:T(8,128)(2,1)S(1)}, bf16[256,256]{1,0:T(8,128)(2,1)S(1)}, u32[]{:S(2)}, u32[]{:S(2)}) collective-permute-start(bf16[256,256]{1,0:T(8,128)(2,1)S(1)} %pad_maximum_fusion.2), channel_id=1, source_target_pairs={{0,192},{1,193},{32,224},{33,225},{64,128},{65,129},{96,160},{97,1... | collective-permute-start | bytes 393224 | tf_op jit(solution)/shard_map/ppermute | solution.py:31
  17.3 3.1 %collective-permute-done.1 = bf16[256,256]{1,0:T(8,128)(2,1)S(1)} collective-permute-done((bf16[256,256]{1,0:T(8,128)(2,1)S(1)}, bf16[256,256]{1,0:T(8,128)(2,1)S(1)}, u32[]{:S(2)}, u32[]{:S(2)}) %collective-permute-start.1) | collective-permute-done | bytes 131104 | tf_op jit(solution)/shard_map/ppermute | solution.py:31
  21.1 3.0 %collective-permute-start.4 = (bf16[512,256]{1,0:T(8,128)(2,1)}, bf16[512,256]{1,0:T(8,128)(2,1)S(1)}, u32[]{:S(2)}, u32[]{:S(2)}) collective-permute-start(bf16[512,256]{1,0:T(8,128)(2,1)} %pad_maximum_fusion.refs_2_), channel_id=1, source_target_pairs={{0,32},{1,33},{32,0},{33,1},{64,96},{65,97},{96,64},{97,65},{128,1... | collective-permute-start | bytes 786440 | tf_op jit(solution)/shard_map/ppermute | solution.py:31
  25.4 7.7 %collective-permute-done.3 = bf16[256,256]{1,0:T(8,128)(2,1)S(1)} collective-permute-done((bf16[256,256]{1,0:T(8,128)(2,1)S(1)}, bf16[256,256]{1,0:T(8,128)(2,1)S(1)}, u32[]{:S(2)}, u32[]{:S(2)}) %collective-permute-start.3) | collective-permute-done | bytes 131104 | tf_op jit(solution)/shard_map/ppermute | solution.py:31
  33.8 1.7 %collective-permute-start.5 = (bf16[512,256]{1,0:T(8,128)(2,1)}, bf16[512,256]{1,0:T(8,128)(2,1)}, u32[]{:S(2)}, u32[]{:S(2)}) collective-permute-start(bf16[512,256]{1,0:T(8,128)(2,1)} %pad_maximum_fusion.1.refs_3_), channel_id=1, source_target_pairs={{0,128},{1,129},{32,160},{33,161},{64,192},{65,193},{96,224},{97,2... | collective-permute-start | bytes 786440 | tf_op jit(solution)/shard_map/ppermute | solution.py:31
  42.7 2.8 %shard_map.51 = (bf16[512,1024]{1,0:T(8,128)(2,1)S(1)}, bf16[512,1024]{1,0:T(8,128)(2,1)S(1)}, f32[256,1024]{1,0:T(8,128)S(1)}, f32[256,256]{1,0:T(8,128)S(1)}, f32[8,1024]{1,0:T(8,128)S(1)}) custom-call(bf16[256,1024]{1,0:T(8,128)(2,1)S(1)} %get-tuple-element.45.refs_0_.z_t_ref, bf16[256,4096]{1,0:T(8,128)(2,1)S(1)} %bitcast.18, ...), custom_call_target="tpu_custom_call" | custom-call | tf_op jit(solution)/shard_map/pallas_call | solution.py:169
  46.4 2.8 %shard_map.52 = (bf16[512,1024]{1,0:T(8,128)(2,1)S(1)}, bf16[512,1024]{1,0:T(8,128)(2,1)S(1)}, f32[256,1024]{1,0:T(8,128)S(1)}, f32[256,256]{1,0:T(8,128)S(1)}, f32[8,1024]{1,0:T(8,128)S(1)}) custom-call(bf16[256,1024]{1,0:T(8,128)(2,1)S(1)} %get-tuple-element.45.refs_0_.z_t_ref, bf16[256,4096]{1,0:T(8,128)(2,1)S(1)} %bitcast.19, ...), custom_call_target="tpu_custom_call" | custom-call | tf_op jit(solution)/shard_map/pallas_call | solution.py:169
  51.2 2.7 %shard_map.53 = (bf16[512,1024]{1,0:T(8,128)(2,1)S(1)}, bf16[512,1024]{1,0:T(8,128)(2,1)S(1)}, f32[256,1024]{1,0:T(8,128)S(1)}, f32[256,256]{1,0:T(8,128)S(1)}, f32[8,1024]{1,0:T(8,128)S(1)}) custom-call(bf16[256,1024]{1,0:T(8,128)(2,1)S(1)} %get-tuple-element.45.refs_0_.z_t_ref, bf16[256,4096]{1,0:T(8,128)(2,1)S(1)} %bitcast.20, ...), custom_call_target="tpu_custom_call" | custom-call | tf_op jit(solution)/shard_map/pallas_call | solution.py:169
  56.0 2.8 %shard_map.54 = (bf16[512,1024]{1,0:T(8,128)(2,1)S(1)}, bf16[512,1024]{1,0:T(8,128)(2,1)S(1)}, f32[256,1024]{1,0:T(8,128)S(1)}, f32[256,256]{1,0:T(8,128)S(1)}, f32[16,8,128]{2,1,0:T(8,128)S(1)}) custom-call(bf16[256,1024]{1,0:T(8,128)(2,1)S(1)} %get-tuple-element.45.refs_0_.z_t_ref, bf16[256,4096]{1,0:T(8,128)(2,1)S(1)} %bitcast.21, ...), custom_call_target="tpu_custom_call" | custom-call | tf_op jit(solution)/shard_map/pallas_call | solution.py:169
  60.8 13.5 %all_to_all.15.totals_ref = f32[16,8,128]{2,1,0:T(8,128)S(1)} all-to-all(f32[16,8,128]{2,1,0:T(8,128)S(1)} %get-tuple-element.58), channel_id=1, replica_groups=mesh['dp'=8,'proto'=16,'crop'=2] {'proto'}, dimensions={0} | all-to-all | bytes 131072 | tf_op jit(solution)/shard_map/all_to_all | solution.py:225
  76.3 7.2 %collective-permute-done.10.other_ref = f32[256,256]{1,0:T(8,128)S(1)} collective-permute-done((f32[256,256]{1,0:T(8,128)S(1)}, f32[256,256]{1,0:T(8,128)S(1)}, u32[]{:S(2)}, u32[]{:S(2)}) %collective-permute-start.10) | collective-permute-done | bytes 262176 | tf_op jit(solution)/shard_map/ppermute | solution.py:22
  84.6 5.4 %all-to-all-start.2 = ((bf16[16,4,16,256]{3,2,1,0:T(8,128)(2,1)}), bf16[16,4,16,256]{3,2,1,0:T(8,128)(2,1)}, u32[]{:S(2)}, u32[]{:S(2)}) async-start(bf16[16,4,16,256]{3,2,1,0:T(8,128)(2,1)} %copy-done.1), calls=%async_computation.2 | async-start | bytes 1048576 | tf_op jit(solution)/shard_map/all_to_all | solution.py:247
  93.4 2.1 %collective-permute-start.14 = (bf16[512,256]{1,0:T(8,128)(2,1)S(1)}, bf16[512,256]{1,0:T(8,128)(2,1)S(1)}, u32[]{:S(2)}, u32[]{:S(2)}) collective-permute-start(bf16[512,256]{1,0:T(8,128)(2,1)S(1)} %get-tuple-element.75), channel_id=1, source_target_pairs={{0,33},{1,32},{32,1},{33,0},{64,97},{65,96},{96,65},{97,64},{128,1... | collective-permute-start | bytes 786440 | tf_op jit(solution)/shard_map/ppermute | solution.py:31
  97.9 2.5 %collective-permute-start.12 = (bf16[512,256]{1,0:T(8,128)(2,1)S(1)}, bf16[512,256]{1,0:T(8,128)(2,1)S(1)}, u32[]{:S(2)}, u32[]{:S(2)}) collective-permute-start(bf16[512,256]{1,0:T(8,128)(2,1)S(1)} %get-tuple-element.69), channel_id=1, source_target_pairs={{0,32},{1,33},{32,0},{33,1},{64,96},{65,97},{96,64},{97,65},{128,1... | collective-permute-start | bytes 786440 | tf_op jit(solution)/shard_map/ppermute | solution.py:31
  100.5 2.2 %collective-permute-start.19 = (bf16[512,256]{1,0:T(8,128)(2,1)S(1)}, bf16[512,256]{1,0:T(8,128)(2,1)S(1)}, u32[]{:S(2)}, u32[]{:S(2)}) collective-permute-start(bf16[512,256]{1,0:T(8,128)(2,1)S(1)} %get-tuple-element.83), channel_id=1, source_target_pairs={{0,192},{1,193},{32,224},{33,225},{64,128},{65,129},{96,160},{97,1... | collective-permute-start | bytes 786440 | tf_op jit(solution)/shard_map/ppermute | solution.py:31
  103.0 2.1 %collective-permute-start.17 = (bf16[512,256]{1,0:T(8,128)(2,1)S(1)}, bf16[512,256]{1,0:T(8,128)(2,1)S(1)}, u32[]{:S(2)}, u32[]{:S(2)}) collective-permute-start(bf16[512,256]{1,0:T(8,128)(2,1)S(1)} %get-tuple-element.81), channel_id=1, source_target_pairs={{0,128},{1,129},{32,160},{33,161},{64,192},{65,193},{96,224},{97,2... | collective-permute-start | bytes 786440 | tf_op jit(solution)/shard_map/ppermute | solution.py:31
  106.1 5.0 %collective-permute-done.12.refs_0_ = bf16[512,256]{1,0:T(8,128)(2,1)S(1)} collective-permute-done((bf16[512,256]{1,0:T(8,128)(2,1)S(1)}, bf16[512,256]{1,0:T(8,128)(2,1)S(1)}, u32[]{:S(2)}, u32[]{:S(2)}) %collective-permute-start.12) | collective-permute-done | bytes 262176 | tf_op jit(solution)/shard_map/ppermute | solution.py:31
  111.2 2.3 %collective-permute-start.15 = (bf16[256,256]{1,0:T(8,128)(2,1)S(1)}, bf16[256,256]{1,0:T(8,128)(2,1)S(1)}, u32[]{:S(2)}, u32[]{:S(2)}) collective-permute-start(bf16[256,256]{1,0:T(8,128)(2,1)S(1)} %get-tuple-element.77), channel_id=1, source_target_pairs={{0,192},{1,193},{32,224},{33,225},{64,128},{65,129},{96,160},{97,1... | collective-permute-start | bytes 393224 | tf_op jit(solution)/shard_map/ppermute | solution.py:31
  113.5 2.6 %collective-permute-done.17.refs_0_ = bf16[512,256]{1,0:T(8,128)(2,1)S(1)} collective-permute-done((bf16[512,256]{1,0:T(8,128)(2,1)S(1)}, bf16[512,256]{1,0:T(8,128)(2,1)S(1)}, u32[]{:S(2)}, u32[]{:S(2)}) %collective-permute-start.17) | collective-permute-done | bytes 262176 | tf_op jit(solution)/shard_map/ppermute | solution.py:31
  116.2 2.0 %collective-permute-start.20 = (bf16[256,256]{1,0:T(8,128)(2,1)S(1)}, bf16[256,256]{1,0:T(8,128)(2,1)S(1)}, u32[]{:S(2)}, u32[]{:S(2)}) collective-permute-start(bf16[256,256]{1,0:T(8,128)(2,1)S(1)} %get-tuple-element.85), channel_id=1, source_target_pairs={{0,33},{1,32},{32,1},{33,0},{64,97},{65,96},{96,65},{97,64},{128,1... | collective-permute-start | bytes 393224 | tf_op jit(solution)/shard_map/ppermute | solution.py:31
  118.9 3.5 %collective-permute-done.20.part_ref = bf16[256,256]{1,0:T(8,128)(2,1)S(1)} collective-permute-done((bf16[256,256]{1,0:T(8,128)(2,1)S(1)}, bf16[256,256]{1,0:T(8,128)(2,1)S(1)}, u32[]{:S(2)}, u32[]{:S(2)}) %collective-permute-start.20) | collective-permute-done | bytes 131104 | tf_op jit(solution)/shard_map/ppermute | solution.py:31
  123.2 3.7 %collective-permute-done.21.part_b_ref = bf16[128,256]{1,0:T(8,128)(2,1)S(1)} collective-permute-done((bf16[128,256]{1,0:T(8,128)(2,1)S(1)}, bf16[128,256]{1,0:T(8,128)(2,1)S(1)}, u32[]{:S(2)}, u32[]{:S(2)}) %collective-permute-start.21) | collective-permute-done | bytes 65568 | tf_op jit(solution)/shard_map/ppermute | solution.py:31
  127.8 1.9 %shard_map.56 = f32[16,4,256]{2,1,0:T(4,128)} custom-call(bf16[16,4,16,256]{3,2,1,0:T(8,128)(2,1)} %all-to-all-done.2.parts_ref, bf16[4,16,256]{2,1,0:T(8,128)(2,1)S(1)} %bitcast.29), custom_call_target="tpu_custom_call" | custom-call | tf_op jit(solution)/shard_map/pallas_call | solution.py:169
  (90 shorter events, 35.5 us)
Async XLA Ops:
  1.7 11.9 %collective-permute-start = (bf16[128,256]{1,0:T(8,128)(2,1)S(1)}, bf16[128,256]{1,0:T(8,128)(2,1)S(1)}, u32[]{:S(2)}, u32[]{:S(2)}) collective-permute-start(bf16[128,256]{1,0:T(8,128)(2,1)S(1)} %get-tuple-element.91), channel_id=1, source_target_pairs={{0,64},{1,65},{32,96},{33,97},{64,0},{65,1},{96,32},{97,33},{128,1... | collective-permute-start | bytes 196616 | tf_op jit(solution)/shard_map/ppermute | solution.py:31
  5.0 36.4 %all-to-all-start = ((bf16[16,64,256]{2,1,0:T(8,128)(2,1)}), bf16[16,64,256]{2,1,0:T(8,128)(2,1)S(1)}, u32[]{:S(2)}, u32[]{:S(2)}) async-start(bf16[16,64,256]{2,1,0:T(8,128)(2,1)} %broadcast_in_dim.14), calls=%async_computation | async-start | bytes 1048576 | tf_op jit(solution)/shard_map/all_to_all | solution.py:196
  13.6 6.8 %collective-permute-start.1 = (bf16[256,256]{1,0:T(8,128)(2,1)S(1)}, bf16[256,256]{1,0:T(8,128)(2,1)S(1)}, u32[]{:S(2)}, u32[]{:S(2)}) collective-permute-start(bf16[256,256]{1,0:T(8,128)(2,1)S(1)} %pad_maximum_fusion.2), channel_id=1, source_target_pairs={{0,192},{1,193},{32,224},{33,225},{64,128},{65,129},{96,160},{97,1... | collective-permute-start | bytes 393224 | tf_op jit(solution)/shard_map/ppermute | solution.py:31
  15.9 8.3 %collective-permute-start.2 = (bf16[128,256]{1,0:T(8,128)(2,1)S(1)}, bf16[128,256]{1,0:T(8,128)(2,1)S(1)}, u32[]{:S(2)}, u32[]{:S(2)}) collective-permute-start(bf16[128,256]{1,0:T(8,128)(2,1)S(1)} %get-tuple-element.90), channel_id=1, source_target_pairs={{0,1},{1,0},{32,33},{33,32},{64,65},{65,64},{96,97},{97,96},{128,1... | collective-permute-start | bytes 196616 | tf_op jit(solution)/shard_map/ppermute | solution.py:31
  21.1 18.5 %collective-permute-start.4 = (bf16[512,256]{1,0:T(8,128)(2,1)}, bf16[512,256]{1,0:T(8,128)(2,1)S(1)}, u32[]{:S(2)}, u32[]{:S(2)}) collective-permute-start(bf16[512,256]{1,0:T(8,128)(2,1)} %pad_maximum_fusion.refs_2_), channel_id=1, source_target_pairs={{0,32},{1,33},{32,0},{33,1},{64,96},{65,97},{96,64},{97,65},{128,1... | collective-permute-start | bytes 786440 | tf_op jit(solution)/shard_map/ppermute | solution.py:31
  24.2 9.0 %collective-permute-start.3 = (bf16[256,256]{1,0:T(8,128)(2,1)S(1)}, bf16[256,256]{1,0:T(8,128)(2,1)S(1)}, u32[]{:S(2)}, u32[]{:S(2)}) collective-permute-start(bf16[256,256]{1,0:T(8,128)(2,1)S(1)} %pad_maximum_fusion.3), channel_id=1, source_target_pairs={{0,33},{1,32},{32,1},{33,0},{64,97},{65,96},{96,65},{97,64},{128,1... | collective-permute-start | bytes 393224 | tf_op jit(solution)/shard_map/ppermute | solution.py:31
  33.8 12.6 %collective-permute-start.5 = (bf16[512,256]{1,0:T(8,128)(2,1)}, bf16[512,256]{1,0:T(8,128)(2,1)}, u32[]{:S(2)}, u32[]{:S(2)}) collective-permute-start(bf16[512,256]{1,0:T(8,128)(2,1)} %pad_maximum_fusion.1.refs_3_), channel_id=1, source_target_pairs={{0,128},{1,129},{32,160},{33,161},{64,192},{65,193},{96,224},{97,2... | collective-permute-start | bytes 786440 | tf_op jit(solution)/shard_map/ppermute | solution.py:31
  35.5 15.7 %collective-permute-start.6 = (bf16[512,256]{1,0:T(8,128)(2,1)}, bf16[512,256]{1,0:T(8,128)(2,1)}, u32[]{:S(2)}, u32[]{:S(2)}) collective-permute-start(bf16[512,256]{1,0:T(8,128)(2,1)} %pad_maximum_fusion.refs_2_), channel_id=1, source_target_pairs={{0,1},{1,0},{32,33},{33,32},{64,65},{65,64},{96,97},{97,96},{128,1... | collective-permute-start | bytes 786440 | tf_op jit(solution)/shard_map/ppermute | solution.py:31
  37.0 14.2 %collective-permute-start.7 = (bf16[512,256]{1,0:T(8,128)(2,1)}, bf16[512,256]{1,0:T(8,128)(2,1)}, u32[]{:S(2)}, u32[]{:S(2)}) collective-permute-start(bf16[512,256]{1,0:T(8,128)(2,1)} %pad_maximum_fusion.1.refs_3_), channel_id=1, source_target_pairs={{0,64},{1,65},{32,96},{33,97},{64,0},{65,1},{96,32},{97,33},{128,1... | collective-permute-start | bytes 786440 | tf_op jit(solution)/shard_map/ppermute | solution.py:31
  38.4 17.6 %collective-permute-start.8 = (bf16[512,256]{1,0:T(8,128)(2,1)}, bf16[512,256]{1,0:T(8,128)(2,1)}, u32[]{:S(2)}, u32[]{:S(2)}) collective-permute-start(bf16[512,256]{1,0:T(8,128)(2,1)} %pad_maximum_fusion.refs_2_), channel_id=1, source_target_pairs={{0,33},{1,32},{32,1},{33,0},{64,97},{65,96},{96,65},{97,64},{128,1... | collective-permute-start | bytes 786440 | tf_op jit(solution)/shard_map/ppermute | solution.py:31
  40.3 15.7 %collective-permute-start.9 = (bf16[512,256]{1,0:T(8,128)(2,1)}, bf16[512,256]{1,0:T(8,128)(2,1)}, u32[]{:S(2)}, u32[]{:S(2)}) collective-permute-start(bf16[512,256]{1,0:T(8,128)(2,1)} %pad_maximum_fusion.1.refs_3_), channel_id=1, source_target_pairs={{0,192},{1,193},{32,224},{33,225},{64,128},{65,129},{96,160},{97,1... | collective-permute-start | bytes 786440 | tf_op jit(solution)/shard_map/ppermute | solution.py:31
  74.3 9.2 %collective-permute-start.10 = (f32[256,256]{1,0:T(8,128)S(1)}, f32[256,256]{1,0:T(8,128)S(1)}, u32[]{:S(2)}, u32[]{:S(2)}) collective-permute-start(f32[256,256]{1,0:T(8,128)S(1)} %get-tuple-element.61.own_ref), channel_id=1, source_target_pairs={{0,1},{1,0},{2,3},{3,2},{4,5},{5,4},{6,7},{7,6},{8,9},{9,8},{10,11... | collective-permute-start | bytes 786440 | tf_op jit(solution)/shard_map/ppermute | solution.py:22
  75.7 14.3 %collective-permute-start.11 = (f32[256,256]{1,0:T(8,128)}, f32[256,256]{1,0:T(8,128)S(1)}, u32[]{:S(2)}, u32[]{:S(2)}) collective-permute-start(f32[256,256]{1,0:T(8,128)} %get-tuple-element.63), channel_id=1, source_target_pairs={{0,1},{1,0},{2,3},{3,2},{4,5},{5,4},{6,7},{7,6},{8,9},{9,8},{10,11... | collective-permute-start | bytes 786440 | tf_op jit(solution)/shard_map/ppermute | solution.py:22
  84.6 43.2 %all-to-all-start.2 = ((bf16[16,4,16,256]{3,2,1,0:T(8,128)(2,1)}), bf16[16,4,16,256]{3,2,1,0:T(8,128)(2,1)}, u32[]{:S(2)}, u32[]{:S(2)}) async-start(bf16[16,4,16,256]{3,2,1,0:T(8,128)(2,1)} %copy-done.1), calls=%async_computation.2 | async-start | bytes 1048576 | tf_op jit(solution)/shard_map/all_to_all | solution.py:247
  93.4 9.6 %collective-permute-start.14 = (bf16[512,256]{1,0:T(8,128)(2,1)S(1)}, bf16[512,256]{1,0:T(8,128)(2,1)S(1)}, u32[]{:S(2)}, u32[]{:S(2)}) collective-permute-start(bf16[512,256]{1,0:T(8,128)(2,1)S(1)} %get-tuple-element.75), channel_id=1, source_target_pairs={{0,33},{1,32},{32,1},{33,0},{64,97},{65,96},{96,65},{97,64},{128,1... | collective-permute-start | bytes 786440 | tf_op jit(solution)/shard_map/ppermute | solution.py:31
  96.4 9.7 %collective-permute-start.13 = (bf16[512,256]{1,0:T(8,128)(2,1)S(1)}, bf16[512,256]{1,0:T(8,128)(2,1)S(1)}, u32[]{:S(2)}, u32[]{:S(2)}) collective-permute-start(bf16[512,256]{1,0:T(8,128)(2,1)S(1)} %get-tuple-element.72), channel_id=1, source_target_pairs={{0,1},{1,0},{32,33},{33,32},{64,65},{65,64},{96,97},{97,96},{128,1... | collective-permute-start | bytes 786440 | tf_op jit(solution)/shard_map/ppermute | solution.py:31
  97.9 13.2 %collective-permute-start.12 = (bf16[512,256]{1,0:T(8,128)(2,1)S(1)}, bf16[512,256]{1,0:T(8,128)(2,1)S(1)}, u32[]{:S(2)}, u32[]{:S(2)}) collective-permute-start(bf16[512,256]{1,0:T(8,128)(2,1)S(1)} %get-tuple-element.69), channel_id=1, source_target_pairs={{0,32},{1,33},{32,0},{33,1},{64,96},{65,97},{96,64},{97,65},{128,1... | collective-permute-start | bytes 786440 | tf_op jit(solution)/shard_map/ppermute | solution.py:31
  100.5 13.0 %collective-permute-start.19 = (bf16[512,256]{1,0:T(8,128)(2,1)S(1)}, bf16[512,256]{1,0:T(8,128)(2,1)S(1)}, u32[]{:S(2)}, u32[]{:S(2)}) collective-permute-start(bf16[512,256]{1,0:T(8,128)(2,1)S(1)} %get-tuple-element.83), channel_id=1, source_target_pairs={{0,192},{1,193},{32,224},{33,225},{64,128},{65,129},{96,160},{97,1... | collective-permute-start | bytes 786440 | tf_op jit(solution)/shard_map/ppermute | solution.py:31
  102.7 10.8 %collective-permute-start.18 = (bf16[512,256]{1,0:T(8,128)(2,1)S(1)}, bf16[512,256]{1,0:T(8,128)(2,1)S(1)}, u32[]{:S(2)}, u32[]{:S(2)}) collective-permute-start(bf16[512,256]{1,0:T(8,128)(2,1)S(1)} %get-tuple-element.82), channel_id=1, source_target_pairs={{0,64},{1,65},{32,96},{33,97},{64,0},{65,1},{96,32},{97,33},{128,1... | collective-permute-start | bytes 786440 | tf_op jit(solution)/shard_map/ppermute | solution.py:31
  103.0 13.0 %collective-permute-start.17 = (bf16[512,256]{1,0:T(8,128)(2,1)S(1)}, bf16[512,256]{1,0:T(8,128)(2,1)S(1)}, u32[]{:S(2)}, u32[]{:S(2)}) collective-permute-start(bf16[512,256]{1,0:T(8,128)(2,1)S(1)} %get-tuple-element.81), channel_id=1, source_target_pairs={{0,128},{1,129},{32,160},{33,161},{64,192},{65,193},{96,224},{97,2... | collective-permute-start | bytes 786440 | tf_op jit(solution)/shard_map/ppermute | solution.py:31
  111.2 7.6 %collective-permute-start.15 = (bf16[256,256]{1,0:T(8,128)(2,1)S(1)}, bf16[256,256]{1,0:T(8,128)(2,1)S(1)}, u32[]{:S(2)}, u32[]{:S(2)}) collective-permute-start(bf16[256,256]{1,0:T(8,128)(2,1)S(1)} %get-tuple-element.77), channel_id=1, source_target_pairs={{0,192},{1,193},{32,224},{33,225},{64,128},{65,129},{96,160},{97,1... | collective-permute-start | bytes 393224 | tf_op jit(solution)/shard_map/ppermute | solution.py:31
  116.2 6.3 %collective-permute-start.20 = (bf16[256,256]{1,0:T(8,128)(2,1)S(1)}, bf16[256,256]{1,0:T(8,128)(2,1)S(1)}, u32[]{:S(2)}, u32[]{:S(2)}) collective-permute-start(bf16[256,256]{1,0:T(8,128)(2,1)S(1)} %get-tuple-element.85), channel_id=1, source_target_pairs={{0,33},{1,32},{32,1},{33,0},{64,97},{65,96},{96,65},{97,64},{128,1... | collective-permute-start | bytes 393224 | tf_op jit(solution)/shard_map/ppermute | solution.py:31
  118.8 4.4 %collective-permute-start.16 = (bf16[128,256]{1,0:T(8,128)(2,1)S(1)}, bf16[128,256]{1,0:T(8,128)(2,1)S(1)}, u32[]{:S(2)}, u32[]{:S(2)}) collective-permute-start(bf16[128,256]{1,0:T(8,128)(2,1)S(1)} %get-tuple-element.79), channel_id=1, source_target_pairs={{0,64},{1,65},{32,96},{33,97},{64,0},{65,1},{96,32},{97,33},{128,1... | collective-permute-start | bytes 196616 | tf_op jit(solution)/shard_map/ppermute | solution.py:31
  122.5 4.4 %collective-permute-start.21 = (bf16[128,256]{1,0:T(8,128)(2,1)S(1)}, bf16[128,256]{1,0:T(8,128)(2,1)S(1)}, u32[]{:S(2)}, u32[]{:S(2)}) collective-permute-start(bf16[128,256]{1,0:T(8,128)(2,1)S(1)} %get-tuple-element.87), channel_id=1, source_target_pairs={{0,1},{1,0},{32,33},{33,32},{64,65},{65,64},{96,97},{97,96},{128,1... | collective-permute-start | bytes 196616 | tf_op jit(solution)/shard_map/ppermute | solution.py:31
  (21 other events, 106.7 us)

commit v2 on v1

--- a/solution.py
+++ b/solution.py
@@ -60,6 +60,17 @@
         first = pl.multiple_of((owner * 2 + kind) * half, half)
         parts.append(code_ref[:, pl.ds(first, half)])
     return jnp.concatenate(parts, axis=1)
+
+
+def split_kernel(proto_ref, emb_ref, first_ref, second_ref, own_ref, spread_ref):
+    half = first_ref.shape[0]
+    first_ref[...] = proto_ref[:half]
+    second_ref[...] = proto_ref[half:]
+    emb = emb_ref[...].astype(f32)
+    own = jnp.concatenate([emb[:, crop] for crop in range(emb.shape[1])]).astype(bf16)
+    own_ref[...] = own.reshape(own_ref.shape)
+    for peer in range(spread_ref.shape[0]):
+        spread_ref[peer] = own
 
 
 def embeddings_kernel(raw_ref, z_t_ref, local_ref, outgoing_ref):
@@ -100,13 +111,19 @@
         total_ref[...] = acc
 
 
-def prototypes_kernel(
-    totals_ref, z_t_ref, local_ref, incoming_ref, code_ref, exp_a_ref, exp_b_ref, *out_refs,
-    distance, crops, own_images
-):
-    weights = row_weights(totals_ref, crops, own_images)
-    zw = (z_t_ref[...].astype(f32) * weights).astype(bf16)
-    target = (local_ref[...] + incoming_ref[...]).astype(bf16)
+def prototypes_kernel(*refs, distance, crops, own_images, first):
+    if first:
+        totals_ref, z_t_ref, local_ref, incoming_ref = refs[:4]
+        weights = row_weights(totals_ref, crops, own_images)
+        zw = (z_t_ref[...].astype(f32) * weights).astype(bf16)
+        target = (local_ref[...] + incoming_ref[...]).astype(bf16)
+        refs[-2][...] = zw
+        refs[-1][...] = target
+        refs = refs[4:-2]
+    else:
+        zw, target = refs[0][...], refs[1][...]
+        refs = refs[2:]
+    code_ref, exp_a_ref, exp_b_ref, *out_refs = refs
     for kind, exp_ref, out_ref in zip(kinds, (exp_a_ref, exp_b_ref), out_refs):
         code = code_columns(code_ref, kind, distance)
         grads = dot(exp_ref[...], zw, 1, 1) - dot(code, target, 0, 0)
@@ -184,18 +201,23 @@
     code = codes[:, 0]
     half = prototypes.shape[1] // 2
 
-    by_crop = jnp.swapaxes(embeddings[:, 0], 0, 1)
-    halves = [prototypes[0, :half], prototypes[0, half:]]
+    *halves, by_crop, spread_emb = call(
+        split_kernel,
+        [
+            shape(half, features, dtype=bf16),
+            shape(half, features, dtype=bf16),
+            shape(crops, own_images, features, dtype=bf16),
+            shape(n_proto, own_rows, features, dtype=bf16),
+        ],
+        prototypes[0], embeddings[:, 0],
+    )
     for step, distance in enumerate((1, 3)):
         moved = []
         for kind in kinds:
             moved.append(exchange(halves[kind], kind, distance))
         halves = [jnp.concatenate(pair) for pair in zip(halves, moved)]
         if step == 0:
-            own_emb = by_crop.reshape(1, own_rows, features)
-            raw_emb = lax.all_to_all(
-                jnp.broadcast_to(own_emb, (n_proto, own_rows, features)), "proto", 0, 0
-            )
+            raw_emb = lax.all_to_all(spread_emb, "proto", 0, 0)
     gathered = {0: halves}
     for d in arrivals:
         gathered[d] = []
@@ -222,23 +244,35 @@
         state = (soft, own_term, totals)
     totals, outgoing = lax.optimization_barrier((totals, outgoing))
     incoming = swapped(outgoing)
+    other_term = swapped(own_term)
     totals = lax.all_to_all(totals, "proto", 0, 0)
-    own_term, totals = lax.optimization_barrier((own_term, totals))
-    other_term = swapped(own_term)
 
     arrived = [[], []]
     for d in (*arrivals, 0):
-        parts = call(
-            functools.partial(prototypes_kernel, distance=d, crops=crops, own_images=own_images),
-            [shape(side * half, features, dtype=bf16 if d else f32)] * 2,
-            totals, z_t, local_sum, incoming, code, *exponents[d],
+        first = d == arrivals[0]
+        outs = call(
+            functools.partial(
+                prototypes_kernel,
+                distance=d, crops=crops, own_images=own_images, first=first,
+            ),
+            [shape(side * half, features, dtype=bf16 if d else f32)] * 2
+            + [shape(features, rows, dtype=bf16), shape(images, features, dtype=bf16)] * first,
+            *((totals, z_t, local_sum, incoming) if first else (zw, target)),
+            code, *exponents[d],
         )
+        parts = outs[:2]
+        if first:
+            zw, target = outs[2:]
         for kind in kinds:
             if d:
                 arrived[kind].append(exchange(parts[kind], 1 - kind, d))
             else:
                 arrived[kind].insert(0, parts[kind])
 
+    held_parts = [arrived[kind][0] for kind in kinds]
+    soft, *held_parts = lax.optimization_barrier((soft, *held_parts))
+    for kind in kinds:
+        arrived[kind][0] = held_parts[kind]
     row_parts = call(
         functools.partial(rows_kernel, crops=crops, own_images=own_images),
         shape(n_proto, crops, own_images, features, dtype=bf16),
@@ -264,7 +298,9 @@
         operands += [keep, exchange(send, kind, 1)]
     grad_proto = call(finish_kernel, shape(*prototypes.shape[1:]), *operands, prototypes[0])
 
-    grad_emb = call(finish_rows_kernel, shape(own_images, crops, features), row_parts, by_crop)
+    grad_emb = call(
+        finish_rows_kernel, shape(own_images, crops, features), row_parts, by_crop
+    )
     return (grad_emb[:, None], grad_proto[None])
 
 

time: 130 us -> 120 us (0.923)
  starting transfers between devices: 46.2 us -> 42.2 us
  local copies, waits for them, and re-layouts: 13.9 us -> 11.4 us
  Pallas kernels: 19.5 us -> 17.5 us
  other arithmetic: 1.45 us -> 0.02 us
    ppermute x2, waiting for transfers between devices: 7.15 us -> 0.01 us  [swapped(): return lax.ppermute(value, 'crop', [(0, 1), (1, 0)])]
    ppermute x20, waiting for transfers between devices: 27.1 us -> 33.6 us  [exchange(): lax.ppermute(value, owners, [(owner, owner ^ mask) for owner in range(sid...]
    ppermute x20, starting transfers between devices: 30.3 us -> 26.9 us  [exchange(): lax.ppermute(value, owners, [(owner, owner ^ mask) for owner in range(sid...]
    pallas_call x16 -> x17, Pallas kernels: 19.5 us -> 17.5 us  [call(): pl.pallas_call(kernel, out_shape=out_shape, in_specs=[kept] * len(operand...]
    concatenate x4 -> x2, other arithmetic: 1.45 us -> 0.02 us  [on_device(): halves = [jnp.concatenate(pair) for pair in zip(halves, moved)]]
  transfers between devices with their start and end apart: 24 -> 24, of which waited for: 10 -> 10; matrix products, arithmetic and copies ran while one was open for 2% -> 0% of each run, Pallas kernels for 11% -> 11%
where the time goes in v2:
time: 120 us; the launch traced here: 119 us
  starting transfers between devices  42.2 us (35%)
  waiting for transfers between devices  33.6 us (28%)
  Pallas kernels  17.5 us (15%)
  blocking collectives  13.5 us (11%)
  local copies, waits for them, and re-layouts  11.4 us (10%)
    ppermute x20, waiting for transfers between devices, exchange(): lax.ppermute(value, owners, [(owner, owner ^ mask) for owner in range(sid...  33.6 us
    ppermute x20, starting transfers between devices, exchange(): lax.ppermute(value, owners, [(owner, owner ^ mask) for owner in range(sid...  26.9 us
    pallas_call x17, Pallas kernels, call(): pl.pallas_call(kernel, out_shape=out_shape, in_specs=[kept] * len(operand...  17.5 us
    all_to_all x1, blocking collectives, on_device(): totals = lax.all_to_all(totals, 'proto', 0, 0)  13.5 us
    unnamed x43, local copies, waits for them, and re-layouts  11.3 us
    all_to_all x1, starting transfers between devices, on_device(): raw_emb = lax.all_to_all(spread_emb, 'proto', 0, 0)  8.59 us
    all_to_all x1, starting transfers between devices, on_device(): row_parts = lax.all_to_all(row_parts, 'proto', 0, 0)  4.75 us
  transfers between devices with their start and end apart: 24, of which 10 were waited for; matrix products, arithmetic and copies ran while one was open for 0% of the time, Pallas kernels for 11%

profile of v2, /device:TPU:32, one launch (start us, length us, event | category | flops | bytes accessed | tf_op | source)
XLA Modules:
  0.0 119.1 jit_solution(17062942463660354917)
XLA Ops:
  3.3 1.5 %collective-permute-start.2 = (bf16[128,256]{1,0:T(8,128)(2,1)S(1)}, bf16[128,256]{1,0:T(8,128)(2,1)S(1)}, u32[]{:S(2)}, u32[]{:S(2)}) collective-permute-start(bf16[128,256]{1,0:T(8,128)(2,1)S(1)} %get-tuple-element.55), channel_id=1, source_target_pairs={{0,1},{1,0},{32,33},{33,32},{64,65},{65,64},{96,97},{97,96},{128,1... | collective-permute-start | bytes 196616 | tf_op jit(solution)/shard_map/ppermute | solution.py:31
  4.8 8.6 %all-to-all-start = ((bf16[16,64,256]{2,1,0:T(8,128)(2,1)}), bf16[16,64,256]{2,1,0:T(8,128)(2,1)S(1)}, u32[]{:S(2)}, u32[]{:S(2)}) async-start(bf16[16,64,256]{2,1,0:T(8,128)(2,1)} %get-tuple-element.52), calls=%async_computation | async-start | bytes 1048576 | tf_op jit(solution)/shard_map/all_to_all | solution.py:220
  13.4 1.6 %collective-permute-start = (bf16[128,256]{1,0:T(8,128)(2,1)S(1)}, bf16[128,256]{1,0:T(8,128)(2,1)S(1)}, u32[]{:S(2)}, u32[]{:S(2)}) collective-permute-start(bf16[128,256]{1,0:T(8,128)(2,1)S(1)} %get-tuple-element.54), channel_id=1, source_target_pairs={{0,64},{1,65},{32,96},{33,97},{64,0},{65,1},{96,32},{97,33},{128,1... | collective-permute-start | bytes 196616 | tf_op jit(solution)/shard_map/ppermute | solution.py:31
  15.0 2.2 %collective-permute-start.3 = (bf16[256,256]{1,0:T(8,128)(2,1)S(1)}, bf16[256,256]{1,0:T(8,128)(2,1)S(1)}, u32[]{:S(2)}, u32[]{:S(2)}) collective-permute-start(bf16[256,256]{1,0:T(8,128)(2,1)S(1)} %pad_maximum_fusion.1), channel_id=1, source_target_pairs={{0,33},{1,32},{32,1},{33,0},{64,97},{65,96},{96,65},{97,64},{128,1... | collective-permute-start | bytes 393224 | tf_op jit(solution)/shard_map/ppermute | solution.py:31
  17.2 4.3 %collective-permute-done.3 = bf16[256,256]{1,0:T(8,128)(2,1)S(1)} collective-permute-done((bf16[256,256]{1,0:T(8,128)(2,1)S(1)}, bf16[256,256]{1,0:T(8,128)(2,1)S(1)}, u32[]{:S(2)}, u32[]{:S(2)}) %collective-permute-start.3) | collective-permute-done | bytes 131104 | tf_op jit(solution)/shard_map/ppermute | solution.py:31
  21.6 3.0 %collective-permute-start.5 = (bf16[512,256]{1,0:T(8,128)(2,1)S(1)}, bf16[512,256]{1,0:T(8,128)(2,1)S(1)}, u32[]{:S(2)}, u32[]{:S(2)}) collective-permute-start(bf16[512,256]{1,0:T(8,128)(2,1)S(1)} %constant_dynamic-update-slice_fusion.3.refs_3_), channel_id=1, source_target_pairs={{0,128},{1,129},{32,160},{33,161},{64,192},{65,193},{96,224},{97,2... | collective-permute-start | bytes 786440 | tf_op jit(solution)/shard_map/ppermute | solution.py:31
  24.9 8.3 %collective-permute-done.1 = bf16[256,256]{1,0:T(8,128)(2,1)S(1)} collective-permute-done((bf16[256,256]{1,0:T(8,128)(2,1)S(1)}, bf16[256,256]{1,0:T(8,128)(2,1)S(1)}, u32[]{:S(2)}, u32[]{:S(2)}) %collective-permute-start.1) | collective-permute-done | bytes 131104 | tf_op jit(solution)/shard_map/ppermute | solution.py:31
  33.2 1.6 %collective-permute-start.4 = (bf16[512,256]{1,0:T(8,128)(2,1)S(1)}, bf16[512,256]{1,0:T(8,128)(2,1)}, u32[]{:S(2)}, u32[]{:S(2)}) collective-permute-start(bf16[512,256]{1,0:T(8,128)(2,1)S(1)} %constant_dynamic-update-slice_fusion.refs_2_), channel_id=1, source_target_pairs={{0,32},{1,33},{32,0},{33,1},{64,96},{65,97},{96,64},{97,65},{128,1... | collective-permute-start | bytes 786440 | tf_op jit(solution)/shard_map/ppermute | solution.py:31
  36.7 2.0 %collective-permute-start.9 = (bf16[512,256]{1,0:T(8,128)(2,1)S(1)}, bf16[512,256]{1,0:T(8,128)(2,1)}, u32[]{:S(2)}, u32[]{:S(2)}) collective-permute-start(bf16[512,256]{1,0:T(8,128)(2,1)S(1)} %constant_dynamic-update-slice_fusion.3.refs_3_), channel_id=1, source_target_pairs={{0,192},{1,193},{32,224},{33,225},{64,128},{65,129},{96,160},{97,1... | collective-permute-start | bytes 786440 | tf_op jit(solution)/shard_map/ppermute | solution.py:31
  40.4 1.8 %shard_map.52 = (bf16[512,1024]{1,0:T(8,128)(2,1)S(1)}, bf16[512,1024]{1,0:T(8,128)(2,1)S(1)}, f32[256,1024]{1,0:T(8,128)S(1)}, f32[256,256]{1,0:T(8,128)S(1)}, f32[8,1024]{1,0:T(8,128)S(1)}) custom-call(bf16[256,1024]{1,0:T(8,128)(2,1)S(1)} %get-tuple-element.53.refs_0_.refs_1_, bf16[256,4096]{1,0:T(8,128)(2,1)S(1)} %bitcast.8, ...), custom_call_target="tpu_custom_call" | custom-call | tf_op jit(solution)/shard_map/pallas_call | solution.py:186
  42.2 1.9 %collective-permute-done.4.refs_5_ = bf16[512,256]{1,0:T(8,128)(2,1)} collective-permute-done((bf16[512,256]{1,0:T(8,128)(2,1)S(1)}, bf16[512,256]{1,0:T(8,128)(2,1)}, u32[]{:S(2)}, u32[]{:S(2)}) %collective-permute-start.4) | collective-permute-done | bytes 262176 | tf_op jit(solution)/shard_map/ppermute | solution.py:31
  44.0 2.6 %shard_map.53 = (bf16[512,1024]{1,0:T(8,128)(2,1)S(1)}, bf16[512,1024]{1,0:T(8,128)(2,1)S(1)}, f32[256,1024]{1,0:T(8,128)S(1)}, f32[256,256]{1,0:T(8,128)S(1)}, f32[8,1024]{1,0:T(8,128)S(1)}) custom-call(bf16[256,1024]{1,0:T(8,128)(2,1)S(1)} %get-tuple-element.53.refs_0_.refs_1_, bf16[256,4096]{1,0:T(8,128)(2,1)S(1)} %bitcast.9, ...), custom_call_target="tpu_custom_call" | custom-call | tf_op jit(solution)/shard_map/pallas_call | solution.py:186
  46.7 1.5 %collective-permute-done.6.refs_5_ = bf16[512,256]{1,0:T(8,128)(2,1)} collective-permute-done((bf16[512,256]{1,0:T(8,128)(2,1)S(1)}, bf16[512,256]{1,0:T(8,128)(2,1)}, u32[]{:S(2)}, u32[]{:S(2)}) %collective-permute-start.6) | collective-permute-done | bytes 262176 | tf_op jit(solution)/shard_map/ppermute | solution.py:31
  48.1 2.7 %shard_map.54 = (bf16[512,1024]{1,0:T(8,128)(2,1)S(1)}, bf16[512,1024]{1,0:T(8,128)(2,1)S(1)}, f32[256,1024]{1,0:T(8,128)S(1)}, f32[256,256]{1,0:T(8,128)S(1)}, f32[8,1024]{1,0:T(8,128)S(1)}) custom-call(bf16[256,1024]{1,0:T(8,128)(2,1)S(1)} %get-tuple-element.53.refs_0_.refs_1_, bf16[256,4096]{1,0:T(8,128)(2,1)S(1)} %bitcast.10, ...), custom_call_target="tpu_custom_call" | custom-call | tf_op jit(solution)/shard_map/pallas_call | solution.py:186
  52.9 2.8 %shard_map.55 = (bf16[512,1024]{1,0:T(8,128)(2,1)S(1)}, bf16[512,1024]{1,0:T(8,128)(2,1)S(1)}, f32[256,1024]{1,0:T(8,128)S(1)}, f32[256,256]{1,0:T(8,128)S(1)}, f32[16,8,128]{2,1,0:T(8,128)S(1)}) custom-call(bf16[256,1024]{1,0:T(8,128)(2,1)S(1)} %get-tuple-element.53.refs_0_.refs_1_, bf16[256,4096]{1,0:T(8,128)(2,1)S(1)} %bitcast.11, ...), custom_call_target="tpu_custom_call" | custom-call | tf_op jit(solution)/shard_map/pallas_call | solution.py:186
  59.6 13.5 %all_to_all.15.refs_0_.totals_ref = f32[16,8,128]{2,1,0:T(8,128)S(1)} all-to-all(f32[16,8,128]{2,1,0:T(8,128)S(1)} %get-tuple-element.67), channel_id=1, replica_groups=mesh['dp'=8,'proto'=16,'crop'=2] {'proto'}, dimensions={0} | all-to-all | bytes 131072 | tf_op jit(solution)/shard_map/all_to_all | solution.py:248
  78.5 4.7 %all-to-all-start.2 = ((bf16[16,4,16,256]{3,2,1,0:T(8,128)(2,1)}), bf16[16,4,16,256]{3,2,1,0:T(8,128)(2,1)S(1)}, u32[]{:S(2)}, u32[]{:S(2)}) async-start(bf16[16,4,16,256]{3,2,1,0:T(8,128)(2,1)} %copy-done.1), calls=%async_computation.2 | async-start | bytes 1048576 | tf_op jit(solution)/shard_map/all_to_all | solution.py:281
  87.8 2.2 %collective-permute-start.14 = (bf16[512,256]{1,0:T(8,128)(2,1)S(1)}, bf16[512,256]{1,0:T(8,128)(2,1)S(1)}, u32[]{:S(2)}, u32[]{:S(2)}) collective-permute-start(bf16[512,256]{1,0:T(8,128)(2,1)S(1)} %get-tuple-element.89), channel_id=1, source_target_pairs={{0,33},{1,32},{32,1},{33,0},{64,97},{65,96},{96,65},{97,64},{128,1... | collective-permute-start | bytes 786440 | tf_op jit(solution)/shard_map/ppermute | solution.py:31
  92.1 2.3 %collective-permute-start.19 = (bf16[512,256]{1,0:T(8,128)(2,1)S(1)}, bf16[512,256]{1,0:T(8,128)(2,1)S(1)}, u32[]{:S(2)}, u32[]{:S(2)}) collective-permute-start(bf16[512,256]{1,0:T(8,128)(2,1)S(1)} %get-tuple-element.97), channel_id=1, source_target_pairs={{0,192},{1,193},{32,224},{33,225},{64,128},{65,129},{96,160},{97,1... | collective-permute-start | bytes 786440 | tf_op jit(solution)/shard_map/ppermute | solution.py:31
  94.8 4.2 %collective-permute-done.14.refs_2_ = bf16[512,256]{1,0:T(8,128)(2,1)S(1)} collective-permute-done((bf16[512,256]{1,0:T(8,128)(2,1)S(1)}, bf16[512,256]{1,0:T(8,128)(2,1)S(1)}, u32[]{:S(2)}, u32[]{:S(2)}) %collective-permute-start.14) | collective-permute-done | bytes 262176 | tf_op jit(solution)/shard_map/ppermute | solution.py:31
  99.0 2.3 %collective-permute-start.15 = (bf16[256,256]{1,0:T(8,128)(2,1)S(1)}, bf16[256,256]{1,0:T(8,128)(2,1)S(1)}, u32[]{:S(2)}, u32[]{:S(2)}) collective-permute-start(bf16[256,256]{1,0:T(8,128)(2,1)S(1)} %get-tuple-element.91), channel_id=1, source_target_pairs={{0,192},{1,193},{32,224},{33,225},{64,128},{65,129},{96,160},{97,1... | collective-permute-start | bytes 393224 | tf_op jit(solution)/shard_map/ppermute | solution.py:31
  102.0 4.2 %collective-permute-done.19.refs_2_ = bf16[512,256]{1,0:T(8,128)(2,1)S(1)} collective-permute-done((bf16[512,256]{1,0:T(8,128)(2,1)S(1)}, bf16[512,256]{1,0:T(8,128)(2,1)S(1)}, u32[]{:S(2)}, u32[]{:S(2)}) %collective-permute-start.19) | collective-permute-done | bytes 262176 | tf_op jit(solution)/shard_map/ppermute | solution.py:31
  109.4 3.5 %collective-permute-done.20.part_ref = bf16[256,256]{1,0:T(8,128)(2,1)S(1)} collective-permute-done((bf16[256,256]{1,0:T(8,128)(2,1)S(1)}, bf16[256,256]{1,0:T(8,128)(2,1)S(1)}, u32[]{:S(2)}, u32[]{:S(2)}) %collective-permute-start.20) | collective-permute-done | bytes 131104 | tf_op jit(solution)/shard_map/ppermute | solution.py:31
  113.5 3.8 %collective-permute-done.21.part_b_ref = bf16[128,256]{1,0:T(8,128)(2,1)S(1)} collective-permute-done((bf16[128,256]{1,0:T(8,128)(2,1)S(1)}, bf16[128,256]{1,0:T(8,128)(2,1)S(1)}, u32[]{:S(2)}, u32[]{:S(2)}) %collective-permute-start.21) | collective-permute-done | bytes 65568 | tf_op jit(solution)/shard_map/ppermute | solution.py:31
  (89 shorter events, 31.2 us)
Async XLA Ops:
  3.3 11.7 %collective-permute-start.2 = (bf16[128,256]{1,0:T(8,128)(2,1)S(1)}, bf16[128,256]{1,0:T(8,128)(2,1)S(1)}, u32[]{:S(2)}, u32[]{:S(2)}) collective-permute-start(bf16[128,256]{1,0:T(8,128)(2,1)S(1)} %get-tuple-element.55), channel_id=1, source_target_pairs={{0,1},{1,0},{32,33},{33,32},{64,65},{65,64},{96,97},{97,96},{128,1... | collective-permute-start | bytes 196616 | tf_op jit(solution)/shard_map/ppermute | solution.py:31
  4.8 34.9 %all-to-all-start = ((bf16[16,64,256]{2,1,0:T(8,128)(2,1)}), bf16[16,64,256]{2,1,0:T(8,128)(2,1)S(1)}, u32[]{:S(2)}, u32[]{:S(2)}) async-start(bf16[16,64,256]{2,1,0:T(8,128)(2,1)} %get-tuple-element.52), calls=%async_computation | async-start | bytes 1048576 | tf_op jit(solution)/shard_map/all_to_all | solution.py:220
  13.4 11.1 %collective-permute-start = (bf16[128,256]{1,0:T(8,128)(2,1)S(1)}, bf16[128,256]{1,0:T(8,128)(2,1)S(1)}, u32[]{:S(2)}, u32[]{:S(2)}) collective-permute-start(bf16[128,256]{1,0:T(8,128)(2,1)S(1)} %get-tuple-element.54), channel_id=1, source_target_pairs={{0,64},{1,65},{32,96},{33,97},{64,0},{65,1},{96,32},{97,33},{128,1... | collective-permute-start | bytes 196616 | tf_op jit(solution)/shard_map/ppermute | solution.py:31
  15.0 6.5 %collective-permute-start.3 = (bf16[256,256]{1,0:T(8,128)(2,1)S(1)}, bf16[256,256]{1,0:T(8,128)(2,1)S(1)}, u32[]{:S(2)}, u32[]{:S(2)}) collective-permute-start(bf16[256,256]{1,0:T(8,128)(2,1)S(1)} %pad_maximum_fusion.1), channel_id=1, source_target_pairs={{0,33},{1,32},{32,1},{33,0},{64,97},{65,96},{96,65},{97,64},{128,1... | collective-permute-start | bytes 393224 | tf_op jit(solution)/shard_map/ppermute | solution.py:31
  21.6 17.1 %collective-permute-start.5 = (bf16[512,256]{1,0:T(8,128)(2,1)S(1)}, bf16[512,256]{1,0:T(8,128)(2,1)S(1)}, u32[]{:S(2)}, u32[]{:S(2)}) collective-permute-start(bf16[512,256]{1,0:T(8,128)(2,1)S(1)} %constant_dynamic-update-slice_fusion.3.refs_3_), channel_id=1, source_target_pairs={{0,128},{1,129},{32,160},{33,161},{64,192},{65,193},{96,224},{97,2... | collective-permute-start | bytes 786440 | tf_op jit(solution)/shard_map/ppermute | solution.py:31
  24.6 8.6 %collective-permute-start.1 = (bf16[256,256]{1,0:T(8,128)(2,1)S(1)}, bf16[256,256]{1,0:T(8,128)(2,1)S(1)}, u32[]{:S(2)}, u32[]{:S(2)}) collective-permute-start(bf16[256,256]{1,0:T(8,128)(2,1)S(1)} %pad_maximum_fusion), channel_id=1, source_target_pairs={{0,192},{1,193},{32,224},{33,225},{64,128},{65,129},{96,160},{97,1... | collective-permute-start | bytes 393224 | tf_op jit(solution)/shard_map/ppermute | solution.py:31
  33.2 10.9 %collective-permute-start.4 = (bf16[512,256]{1,0:T(8,128)(2,1)S(1)}, bf16[512,256]{1,0:T(8,128)(2,1)}, u32[]{:S(2)}, u32[]{:S(2)}) collective-permute-start(bf16[512,256]{1,0:T(8,128)(2,1)S(1)} %constant_dynamic-update-slice_fusion.refs_2_), channel_id=1, source_target_pairs={{0,32},{1,33},{32,0},{33,1},{64,96},{65,97},{96,64},{97,65},{128,1... | collective-permute-start | bytes 786440 | tf_op jit(solution)/shard_map/ppermute | solution.py:31
  34.8 11.9 %collective-permute-start.7 = (bf16[512,256]{1,0:T(8,128)(2,1)S(1)}, bf16[512,256]{1,0:T(8,128)(2,1)}, u32[]{:S(2)}, u32[]{:S(2)}) collective-permute-start(bf16[512,256]{1,0:T(8,128)(2,1)S(1)} %constant_dynamic-update-slice_fusion.3.refs_3_), channel_id=1, source_target_pairs={{0,64},{1,65},{32,96},{33,97},{64,0},{65,1},{96,32},{97,33},{128,1... | collective-permute-start | bytes 786440 | tf_op jit(solution)/shard_map/ppermute | solution.py:31
  35.2 12.9 %collective-permute-start.6 = (bf16[512,256]{1,0:T(8,128)(2,1)S(1)}, bf16[512,256]{1,0:T(8,128)(2,1)}, u32[]{:S(2)}, u32[]{:S(2)}) collective-permute-start(bf16[512,256]{1,0:T(8,128)(2,1)S(1)} %constant_dynamic-update-slice_fusion.refs_2_), channel_id=1, source_target_pairs={{0,1},{1,0},{32,33},{33,32},{64,65},{65,64},{96,97},{97,96},{128,1... | collective-permute-start | bytes 786440 | tf_op jit(solution)/shard_map/ppermute | solution.py:31
  36.7 16.2 %collective-permute-start.9 = (bf16[512,256]{1,0:T(8,128)(2,1)S(1)}, bf16[512,256]{1,0:T(8,128)(2,1)}, u32[]{:S(2)}, u32[]{:S(2)}) collective-permute-start(bf16[512,256]{1,0:T(8,128)(2,1)S(1)} %constant_dynamic-update-slice_fusion.3.refs_3_), channel_id=1, source_target_pairs={{0,192},{1,193},{32,224},{33,225},{64,128},{65,129},{96,160},{97,1... | collective-permute-start | bytes 786440 | tf_op jit(solution)/shard_map/ppermute | solution.py:31
  38.6 14.3 %collective-permute-start.8 = (bf16[512,256]{1,0:T(8,128)(2,1)S(1)}, bf16[512,256]{1,0:T(8,128)(2,1)}, u32[]{:S(2)}, u32[]{:S(2)}) collective-permute-start(bf16[512,256]{1,0:T(8,128)(2,1)S(1)} %constant_dynamic-update-slice_fusion.refs_2_), channel_id=1, source_target_pairs={{0,33},{1,32},{32,1},{33,0},{64,97},{65,96},{96,65},{97,64},{128,1... | collective-permute-start | bytes 786440 | tf_op jit(solution)/shard_map/ppermute | solution.py:31
  57.6 15.5 %collective-permute-start.10 = (f32[256,256]{1,0:T(8,128)S(1)}, f32[256,256]{1,0:T(8,128)S(1)}, u32[]{:S(2)}, u32[]{:S(2)}) collective-permute-start(f32[256,256]{1,0:T(8,128)S(1)} %get-tuple-element.70), channel_id=1, source_target_pairs={{0,1},{1,0},{2,3},{3,2},{4,5},{5,4},{6,7},{7,6},{8,9},{9,8},{10,11... | collective-permute-start | bytes 786440 | tf_op jit(solution)/shard_map/ppermute | solution.py:22
  58.2 19.1 %collective-permute-start.11 = (f32[256,256]{1,0:T(8,128)S(1)}, f32[256,256]{1,0:T(8,128)S(1)}, u32[]{:S(2)}, u32[]{:S(2)}) collective-permute-start(f32[256,256]{1,0:T(8,128)S(1)} %get-tuple-element.80.own_ref), channel_id=1, source_target_pairs={{0,1},{1,0},{2,3},{3,2},{4,5},{5,4},{6,7},{7,6},{8,9},{9,8},{10,11... | collective-permute-start | bytes 786440 | tf_op jit(solution)/shard_map/ppermute | solution.py:22
  78.5 39.7 %all-to-all-start.2 = ((bf16[16,4,16,256]{3,2,1,0:T(8,128)(2,1)}), bf16[16,4,16,256]{3,2,1,0:T(8,128)(2,1)S(1)}, u32[]{:S(2)}, u32[]{:S(2)}) async-start(bf16[16,4,16,256]{3,2,1,0:T(8,128)(2,1)} %copy-done.1), calls=%async_computation.2 | async-start | bytes 1048576 | tf_op jit(solution)/shard_map/all_to_all | solution.py:281
  83.3 11.1 %collective-permute-start.12 = (bf16[512,256]{1,0:T(8,128)(2,1)}, bf16[512,256]{1,0:T(8,128)(2,1)S(1)}, u32[]{:S(2)}, u32[]{:S(2)}) collective-permute-start(bf16[512,256]{1,0:T(8,128)(2,1)} %copy-done.19), channel_id=1, source_target_pairs={{0,32},{1,33},{32,0},{33,1},{64,96},{65,97},{96,64},{97,65},{128,1... | collective-permute-start | bytes 786440 | tf_op jit(solution)/shard_map/ppermute | solution.py:31
  87.8 11.1 %collective-permute-start.14 = (bf16[512,256]{1,0:T(8,128)(2,1)S(1)}, bf16[512,256]{1,0:T(8,128)(2,1)S(1)}, u32[]{:S(2)}, u32[]{:S(2)}) collective-permute-start(bf16[512,256]{1,0:T(8,128)(2,1)S(1)} %get-tuple-element.89), channel_id=1, source_target_pairs={{0,33},{1,32},{32,1},{33,0},{64,97},{65,96},{96,65},{97,64},{128,1... | collective-permute-start | bytes 786440 | tf_op jit(solution)/shard_map/ppermute | solution.py:31
  91.0 8.0 %collective-permute-start.13 = (bf16[512,256]{1,0:T(8,128)(2,1)S(1)}, bf16[512,256]{1,0:T(8,128)(2,1)S(1)}, u32[]{:S(2)}, u32[]{:S(2)}) collective-permute-start(bf16[512,256]{1,0:T(8,128)(2,1)S(1)} %get-tuple-element.86), channel_id=1, source_target_pairs={{0,1},{1,0},{32,33},{33,32},{64,65},{65,64},{96,97},{97,96},{128,1... | collective-permute-start | bytes 786440 | tf_op jit(solution)/shard_map/ppermute | solution.py:31
  91.3 10.7 %collective-permute-start.17 = (bf16[512,256]{1,0:T(8,128)(2,1)S(1)}, bf16[512,256]{1,0:T(8,128)(2,1)S(1)}, u32[]{:S(2)}, u32[]{:S(2)}) collective-permute-start(bf16[512,256]{1,0:T(8,128)(2,1)S(1)} %copy-done.18), channel_id=1, source_target_pairs={{0,128},{1,129},{32,160},{33,161},{64,192},{65,193},{96,224},{97,2... | collective-permute-start | bytes 786440 | tf_op jit(solution)/shard_map/ppermute | solution.py:31
  92.1 14.1 %collective-permute-start.19 = (bf16[512,256]{1,0:T(8,128)(2,1)S(1)}, bf16[512,256]{1,0:T(8,128)(2,1)S(1)}, u32[]{:S(2)}, u32[]{:S(2)}) collective-permute-start(bf16[512,256]{1,0:T(8,128)(2,1)S(1)} %get-tuple-element.97), channel_id=1, source_target_pairs={{0,192},{1,193},{32,224},{33,225},{64,128},{65,129},{96,160},{97,1... | collective-permute-start | bytes 786440 | tf_op jit(solution)/shard_map/ppermute | solution.py:31
  94.4 11.8 %collective-permute-start.18 = (bf16[512,256]{1,0:T(8,128)(2,1)S(1)}, bf16[512,256]{1,0:T(8,128)(2,1)S(1)}, u32[]{:S(2)}, u32[]{:S(2)}) collective-permute-start(bf16[512,256]{1,0:T(8,128)(2,1)S(1)} %get-tuple-element.96), channel_id=1, source_target_pairs={{0,64},{1,65},{32,96},{33,97},{64,0},{65,1},{96,32},{97,33},{128,1... | collective-permute-start | bytes 786440 | tf_op jit(solution)/shard_map/ppermute | solution.py:31
  99.0 9.8 %collective-permute-start.15 = (bf16[256,256]{1,0:T(8,128)(2,1)S(1)}, bf16[256,256]{1,0:T(8,128)(2,1)S(1)}, u32[]{:S(2)}, u32[]{:S(2)}) collective-permute-start(bf16[256,256]{1,0:T(8,128)(2,1)S(1)} %get-tuple-element.91), channel_id=1, source_target_pairs={{0,192},{1,193},{32,224},{33,225},{64,128},{65,129},{96,160},{97,1... | collective-permute-start | bytes 393224 | tf_op jit(solution)/shard_map/ppermute | solution.py:31
  106.3 6.6 %collective-permute-start.20 = (bf16[256,256]{1,0:T(8,128)(2,1)S(1)}, bf16[256,256]{1,0:T(8,128)(2,1)S(1)}, u32[]{:S(2)}, u32[]{:S(2)}) collective-permute-start(bf16[256,256]{1,0:T(8,128)(2,1)S(1)} %get-tuple-element.99), channel_id=1, source_target_pairs={{0,33},{1,32},{32,1},{33,0},{64,97},{65,96},{96,65},{97,64},{128,1... | collective-permute-start | bytes 393224 | tf_op jit(solution)/shard_map/ppermute | solution.py:31
  108.9 4.5 %collective-permute-start.16 = (bf16[128,256]{1,0:T(8,128)(2,1)S(1)}, bf16[128,256]{1,0:T(8,128)(2,1)S(1)}, u32[]{:S(2)}, u32[]{:S(2)}) collective-permute-start(bf16[128,256]{1,0:T(8,128)(2,1)S(1)} %get-tuple-element.93), channel_id=1, source_target_pairs={{0,64},{1,65},{32,96},{33,97},{64,0},{65,1},{96,32},{97,33},{128,1... | collective-permute-start | bytes 196616 | tf_op jit(solution)/shard_map/ppermute | solution.py:31
  112.9 4.4 %collective-permute-start.21 = (bf16[128,256]{1,0:T(8,128)(2,1)S(1)}, bf16[128,256]{1,0:T(8,128)(2,1)S(1)}, u32[]{:S(2)}, u32[]{:S(2)}) collective-permute-start(bf16[128,256]{1,0:T(8,128)(2,1)S(1)} %get-tuple-element.101), channel_id=1, source_target_pairs={{0,1},{1,0},{32,33},{33,32},{64,65},{65,64},{96,97},{97,96},{128,1... | collective-permute-start | bytes 196616 | tf_op jit(solution)/shard_map/ppermute | solution.py:31
  (20 other events, 110.9 us)

commit v3 on v2

--- a/solution.py
+++ b/solution.py
@@ -62,11 +62,16 @@
     return jnp.concatenate(parts, axis=1)
 
 
-def split_kernel(proto_ref, emb_ref, first_ref, second_ref, own_ref, spread_ref):
+def split_kernel(
+    proto_ref, emb_ref, first_ref, second_ref, own_ref, spread_ref, proto_buf, emb_buf, sem_a, sem_b
+):
+    proto_copy, emb_copy = fetch((proto_ref, emb_ref), (proto_buf, emb_buf), (sem_a, sem_b))
     half = first_ref.shape[0]
-    first_ref[...] = proto_ref[:half]
-    second_ref[...] = proto_ref[half:]
-    emb = emb_ref[...].astype(f32)
+    proto_copy.wait()
+    first_ref[...] = proto_buf[:half]
+    second_ref[...] = proto_buf[half:]
+    emb_copy.wait()
+    emb = emb_buf[...].astype(f32)
     own = jnp.concatenate([emb[:, crop] for crop in range(emb.shape[1])]).astype(bf16)
     own_ref[...] = own.reshape(own_ref.shape)
     for peer in range(spread_ref.shape[0]):
@@ -84,31 +89,40 @@
     z_t_ref[...] = z.reshape(-1, features).T.astype(bf16)
 
 
-def scores_kernel(*refs, distance, first, last):
-    z_t_ref, code_ref = refs[:2]
-    before = () if first else refs[2:5]
-    refs = refs[2 + len(before) :]
-    raw_refs, exp_refs, (soft_ref, own_ref, total_ref) = refs[:2], refs[2:4], refs[4:]
+def scores_kernel(*refs, distance, n_before):
+    z_t_ref, code_ref, *raw_refs = refs[:4]
+    own_before, acc_before = refs[4 : 4 + n_before], refs[4 + n_before : 4 + 2 * n_before]
+    exp_a_ref, exp_b_ref, soft_ref, own_ref, total_ref = refs[4 + 2 * n_before : 9 + 2 * n_before]
+    raw_bufs, copies = raw_refs, ()
+    if distance:
+        raw_bufs, semaphores = refs[-4:-2], refs[-2:]
+        copies = fetch(raw_refs, raw_bufs, semaphores)
     rows = z_t_ref.shape[1]
-    soft, own, acc = (None, None, None) if first else (ref[...] for ref in before)
+    soft = own = acc = None
     add = lambda a, b: b if a is None else a + b
-    for kind in kinds:
-        c = normalize_rows(raw_refs[kind][...])[0].astype(bf16)
+    for kind, exp_ref in zip(kinds, (exp_a_ref, exp_b_ref)):
+        if copies:
+            copies[kind].wait()
+        c = normalize_rows(raw_bufs[kind][...])[0].astype(bf16)
         exponent = jnp.exp(dot(c, z_t_ref[...], 1, 0) * sharpness)
         acc = add(acc, jnp.sum(exponent.reshape(-1, 8, rows), axis=0))
         exponent = exponent.astype(bf16)
-        exp_refs[kind][...] = exponent
+        exp_ref[...] = exponent
         soft = add(soft, dot(c, exponent, 0, 0))
         own = add(own, dot(code_columns(code_ref, kind, distance), c, 1, 0))
     soft_ref[...] = soft
+    for before in own_before:
+        own = own + before[...]
     own_ref[...] = own
-    if last:
-        totals = jnp.sum(acc, axis=0, keepdims=True)
-        for r in range(rows // 128):
-            lanes = jnp.broadcast_to(totals[:, r * 128 : (r + 1) * 128], (total_ref.shape[0], 128))
-            total_ref[:, r] = lanes
-    else:
+    if not n_before:
         total_ref[...] = acc
+        return
+    for before in acc_before:
+        acc = acc + before[...]
+    totals = jnp.sum(acc, axis=0, keepdims=True)
+    for r in range(rows // 128):
+        lanes = jnp.broadcast_to(totals[:, r * 128 : (r + 1) * 128], (total_ref.shape[0], 128))
+        total_ref[:, r] = lanes
 
 
 def prototypes_kernel(*refs, distance, crops, own_images, first):
@@ -130,11 +144,13 @@
         out_ref[...] = grads.astype(out_ref.dtype)
 
 
-def rows_kernel(totals_ref, soft_ref, own_ref, other_ref, out_ref, *, crops, own_images):
+def rows_kernel(totals_ref, own_ref, other_ref, *refs, crops, own_images):
+    *soft_refs, out_ref = refs
+    soft_sum = sum(ref[...] for ref in soft_refs[1:]) + soft_refs[0][...]
     weights = row_weights(totals_ref, crops, own_images)
     n_proto = out_ref.shape[0]
     features = out_ref.shape[3]
-    soft = (soft_ref[...] * weights).T.reshape(n_proto, crops, own_images, features)
+    soft = (soft_sum * weights).T.reshape(n_proto, crops, own_images, features)
     own = own_ref[...].reshape(n_proto, own_images, features)
     other = other_ref[...].reshape(n_proto, own_images, features)
     for crop in range(crops):
@@ -151,10 +167,14 @@
 
 
 def far_sum_kernel(held_ref, *refs):
-    parts, (keep_ref, send_ref) = refs[:-2], refs[-2:]
+    n = len(arrivals)
+    sources, (keep_ref, send_ref), refs = refs[:n], refs[n : n + 2], refs[n + 2 :]
+    buffers, semaphores = refs[:n], refs[n:]
+    copies = fetch(sources, buffers, semaphores)
     total = held_ref[...]
-    for part in parts:
-        total = total + part[...].astype(f32)
+    for copy, buffer in zip(copies, buffers):
+        copy.wait()
+        total = total + buffer[...].astype(f32)
     half = total.shape[0] // 2
     keep_ref[...] = total[:half]
     send_ref[...] = total[half:].astype(bf16)
@@ -181,15 +201,28 @@
     return jax.ShapeDtypeStruct(dims, dtype)
 
 
-def call(kernel, out_shape, *operands, mib=12):
+def call(kernel, out_shape, *operands, mib=12, fetched=(), scratch=()):
     kept = pl.BlockSpec(memory_space=pltpu.VMEM)
+    there = pl.BlockSpec(memory_space=pl.ANY)
     return pl.pallas_call(
         kernel,
         out_shape=out_shape,
-        in_specs=[kept] * len(operands),
+        in_specs=[there if i in fetched else kept for i in range(len(operands))],
         out_specs=jax.tree.map(lambda _: kept, out_shape),
+        scratch_shapes=[
+            *(pltpu.VMEM(operands[i].shape, operands[i].dtype) for i in fetched),
+            *(pltpu.SemaphoreType.DMA(()) for _ in fetched),
+            *scratch,
+        ],
         compiler_params=pltpu.CompilerParams(vmem_limit_bytes=mib << 20),
     )(*operands)
+
+
+def fetch(sources, buffers, semaphores):
+    copies = [pltpu.make_async_copy(*each) for each in zip(sources, buffers, semaphores)]
+    for copy in copies:
+        copy.start()
+    return copies
 
 
 def on_device(embeddings, codes, prototypes):
@@ -209,15 +242,15 @@
             shape(crops, own_images, features, dtype=bf16),
             shape(n_proto, own_rows, features, dtype=bf16),
         ],
-        prototypes[0], embeddings[:, 0],
-    )
-    for step, distance in enumerate((1, 3)):
-        moved = []
+        *(pltpu.with_memory_space_constraint(x, pltpu.HBM) for x in (prototypes[0], embeddings[:, 0])),
+        fetched=(0, 1),
+    )
+    blocks = [[halves[kind]] for kind in kinds]
+    for j in near[1:]:
         for kind in kinds:
-            moved.append(exchange(halves[kind], kind, distance))
-        halves = [jnp.concatenate(pair) for pair in zip(halves, moved)]
-        if step == 0:
-            raw_emb = lax.all_to_all(spread_emb, "proto", 0, 0)
+            blocks[kind].append(exchange(halves[kind], kind, j))
+    halves = [jnp.concatenate(each) for each in blocks]
+    raw_emb = lax.all_to_all(spread_emb, "proto", 0, 0)
     gathered = {0: halves}
     for d in arrivals:
         gathered[d] = []
@@ -231,17 +264,20 @@
     )
 
     exponents = {}
-    state = ()
+    soft, own_sums, sums = [], [], []
     for d in (0, *arrivals):
-        last = d == arrivals[-1]
-        total_dims = (n_proto, rows // 128, 128) if last else (8, rows)
-        *exponents[d], soft, own_term, totals = call(
-            functools.partial(scores_kernel, distance=d, first=not state, last=last),
+        before = (*own_sums, *sums) if d == arrivals[-1] else ()
+        total_dims = (n_proto, rows // 128, 128) if before else (8, rows)
+        *exponents[d], soft_part, own_term, totals = call(
+            functools.partial(scores_kernel, distance=d, n_before=len(before) // 2),
             [shape(side * half, rows, dtype=bf16)] * 2
             + [shape(features, rows), shape(images, features), shape(*total_dims)],
-            z_t, code, *state, *gathered[d],
+            z_t, code, *gathered[d], *before,
+            fetched=(2, 3) if d else (),
         )
-        state = (soft, own_term, totals)
+        soft.append(soft_part)
+        own_sums.append(own_term)
+        sums.append(totals)
     totals, outgoing = lax.optimization_barrier((totals, outgoing))
     incoming = swapped(outgoing)
     other_term = swapped(own_term)
@@ -270,13 +306,13 @@
                 arrived[kind].insert(0, parts[kind])
 
     held_parts = [arrived[kind][0] for kind in kinds]
-    soft, *held_parts = lax.optimization_barrier((soft, *held_parts))
+    soft[0], *held_parts = lax.optimization_barrier((soft[0], *held_parts))
     for kind in kinds:
         arrived[kind][0] = held_parts[kind]
     row_parts = call(
         functools.partial(rows_kernel, crops=crops, own_images=own_images),
         shape(n_proto, crops, own_images, features, dtype=bf16),
-        totals, soft, own_term, other_term,
+        totals, own_term, other_term, *soft,
     )
     row_parts = lax.all_to_all(row_parts, "proto", 0, 0)
 
@@ -286,6 +322,7 @@
             far_sum_kernel,
             [shape(2 * half, features), shape(2 * half, features, dtype=bf16)],
             *arrived[kind],
+            fetched=tuple(range(1, len(arrived[kind]))),
         )
         held.append((keep, exchange(send, kind, 3)))
     operands = []

time: 120 us -> 114 us (0.950)
  waiting for transfers between devices: 33.6 us -> 21.6 us
  starting transfers between devices: 42.2 us -> 45.8 us
  Pallas kernels: 17.5 us -> 20.3 us
    ppermute x20 -> x22, waiting for transfers between devices: 33.6 us -> 21.6 us  [exchange(): lax.ppermute(value, owners, [(owner, owner ^ mask) for owner in range(sid...]
    ppermute x20 -> x22, starting transfers between devices: 26.9 us -> 30.5 us  [exchange(): lax.ppermute(value, owners, [(owner, owner ^ mask) for owner in range(sid...]
    pallas_call x17, Pallas kernels: 17.5 us -> 20.3 us  [call(): pl.pallas_call(kernel, out_shape=out_shape, in_specs=[there if i in fetch...]
    unnamed x43 -> x42, local copies, waits for them, and re-layouts: 11.3 us -> 10.5 us
  transfers between devices with their start and end apart: 24 -> 26, of which waited for: 10 -> 7; matrix products, arithmetic and copies ran while one was open for 0% -> 2% of each run, Pallas kernels for 11% -> 12%
where the time goes in v3:
time: 114 us
  starting transfers between devices  45.8 us (40%)
  waiting for transfers between devices  21.6 us (19%)
  Pallas kernels  20.3 us (18%)
  blocking collectives  13.5 us (12%)
  local copies, waits for them, and re-layouts  11.4 us (10%)
    ppermute x22, starting transfers between devices, exchange(): lax.ppermute(value, owners, [(owner, owner ^ mask) for owner in range(sid...  30.5 us
    ppermute x22, waiting for transfers between devices, exchange(): lax.ppermute(value, owners, [(owner, owner ^ mask) for owner in range(sid...  21.6 us
    pallas_call x17, Pallas kernels, call(): pl.pallas_call(kernel, out_shape=out_shape, in_specs=[there if i in fetch...  20.3 us
    all_to_all x1, blocking collectives, on_device(): totals = lax.all_to_all(totals, 'proto', 0, 0)  13.5 us
    unnamed x42, local copies, waits for them, and re-layouts  10.5 us
    all_to_all x1, starting transfers between devices, on_device(): raw_emb = lax.all_to_all(spread_emb, 'proto', 0, 0)  8.59 us
    all_to_all x1, starting transfers between devices, on_device(): row_parts = lax.all_to_all(row_parts, 'proto', 0, 0)  4.76 us
  transfers between devices with their start and end apart: 26, of which 7 were waited for; matrix products, arithmetic and copies ran while one was open for 2% of the time, Pallas kernels for 12%

profile of v3, /device:TPU:32, one launch (start us, length us, event | category | flops | bytes accessed | tf_op | source)
XLA Modules:
  0.0 113.5 jit_solution(17192705036233194905)
XLA Ops:
  0.6 2.0 %shard_map.50 = (bf16[128,256]{1,0:T(8,128)(2,1)S(1)}, bf16[128,256]{1,0:T(8,128)(2,1)S(1)}, bf16[4,16,256]{2,1,0:T(8,128)(2,1)S(1)}, bf16[16,64,256]{2,1,0:T(8,128)(2,1)}) custom-call(bf16[256,256]{1,0:T(8,128)(2,1)} %bitcast.17, bf16[16,4,256]{2,1,0:T(4,128)(2,1)} %bitcast.21), custom_call_target="tpu_custom_call" | custom-call | tf_op jit(solution)/shard_map/pallas_call | solution.py:207
  2.6 3.3 %collective-permute-start.2 = (bf16[128,256]{1,0:T(8,128)(2,1)S(1)}, bf16[128,256]{1,0:T(8,128)(2,1)}, u32[]{:S(2)}, u32[]{:S(2)}) collective-permute-start(bf16[128,256]{1,0:T(8,128)(2,1)S(1)} %get-tuple-element.54), channel_id=1, source_target_pairs={{0,128},{1,129},{32,160},{33,161},{64,192},{65,193},{96,224},{97,2... | collective-permute-start | bytes 196616 | tf_op jit(solution)/shard_map/ppermute | solution.py:31
  6.9 3.0 %collective-permute-start.6 = (bf16[128,256]{1,0:T(8,128)(2,1)S(1)}, bf16[128,256]{1,0:T(8,128)(2,1)S(1)}, u32[]{:S(2)}, u32[]{:S(2)}) collective-permute-start(bf16[128,256]{1,0:T(8,128)(2,1)S(1)} %get-tuple-element.55), channel_id=1, source_target_pairs={{0,32},{1,33},{32,0},{33,1},{64,96},{65,97},{96,64},{97,65},{128,1... | collective-permute-start | bytes 196616 | tf_op jit(solution)/shard_map/ppermute | solution.py:31
  10.6 8.6 %all-to-all-start = ((bf16[16,64,256]{2,1,0:T(8,128)(2,1)}), bf16[16,64,256]{2,1,0:T(8,128)(2,1)S(1)}, u32[]{:S(2)}, u32[]{:S(2)}) async-start(bf16[16,64,256]{2,1,0:T(8,128)(2,1)} %get-tuple-element.52), calls=%async_computation | async-start | bytes 1048576 | tf_op jit(solution)/shard_map/all_to_all | solution.py:253
  19.8 4.9 %collective-permute-done.5 = bf16[128,256]{1,0:T(8,128)(2,1)S(1)} collective-permute-done((bf16[128,256]{1,0:T(8,128)(2,1)S(1)}, bf16[128,256]{1,0:T(8,128)(2,1)S(1)}, u32[]{:S(2)}, u32[]{:S(2)}) %collective-permute-start.5) | collective-permute-done | bytes 65568 | tf_op jit(solution)/shard_map/ppermute | solution.py:31
  24.8 2.1 %collective-permute-start.11 = (bf16[512,256]{1,0:T(8,128)(2,1)S(1)}, bf16[512,256]{1,0:T(8,128)(2,1)S(1)}, u32[]{:S(2)}, u32[]{:S(2)}) collective-permute-start(bf16[512,256]{1,0:T(8,128)(2,1)S(1)} %constant_dynamic-update-slice_fusion.4.refs_3_), channel_id=1, source_target_pairs={{0,64},{1,65},{32,96},{33,97},{64,0},{65,1},{96,32},{97,33},{128,1... | collective-permute-start | bytes 786440 | tf_op jit(solution)/shard_map/ppermute | solution.py:31
  29.6 1.7 %collective-permute-start.9 = (bf16[512,256]{1,0:T(8,128)(2,1)S(1)}, bf16[512,256]{1,0:T(8,128)(2,1)}, u32[]{:S(2)}, u32[]{:S(2)}) collective-permute-start(bf16[512,256]{1,0:T(8,128)(2,1)S(1)} %constant_dynamic-update-slice_fusion.4.refs_3_), channel_id=1, source_target_pairs={{0,128},{1,129},{32,160},{33,161},{64,192},{65,193},{96,224},{97,2... | collective-permute-start | bytes 786440 | tf_op jit(solution)/shard_map/ppermute | solution.py:31
  31.3 1.8 %collective-permute-start.8 = (bf16[512,256]{1,0:T(8,128)(2,1)S(1)}, bf16[512,256]{1,0:T(8,128)(2,1)}, u32[]{:S(2)}, u32[]{:S(2)}) collective-permute-start(bf16[512,256]{1,0:T(8,128)(2,1)S(1)} %constant_dynamic-update-slice_fusion.refs_2_), channel_id=1, source_target_pairs={{0,32},{1,33},{32,0},{33,1},{64,96},{65,97},{96,64},{97,65},{128,1... | collective-permute-start | bytes 786440 | tf_op jit(solution)/shard_map/ppermute | solution.py:31
  34.1 2.7 %collective-permute-start.3 = (bf16[512,256]{1,0:T(8,128)(2,1)S(1)}, bf16[512,256]{1,0:T(8,128)(2,1)}, u32[]{:S(2)}, u32[]{:S(2)}) collective-permute-start(bf16[512,256]{1,0:T(8,128)(2,1)S(1)} %constant_dynamic-update-slice_fusion.refs_2_), channel_id=1, source_target_pairs={{0,33},{1,32},{32,1},{33,0},{64,97},{65,96},{96,65},{97,64},{128,1... | collective-permute-start | bytes 786440 | tf_op jit(solution)/shard_map/ppermute | solution.py:31
  37.5 1.8 %shard_map.52 = (bf16[512,1024]{1,0:T(8,128)(2,1)S(1)}, bf16[512,1024]{1,0:T(8,128)(2,1)S(1)}, f32[256,1024]{1,0:T(8,128)S(1)}, f32[256,256]{1,0:T(8,128)S(1)}, f32[8,1024]{1,0:T(8,128)S(1)}) custom-call(bf16[256,1024]{1,0:T(8,128)(2,1)S(1)} %get-tuple-element.53.refs_0_.refs_1_, bf16[256,4096]{1,0:T(8,128)(2,1)S(1)} %bitcast.8, ...), custom_call_target="tpu_custom_call" | custom-call | tf_op jit(solution)/shard_map/pallas_call | solution.py:207
  39.2 3.1 %shard_map.54 = (bf16[512,1024]{1,0:T(8,128)(2,1)S(1)}, bf16[512,1024]{1,0:T(8,128)(2,1)S(1)}, f32[256,1024]{1,0:T(8,128)S(1)}, f32[256,256]{1,0:T(8,128)S(1)}, f32[8,1024]{1,0:T(8,128)S(1)}) custom-call(bf16[256,1024]{1,0:T(8,128)(2,1)S(1)} %get-tuple-element.53.refs_0_.refs_1_, bf16[256,4096]{1,0:T(8,128)(2,1)S(1)} %bitcast.9, ...), custom_call_target="tpu_custom_call" | custom-call | tf_op jit(solution)/shard_map/pallas_call | solution.py:207
  44.4 3.1 %shard_map.53 = (bf16[512,1024]{1,0:T(8,128)(2,1)S(1)}, bf16[512,1024]{1,0:T(8,128)(2,1)S(1)}, f32[256,1024]{1,0:T(8,128)S(1)}, f32[256,256]{1,0:T(8,128)S(1)}, f32[8,1024]{1,0:T(8,128)S(1)}) custom-call(bf16[256,1024]{1,0:T(8,128)(2,1)S(1)} %get-tuple-element.53.refs_0_.refs_1_, bf16[256,4096]{1,0:T(8,128)(2,1)S(1)} %bitcast.10, ...), custom_call_target="tpu_custom_call" | custom-call | tf_op jit(solution)/shard_map/pallas_call | solution.py:207
  47.6 3.2 %shard_map.55 = (bf16[512,1024]{1,0:T(8,128)(2,1)S(1)}, bf16[512,1024]{1,0:T(8,128)(2,1)S(1)}, f32[256,1024]{1,0:T(8,128)S(1)}, f32[256,256]{1,0:T(8,128)S(1)}, f32[16,8,128]{2,1,0:T(8,128)S(1)}) custom-call(bf16[256,1024]{1,0:T(8,128)(2,1)S(1)} %get-tuple-element.53.refs_0_.refs_1_, bf16[256,4096]{1,0:T(8,128)(2,1)S(1)} %bitcast.11, ...), custom_call_target="tpu_custom_call" | custom-call | tf_op jit(solution)/shard_map/pallas_call | solution.py:207
  52.7 2.0 %collective-permute-start.12 = (f32[256,256]{1,0:T(8,128)S(1)}, f32[256,256]{1,0:T(8,128)S(1)}, u32[]{:S(2)}, u32[]{:S(2)}) collective-permute-start(f32[256,256]{1,0:T(8,128)S(1)} %get-tuple-element.65.own_ref), channel_id=1, source_target_pairs={{0,1},{1,0},{2,3},{3,2},{4,5},{5,4},{6,7},{7,6},{8,9},{9,8},{10,11... | collective-permute-start | bytes 786440 | tf_op jit(solution)/shard_map/ppermute | solution.py:22
  54.7 13.5 %all_to_all.15.refs_0_.totals_ref = f32[16,8,128]{2,1,0:T(8,128)S(1)} all-to-all(f32[16,8,128]{2,1,0:T(8,128)S(1)} %get-tuple-element.64), channel_id=1, replica_groups=mesh['dp'=8,'proto'=16,'crop'=2] {'proto'}, dimensions={0} | all-to-all | bytes 131072 | tf_op jit(solution)/shard_map/all_to_all | solution.py:284
  72.9 4.8 %all-to-all-start.2 = ((bf16[16,4,16,256]{3,2,1,0:T(8,128)(2,1)}), bf16[16,4,16,256]{3,2,1,0:T(8,128)(2,1)S(1)}, u32[]{:S(2)}, u32[]{:S(2)}) async-start(bf16[16,4,16,256]{3,2,1,0:T(8,128)(2,1)} %copy-done.1), calls=%async_computation.2 | async-start | bytes 1048576 | tf_op jit(solution)/shard_map/all_to_all | solution.py:317
  82.3 1.6 %collective-permute-start.16 = (bf16[512,256]{1,0:T(8,128)(2,1)S(1)}, bf16[512,256]{1,0:T(8,128)(2,1)S(1)}, u32[]{:S(2)}, u32[]{:S(2)}) collective-permute-start(bf16[512,256]{1,0:T(8,128)(2,1)S(1)} %get-tuple-element.89), channel_id=1, source_target_pairs={{0,33},{1,32},{32,1},{33,0},{64,97},{65,96},{96,65},{97,64},{128,1... | collective-permute-start | bytes 786440 | tf_op jit(solution)/shard_map/ppermute | solution.py:31
  85.7 2.4 %collective-permute-start.19 = (bf16[512,256]{1,0:T(8,128)(2,1)S(1)}, bf16[512,256]{1,0:T(8,128)(2,1)S(1)}, u32[]{:S(2)}, u32[]{:S(2)}) collective-permute-start(bf16[512,256]{1,0:T(8,128)(2,1)S(1)} %copy-done.16), channel_id=1, source_target_pairs={{0,128},{1,129},{32,160},{33,161},{64,192},{65,193},{96,224},{97,2... | collective-permute-start | bytes 786440 | tf_op jit(solution)/shard_map/ppermute | solution.py:31
  89.2 4.2 %collective-permute-done.16.refs_2_ = bf16[512,256]{1,0:T(8,128)(2,1)S(1)} collective-permute-done((bf16[512,256]{1,0:T(8,128)(2,1)S(1)}, bf16[512,256]{1,0:T(8,128)(2,1)S(1)}, u32[]{:S(2)}, u32[]{:S(2)}) %collective-permute-start.16) | collective-permute-done | bytes 262176 | tf_op jit(solution)/shard_map/ppermute | solution.py:31
  93.7 2.3 %collective-permute-start.17 = (bf16[256,256]{1,0:T(8,128)(2,1)S(1)}, bf16[256,256]{1,0:T(8,128)(2,1)S(1)}, u32[]{:S(2)}, u32[]{:S(2)}) collective-permute-start(bf16[256,256]{1,0:T(8,128)(2,1)S(1)} %get-tuple-element.91), channel_id=1, source_target_pairs={{0,192},{1,193},{32,224},{33,225},{64,128},{65,129},{96,160},{97,1... | collective-permute-start | bytes 393224 | tf_op jit(solution)/shard_map/ppermute | solution.py:31
  96.4 4.0 %collective-permute-done.21.refs_2_ = bf16[512,256]{1,0:T(8,128)(2,1)S(1)} collective-permute-done((bf16[512,256]{1,0:T(8,128)(2,1)S(1)}, bf16[512,256]{1,0:T(8,128)(2,1)S(1)}, u32[]{:S(2)}, u32[]{:S(2)}) %collective-permute-start.21) | collective-permute-done | bytes 262176 | tf_op jit(solution)/shard_map/ppermute | solution.py:31
  100.7 1.9 %collective-permute-start.22 = (bf16[256,256]{1,0:T(8,128)(2,1)S(1)}, bf16[256,256]{1,0:T(8,128)(2,1)S(1)}, u32[]{:S(2)}, u32[]{:S(2)}) collective-permute-start(bf16[256,256]{1,0:T(8,128)(2,1)S(1)} %get-tuple-element.99), channel_id=1, source_target_pairs={{0,33},{1,32},{32,1},{33,0},{64,97},{65,96},{96,65},{97,64},{128,1... | collective-permute-start | bytes 393224 | tf_op jit(solution)/shard_map/ppermute | solution.py:31
  104.0 3.3 %collective-permute-done.22.part_ref = bf16[256,256]{1,0:T(8,128)(2,1)S(1)} collective-permute-done((bf16[256,256]{1,0:T(8,128)(2,1)S(1)}, bf16[256,256]{1,0:T(8,128)(2,1)S(1)}, u32[]{:S(2)}, u32[]{:S(2)}) %collective-permute-start.22) | collective-permute-done | bytes 131104 | tf_op jit(solution)/shard_map/ppermute | solution.py:31
  107.5 4.2 %collective-permute-done.23.part_b_ref = bf16[128,256]{1,0:T(8,128)(2,1)S(1)} collective-permute-done((bf16[128,256]{1,0:T(8,128)(2,1)S(1)}, bf16[128,256]{1,0:T(8,128)(2,1)S(1)}, u32[]{:S(2)}, u32[]{:S(2)}) %collective-permute-start.23) | collective-permute-done | bytes 65568 | tf_op jit(solution)/shard_map/ppermute | solution.py:31
  (90 shorter events, 27.2 us)
Async XLA Ops:
  2.6 26.0 %collective-permute-start.2 = (bf16[128,256]{1,0:T(8,128)(2,1)S(1)}, bf16[128,256]{1,0:T(8,128)(2,1)}, u32[]{:S(2)}, u32[]{:S(2)}) collective-permute-start(bf16[128,256]{1,0:T(8,128)(2,1)S(1)} %get-tuple-element.54), channel_id=1, source_target_pairs={{0,128},{1,129},{32,160},{33,161},{64,192},{65,193},{96,224},{97,2... | collective-permute-start | bytes 196616 | tf_op jit(solution)/shard_map/ppermute | solution.py:31
  5.9 21.8 %collective-permute-start.1 = (bf16[128,256]{1,0:T(8,128)(2,1)S(1)}, bf16[128,256]{1,0:T(8,128)(2,1)}, u32[]{:S(2)}, u32[]{:S(2)}) collective-permute-start(bf16[128,256]{1,0:T(8,128)(2,1)S(1)} %get-tuple-element.54), channel_id=1, source_target_pairs={{0,192},{1,193},{32,224},{33,225},{64,128},{65,129},{96,160},{97,1... | collective-permute-start | bytes 196616 | tf_op jit(solution)/shard_map/ppermute | solution.py:31
  6.9 19.9 %collective-permute-start = (bf16[128,256]{1,0:T(8,128)(2,1)S(1)}, bf16[128,256]{1,0:T(8,128)(2,1)}, u32[]{:S(2)}, u32[]{:S(2)}) collective-permute-start(bf16[128,256]{1,0:T(8,128)(2,1)S(1)} %get-tuple-element.54), channel_id=1, source_target_pairs={{0,64},{1,65},{32,96},{33,97},{64,0},{65,1},{96,32},{97,33},{128,1... | collective-permute-start | bytes 196616 | tf_op jit(solution)/shard_map/ppermute | solution.py:31
  6.9 17.8 %collective-permute-start.6 = (bf16[128,256]{1,0:T(8,128)(2,1)S(1)}, bf16[128,256]{1,0:T(8,128)(2,1)S(1)}, u32[]{:S(2)}, u32[]{:S(2)}) collective-permute-start(bf16[128,256]{1,0:T(8,128)(2,1)S(1)} %get-tuple-element.55), channel_id=1, source_target_pairs={{0,32},{1,33},{32,0},{33,1},{64,96},{65,97},{96,64},{97,65},{128,1... | collective-permute-start | bytes 196616 | tf_op jit(solution)/shard_map/ppermute | solution.py:31
  10.0 9.2 %collective-permute-start.4 = (bf16[128,256]{1,0:T(8,128)(2,1)S(1)}, bf16[128,256]{1,0:T(8,128)(2,1)S(1)}, u32[]{:S(2)}, u32[]{:S(2)}) collective-permute-start(bf16[128,256]{1,0:T(8,128)(2,1)S(1)} %get-tuple-element.55), channel_id=1, source_target_pairs={{0,1},{1,0},{32,33},{33,32},{64,65},{65,64},{96,97},{97,96},{128,1... | collective-permute-start | bytes 196616 | tf_op jit(solution)/shard_map/ppermute | solution.py:31
  10.6 26.3 %all-to-all-start = ((bf16[16,64,256]{2,1,0:T(8,128)(2,1)}), bf16[16,64,256]{2,1,0:T(8,128)(2,1)S(1)}, u32[]{:S(2)}, u32[]{:S(2)}) async-start(bf16[16,64,256]{2,1,0:T(8,128)(2,1)} %get-tuple-element.52), calls=%async_computation | async-start | bytes 1048576 | tf_op jit(solution)/shard_map/all_to_all | solution.py:253
  19.2 5.6 %collective-permute-start.5 = (bf16[128,256]{1,0:T(8,128)(2,1)S(1)}, bf16[128,256]{1,0:T(8,128)(2,1)S(1)}, u32[]{:S(2)}, u32[]{:S(2)}) collective-permute-start(bf16[128,256]{1,0:T(8,128)(2,1)S(1)} %get-tuple-element.55), channel_id=1, source_target_pairs={{0,33},{1,32},{32,1},{33,0},{64,97},{65,96},{96,65},{97,64},{128,1... | collective-permute-start | bytes 196616 | tf_op jit(solution)/shard_map/ppermute | solution.py:31
  24.8 9.4 %collective-permute-start.11 = (bf16[512,256]{1,0:T(8,128)(2,1)S(1)}, bf16[512,256]{1,0:T(8,128)(2,1)S(1)}, u32[]{:S(2)}, u32[]{:S(2)}) collective-permute-start(bf16[512,256]{1,0:T(8,128)(2,1)S(1)} %constant_dynamic-update-slice_fusion.4.refs_3_), channel_id=1, source_target_pairs={{0,64},{1,65},{32,96},{33,97},{64,0},{65,1},{96,32},{97,33},{128,1... | collective-permute-start | bytes 786440 | tf_op jit(solution)/shard_map/ppermute | solution.py:31
  29.4 9.8 %collective-permute-start.10 = (bf16[512,256]{1,0:T(8,128)(2,1)S(1)}, bf16[512,256]{1,0:T(8,128)(2,1)}, u32[]{:S(2)}, u32[]{:S(2)}) collective-permute-start(bf16[512,256]{1,0:T(8,128)(2,1)S(1)} %constant_dynamic-update-slice_fusion.refs_2_), channel_id=1, source_target_pairs={{0,1},{1,0},{32,33},{33,32},{64,65},{65,64},{96,97},{97,96},{128,1... | collective-permute-start | bytes 786440 | tf_op jit(solution)/shard_map/ppermute | solution.py:31
  29.6 14.7 %collective-permute-start.9 = (bf16[512,256]{1,0:T(8,128)(2,1)S(1)}, bf16[512,256]{1,0:T(8,128)(2,1)}, u32[]{:S(2)}, u32[]{:S(2)}) collective-permute-start(bf16[512,256]{1,0:T(8,128)(2,1)S(1)} %constant_dynamic-update-slice_fusion.4.refs_3_), channel_id=1, source_target_pairs={{0,128},{1,129},{32,160},{33,161},{64,192},{65,193},{96,224},{97,2... | collective-permute-start | bytes 786440 | tf_op jit(solution)/shard_map/ppermute | solution.py:31
  31.3 13.0 %collective-permute-start.8 = (bf16[512,256]{1,0:T(8,128)(2,1)S(1)}, bf16[512,256]{1,0:T(8,128)(2,1)}, u32[]{:S(2)}, u32[]{:S(2)}) collective-permute-start(bf16[512,256]{1,0:T(8,128)(2,1)S(1)} %constant_dynamic-update-slice_fusion.refs_2_), channel_id=1, source_target_pairs={{0,32},{1,33},{32,0},{33,1},{64,96},{65,97},{96,64},{97,65},{128,1... | collective-permute-start | bytes 786440 | tf_op jit(solution)/shard_map/ppermute | solution.py:31
  33.1 14.4 %collective-permute-start.7 = (bf16[512,256]{1,0:T(8,128)(2,1)S(1)}, bf16[512,256]{1,0:T(8,128)(2,1)}, u32[]{:S(2)}, u32[]{:S(2)}) collective-permute-start(bf16[512,256]{1,0:T(8,128)(2,1)S(1)} %constant_dynamic-update-slice_fusion.4.refs_3_), channel_id=1, source_target_pairs={{0,192},{1,193},{32,224},{33,225},{64,128},{65,129},{96,160},{97,1... | collective-permute-start | bytes 786440 | tf_op jit(solution)/shard_map/ppermute | solution.py:31
  34.1 13.4 %collective-permute-start.3 = (bf16[512,256]{1,0:T(8,128)(2,1)S(1)}, bf16[512,256]{1,0:T(8,128)(2,1)}, u32[]{:S(2)}, u32[]{:S(2)}) collective-permute-start(bf16[512,256]{1,0:T(8,128)(2,1)S(1)} %constant_dynamic-update-slice_fusion.refs_2_), channel_id=1, source_target_pairs={{0,33},{1,32},{32,1},{33,0},{64,97},{65,96},{96,65},{97,64},{128,1... | collective-permute-start | bytes 786440 | tf_op jit(solution)/shard_map/ppermute | solution.py:31
  52.7 15.6 %collective-permute-start.13 = (f32[256,256]{1,0:T(8,128)S(1)}, f32[256,256]{1,0:T(8,128)S(1)}, u32[]{:S(2)}, u32[]{:S(2)}) collective-permute-start(f32[256,256]{1,0:T(8,128)S(1)} %get-tuple-element.68), channel_id=1, source_target_pairs={{0,1},{1,0},{2,3},{3,2},{4,5},{5,4},{6,7},{7,6},{8,9},{9,8},{10,11... | collective-permute-start | bytes 786440 | tf_op jit(solution)/shard_map/ppermute | solution.py:22
  52.7 19.0 %collective-permute-start.12 = (f32[256,256]{1,0:T(8,128)S(1)}, f32[256,256]{1,0:T(8,128)S(1)}, u32[]{:S(2)}, u32[]{:S(2)}) collective-permute-start(f32[256,256]{1,0:T(8,128)S(1)} %get-tuple-element.65.own_ref), channel_id=1, source_target_pairs={{0,1},{1,0},{2,3},{3,2},{4,5},{5,4},{6,7},{7,6},{8,9},{9,8},{10,11... | collective-permute-start | bytes 786440 | tf_op jit(solution)/shard_map/ppermute | solution.py:22
  72.9 39.7 %all-to-all-start.2 = ((bf16[16,4,16,256]{3,2,1,0:T(8,128)(2,1)}), bf16[16,4,16,256]{3,2,1,0:T(8,128)(2,1)S(1)}, u32[]{:S(2)}, u32[]{:S(2)}) async-start(bf16[16,4,16,256]{3,2,1,0:T(8,128)(2,1)} %copy-done.1), calls=%async_computation.2 | async-start | bytes 1048576 | tf_op jit(solution)/shard_map/all_to_all | solution.py:317
  77.7 11.5 %collective-permute-start.14 = (bf16[512,256]{1,0:T(8,128)(2,1)}, bf16[512,256]{1,0:T(8,128)(2,1)S(1)}, u32[]{:S(2)}, u32[]{:S(2)}) collective-permute-start(bf16[512,256]{1,0:T(8,128)(2,1)} %copy-done.17), channel_id=1, source_target_pairs={{0,32},{1,33},{32,0},{33,1},{64,96},{65,97},{96,64},{97,65},{128,1... | collective-permute-start | bytes 786440 | tf_op jit(solution)/shard_map/ppermute | solution.py:31
  82.3 11.0 %collective-permute-start.16 = (bf16[512,256]{1,0:T(8,128)(2,1)S(1)}, bf16[512,256]{1,0:T(8,128)(2,1)S(1)}, u32[]{:S(2)}, u32[]{:S(2)}) collective-permute-start(bf16[512,256]{1,0:T(8,128)(2,1)S(1)} %get-tuple-element.89), channel_id=1, source_target_pairs={{0,33},{1,32},{32,1},{33,0},{64,97},{65,96},{96,65},{97,64},{128,1... | collective-permute-start | bytes 786440 | tf_op jit(solution)/shard_map/ppermute | solution.py:31
  84.8 8.5 %collective-permute-start.15 = (bf16[512,256]{1,0:T(8,128)(2,1)S(1)}, bf16[512,256]{1,0:T(8,128)(2,1)S(1)}, u32[]{:S(2)}, u32[]{:S(2)}) collective-permute-start(bf16[512,256]{1,0:T(8,128)(2,1)S(1)} %get-tuple-element.86), channel_id=1, source_target_pairs={{0,1},{1,0},{32,33},{33,32},{64,65},{65,64},{96,97},{97,96},{128,1... | collective-permute-start | bytes 786440 | tf_op jit(solution)/shard_map/ppermute | solution.py:31
  85.7 10.7 %collective-permute-start.19 = (bf16[512,256]{1,0:T(8,128)(2,1)S(1)}, bf16[512,256]{1,0:T(8,128)(2,1)S(1)}, u32[]{:S(2)}, u32[]{:S(2)}) collective-permute-start(bf16[512,256]{1,0:T(8,128)(2,1)S(1)} %copy-done.16), channel_id=1, source_target_pairs={{0,128},{1,129},{32,160},{33,161},{64,192},{65,193},{96,224},{97,2... | collective-permute-start | bytes 786440 | tf_op jit(solution)/shard_map/ppermute | solution.py:31
  88.1 12.3 %collective-permute-start.21 = (bf16[512,256]{1,0:T(8,128)(2,1)S(1)}, bf16[512,256]{1,0:T(8,128)(2,1)S(1)}, u32[]{:S(2)}, u32[]{:S(2)}) collective-permute-start(bf16[512,256]{1,0:T(8,128)(2,1)S(1)} %get-tuple-element.97), channel_id=1, source_target_pairs={{0,192},{1,193},{32,224},{33,225},{64,128},{65,129},{96,160},{97,1... | collective-permute-start | bytes 786440 | tf_op jit(solution)/shard_map/ppermute | solution.py:31
  89.2 11.2 %collective-permute-start.20 = (bf16[512,256]{1,0:T(8,128)(2,1)S(1)}, bf16[512,256]{1,0:T(8,128)(2,1)S(1)}, u32[]{:S(2)}, u32[]{:S(2)}) collective-permute-start(bf16[512,256]{1,0:T(8,128)(2,1)S(1)} %get-tuple-element.96), channel_id=1, source_target_pairs={{0,64},{1,65},{32,96},{33,97},{64,0},{65,1},{96,32},{97,33},{128,1... | collective-permute-start | bytes 786440 | tf_op jit(solution)/shard_map/ppermute | solution.py:31
  93.7 9.5 %collective-permute-start.17 = (bf16[256,256]{1,0:T(8,128)(2,1)S(1)}, bf16[256,256]{1,0:T(8,128)(2,1)S(1)}, u32[]{:S(2)}, u32[]{:S(2)}) collective-permute-start(bf16[256,256]{1,0:T(8,128)(2,1)S(1)} %get-tuple-element.91), channel_id=1, source_target_pairs={{0,192},{1,193},{32,224},{33,225},{64,128},{65,129},{96,160},{97,1... | collective-permute-start | bytes 393224 | tf_op jit(solution)/shard_map/ppermute | solution.py:31
  100.7 6.6 %collective-permute-start.22 = (bf16[256,256]{1,0:T(8,128)(2,1)S(1)}, bf16[256,256]{1,0:T(8,128)(2,1)S(1)}, u32[]{:S(2)}, u32[]{:S(2)}) collective-permute-start(bf16[256,256]{1,0:T(8,128)(2,1)S(1)} %get-tuple-element.99), channel_id=1, source_target_pairs={{0,33},{1,32},{32,1},{33,0},{64,97},{65,96},{96,65},{97,64},{128,1... | collective-permute-start | bytes 393224 | tf_op jit(solution)/shard_map/ppermute | solution.py:31
  (20 other events, 115.9 us)

commit v4 on v3

--- a/solution.py
+++ b/solution.py
@@ -51,15 +51,28 @@
     return views / flat
 
 
-def code_columns(code_ref, kind, distance):
+def fetch_codes(code_ref, buffer, semaphores, distance):
     place = lax.axis_index(owners)
     half = code_ref.shape[1] // (2 * side * side)
-    parts = []
-    for j in near:
-        owner = place ^ (mask_of(kind, j) + mask_of(1 - kind, distance))
-        first = pl.multiple_of((owner * 2 + kind) * half, half)
-        parts.append(code_ref[:, pl.ds(first, half)])
-    return jnp.concatenate(parts, axis=1)
+    copies = [[], []]
+    for kind in kinds:
+        for index, j in enumerate(near):
+            owner = place ^ (mask_of(kind, j) + mask_of(1 - kind, distance))
+            first = pl.multiple_of((owner * 2 + kind) * half, half)
+            copy = pltpu.make_async_copy(
+                code_ref.at[:, pl.ds(first, half)],
+                buffer.at[kind, :, pl.ds(index * half, half)],
+                semaphores.at[kind * side + index],
+            )
+            copy.start()
+            copies[kind].append(copy)
+    return copies
+
+
+def fetched_code(copies, buffer, kind):
+    for copy in copies[kind]:
+        copy.wait()
+    return buffer[kind]
 
 
 def split_kernel(
@@ -93,23 +106,19 @@
     z_t_ref, code_ref, *raw_refs = refs[:4]
     own_before, acc_before = refs[4 : 4 + n_before], refs[4 + n_before : 4 + 2 * n_before]
     exp_a_ref, exp_b_ref, soft_ref, own_ref, total_ref = refs[4 + 2 * n_before : 9 + 2 * n_before]
-    raw_bufs, copies = raw_refs, ()
-    if distance:
-        raw_bufs, semaphores = refs[-4:-2], refs[-2:]
-        copies = fetch(raw_refs, raw_bufs, semaphores)
+    code_buf, semaphores = refs[-2:]
+    copies = fetch_codes(code_ref, code_buf, semaphores, distance)
     rows = z_t_ref.shape[1]
     soft = own = acc = None
     add = lambda a, b: b if a is None else a + b
     for kind, exp_ref in zip(kinds, (exp_a_ref, exp_b_ref)):
-        if copies:
-            copies[kind].wait()
-        c = normalize_rows(raw_bufs[kind][...])[0].astype(bf16)
+        c = normalize_rows(raw_refs[kind][...])[0].astype(bf16)
         exponent = jnp.exp(dot(c, z_t_ref[...], 1, 0) * sharpness)
         acc = add(acc, jnp.sum(exponent.reshape(-1, 8, rows), axis=0))
         exponent = exponent.astype(bf16)
         exp_ref[...] = exponent
         soft = add(soft, dot(c, exponent, 0, 0))
-        own = add(own, dot(code_columns(code_ref, kind, distance), c, 1, 0))
+        own = add(own, dot(fetched_code(copies, code_buf, kind), c, 1, 0))
     soft_ref[...] = soft
     for before in own_before:
         own = own + before[...]
@@ -126,6 +135,9 @@
 
 
 def prototypes_kernel(*refs, distance, crops, own_images, first):
+    *refs, code_buf, semaphores = refs
+    code_ref, *refs = refs
+    copies = fetch_codes(code_ref, code_buf, semaphores, distance)
     if first:
         totals_ref, z_t_ref, local_ref, incoming_ref = refs[:4]
         weights = row_weights(totals_ref, crops, own_images)
@@ -137,10 +149,10 @@
     else:
         zw, target = refs[0][...], refs[1][...]
         refs = refs[2:]
-    code_ref, exp_a_ref, exp_b_ref, *out_refs = refs
+    exp_a_ref, exp_b_ref, *out_refs = refs
     for kind, exp_ref, out_ref in zip(kinds, (exp_a_ref, exp_b_ref), out_refs):
-        code = code_columns(code_ref, kind, distance)
-        grads = dot(exp_ref[...], zw, 1, 1) - dot(code, target, 0, 0)
+        grads = dot(exp_ref[...], zw, 1, 1)
+        grads = grads - dot(fetched_code(copies, code_buf, kind), target, 0, 0)
         out_ref[...] = grads.astype(out_ref.dtype)
 
 
@@ -167,14 +179,10 @@
 
 
 def far_sum_kernel(held_ref, *refs):
-    n = len(arrivals)
-    sources, (keep_ref, send_ref), refs = refs[:n], refs[n : n + 2], refs[n + 2 :]
-    buffers, semaphores = refs[:n], refs[n:]
-    copies = fetch(sources, buffers, semaphores)
+    parts, (keep_ref, send_ref) = refs[:-2], refs[-2:]
     total = held_ref[...]
-    for copy, buffer in zip(copies, buffers):
-        copy.wait()
-        total = total + buffer[...].astype(f32)
+    for part in parts:
+        total = total + part[...].astype(f32)
     half = total.shape[0] // 2
     keep_ref[...] = total[:half]
     send_ref[...] = total[half:].astype(bf16)
@@ -201,13 +209,17 @@
     return jax.ShapeDtypeStruct(dims, dtype)
 
 
-def call(kernel, out_shape, *operands, mib=12, fetched=(), scratch=()):
+def call(kernel, out_shape, *operands, mib=12, fetched=(), held=(), scratch=()):
+    operands = [
+        pltpu.with_memory_space_constraint(x, pltpu.HBM) if i in held else x
+        for i, x in enumerate(operands)
+    ]
     kept = pl.BlockSpec(memory_space=pltpu.VMEM)
     there = pl.BlockSpec(memory_space=pl.ANY)
     return pl.pallas_call(
         kernel,
         out_shape=out_shape,
-        in_specs=[there if i in fetched else kept for i in range(len(operands))],
+        in_specs=[there if i in (*fetched, *held) else kept for i in range(len(operands))],
         out_specs=jax.tree.map(lambda _: kept, out_shape),
         scratch_shapes=[
             *(pltpu.VMEM(operands[i].shape, operands[i].dtype) for i in fetched),
@@ -242,15 +254,16 @@
             shape(crops, own_images, features, dtype=bf16),
             shape(n_proto, own_rows, features, dtype=bf16),
         ],
-        *(pltpu.with_memory_space_constraint(x, pltpu.HBM) for x in (prototypes[0], embeddings[:, 0])),
-        fetched=(0, 1),
-    )
-    blocks = [[halves[kind]] for kind in kinds]
-    for j in near[1:]:
+        prototypes[0], embeddings[:, 0],
+        fetched=(0, 1), held=(0, 1),
+    )
+    for step, distance in enumerate((1, 3)):
+        moved = []
         for kind in kinds:
-            blocks[kind].append(exchange(halves[kind], kind, j))
-    halves = [jnp.concatenate(each) for each in blocks]
-    raw_emb = lax.all_to_all(spread_emb, "proto", 0, 0)
+            moved.append(exchange(halves[kind], kind, distance))
+        halves = [jnp.concatenate(pair) for pair in zip(halves, moved)]
+        if step == 0:
+            raw_emb = lax.all_to_all(spread_emb, "proto", 0, 0)
     gathered = {0: halves}
     for d in arrivals:
         gathered[d] = []
@@ -263,6 +276,10 @@
         raw_emb.reshape(n_proto, crops, own_images, features),
     )
 
+    code_scratch = [
+        pltpu.VMEM((2, images, side * half), bf16),
+        pltpu.SemaphoreType.DMA((2 * side,)),
+    ]
     exponents = {}
     soft, own_sums, sums = [], [], []
     for d in (0, *arrivals):
@@ -273,7 +290,8 @@
             [shape(side * half, rows, dtype=bf16)] * 2
             + [shape(features, rows), shape(images, features), shape(*total_dims)],
             z_t, code, *gathered[d], *before,
-            fetched=(2, 3) if d else (),
+            held=(1,),
+            scratch=code_scratch,
         )
         soft.append(soft_part)
         own_sums.append(own_term)
@@ -293,8 +311,10 @@
             ),
             [shape(side * half, features, dtype=bf16 if d else f32)] * 2
             + [shape(features, rows, dtype=bf16), shape(images, features, dtype=bf16)] * first,
-            *((totals, z_t, local_sum, incoming) if first else (zw, target)),
-            code, *exponents[d],
+            code, *((totals, z_t, local_sum, incoming) if first else (zw, target)),
+            *exponents[d],
+            held=(0,),
+            scratch=code_scratch,
         )
         parts = outs[:2]
         if first:
@@ -322,7 +342,6 @@
             far_sum_kernel,
             [shape(2 * half, features), shape(2 * half, features, dtype=bf16)],
             *arrived[kind],
-            fetched=tuple(range(1, len(arrived[kind]))),
         )
         held.append((keep, exchange(send, kind, 3)))
     operands = []

time: 114 us -> 122 us (1.070)
  Pallas kernels: 20.3 us -> 29.7 us
  local copies, waits for them, and re-layouts: 11.4 us -> 8.2 us
  waiting for transfers between devices: 21.6 us -> 23.8 us
    pallas_call x17, Pallas kernels: 20.3 us -> 29.7 us  [call(): pl.pallas_call(kernel, out_shape=out_shape, in_specs=[there if i in (*fet...]
    unnamed x42 -> x31, local copies, waits for them, and re-layouts: 10.5 us -> 8.19 us
    ppermute x22 -> x20, waiting for transfers between devices: 21.6 us -> 23.8 us  [exchange(): lax.ppermute(value, owners, [(owner, owner ^ mask) for owner in range(sid...]
    ppermute x22 -> x20, starting transfers between devices: 30.5 us -> 29.5 us  [exchange(): lax.ppermute(value, owners, [(owner, owner ^ mask) for owner in range(sid...]
  transfers between devices with their start and end apart: 26 -> 24, of which waited for: 7 -> 10; matrix products, arithmetic and copies ran while one was open for 2% -> 0% of each run, Pallas kernels for 12% -> 18%
where the time goes in v4:
time: 122 us; the launch traced here: 121 us
  starting transfers between devices  44.8 us (37%)
  Pallas kernels  29.7 us (24%)
  waiting for transfers between devices  23.8 us (20%)
  blocking collectives  13.5 us (11%)
  local copies, waits for them, and re-layouts  8.2 us (7%)
    pallas_call x17, Pallas kernels, call(): pl.pallas_call(kernel, out_shape=out_shape, in_specs=[there if i in (*fet...  29.7 us
    ppermute x20, starting transfers between devices, exchange(): lax.ppermute(value, owners, [(owner, owner ^ mask) for owner in range(sid...  29.5 us
    ppermute x20, waiting for transfers between devices, exchange(): lax.ppermute(value, owners, [(owner, owner ^ mask) for owner in range(sid...  23.8 us
    all_to_all x1, blocking collectives, on_device(): totals = lax.all_to_all(totals, 'proto', 0, 0)  13.5 us
    all_to_all x1, starting transfers between devices, on_device(): raw_emb = lax.all_to_all(spread_emb, 'proto', 0, 0)  8.59 us
    unnamed x31, local copies, waits for them, and re-layouts  8.19 us
    all_to_all x1, starting transfers between devices, on_device(): row_parts = lax.all_to_all(row_parts, 'proto', 0, 0)  4.76 us
  transfers between devices with their start and end apart: 24, of which 10 were waited for; matrix products, arithmetic and copies ran while one was open for 0% of the time, Pallas kernels for 18%

profile of v4, /device:TPU:32, one launch (start us, length us, event | category | flops | bytes accessed | tf_op | source)
XLA Modules:
  0.0 121.0 jit_solution(12651049979693124558)
XLA Ops:
  4.5 8.6 %all-to-all-start = ((bf16[16,64,256]{2,1,0:T(8,128)(2,1)}), bf16[16,64,256]{2,1,0:T(8,128)(2,1)S(1)}, u32[]{:S(2)}, u32[]{:S(2)}) async-start(bf16[16,64,256]{2,1,0:T(8,128)(2,1)} %get-tuple-element.52), calls=%async_computation | async-start | bytes 1048576 | tf_op jit(solution)/shard_map/all_to_all | solution.py:266
  14.7 2.2 %collective-permute-start.4 = (bf16[256,256]{1,0:T(8,128)(2,1)S(1)}, bf16[256,256]{1,0:T(8,128)(2,1)S(1)}, u32[]{:S(2)}, u32[]{:S(2)}) collective-permute-start(bf16[256,256]{1,0:T(8,128)(2,1)S(1)} %pad_maximum_fusion.1), channel_id=1, source_target_pairs={{0,33},{1,32},{32,1},{33,0},{64,97},{65,96},{96,65},{97,64},{128,1... | collective-permute-start | bytes 393224 | tf_op jit(solution)/shard_map/ppermute | solution.py:31
  16.9 4.3 %collective-permute-done.4 = bf16[256,256]{1,0:T(8,128)(2,1)S(1)} collective-permute-done((bf16[256,256]{1,0:T(8,128)(2,1)S(1)}, bf16[256,256]{1,0:T(8,128)(2,1)S(1)}, u32[]{:S(2)}, u32[]{:S(2)}) %collective-permute-start.4) | collective-permute-done | bytes 131104 | tf_op jit(solution)/shard_map/ppermute | solution.py:31
  21.8 3.1 %collective-permute-start.1 = (bf16[256,256]{1,0:T(8,128)(2,1)S(1)}, bf16[256,256]{1,0:T(8,128)(2,1)S(1)}, u32[]{:S(2)}, u32[]{:S(2)}) collective-permute-start(bf16[256,256]{1,0:T(8,128)(2,1)S(1)} %pad_maximum_fusion), channel_id=1, source_target_pairs={{0,192},{1,193},{32,224},{33,225},{64,128},{65,129},{96,160},{97,1... | collective-permute-start | bytes 393224 | tf_op jit(solution)/shard_map/ppermute | solution.py:31
  24.9 3.2 %collective-permute-done.1 = bf16[256,256]{1,0:T(8,128)(2,1)S(1)} collective-permute-done((bf16[256,256]{1,0:T(8,128)(2,1)S(1)}, bf16[256,256]{1,0:T(8,128)(2,1)S(1)}, u32[]{:S(2)}, u32[]{:S(2)}) %collective-permute-start.1) | collective-permute-done | bytes 131104 | tf_op jit(solution)/shard_map/ppermute | solution.py:31
  28.2 2.1 %collective-permute-start.7 = (bf16[512,256]{1,0:T(8,128)(2,1)S(1)}, bf16[512,256]{1,0:T(8,128)(2,1)}, u32[]{:S(2)}, u32[]{:S(2)}) collective-permute-start(bf16[512,256]{1,0:T(8,128)(2,1)S(1)} %constant_dynamic-update-slice_fusion.3.refs_3_), channel_id=1, source_target_pairs={{0,128},{1,129},{32,160},{33,161},{64,192},{65,193},{96,224},{97,2... | collective-permute-start | bytes 786440 | tf_op jit(solution)/shard_map/ppermute | solution.py:31
  30.3 3.5 %collective-permute-start.6 = (bf16[512,256]{1,0:T(8,128)(2,1)S(1)}, bf16[512,256]{1,0:T(8,128)(2,1)}, u32[]{:S(2)}, u32[]{:S(2)}) collective-permute-start(bf16[512,256]{1,0:T(8,128)(2,1)S(1)} %constant_dynamic-update-slice_fusion.refs_2_), channel_id=1, source_target_pairs={{0,32},{1,33},{32,0},{33,1},{64,96},{65,97},{96,64},{97,65},{128,1... | collective-permute-start | bytes 786440 | tf_op jit(solution)/shard_map/ppermute | solution.py:31
  36.6 2.7 %shard_map.52 = (bf16[512,1024]{1,0:T(8,128)(2,1)S(1)}, bf16[512,1024]{1,0:T(8,128)(2,1)S(1)}, f32[256,1024]{1,0:T(8,128)S(1)}, f32[256,256]{1,0:T(8,128)S(1)}, f32[8,1024]{1,0:T(8,128)S(1)}) custom-call(bf16[256,1024]{1,0:T(8,128)(2,1)S(1)} %get-tuple-element.53.refs_0_.refs_2_, bf16[256,4096]{1,0:T(8,128)(2,1)} %bitcast.11, ...), custom_call_target="tpu_custom_call" | custom-call | tf_op jit(solution)/shard_map/pallas_call | solution.py:219
  41.0 2.7 %shard_map.54 = (bf16[512,1024]{1,0:T(8,128)(2,1)S(1)}, bf16[512,1024]{1,0:T(8,128)(2,1)S(1)}, f32[256,1024]{1,0:T(8,128)S(1)}, f32[256,256]{1,0:T(8,128)S(1)}, f32[8,1024]{1,0:T(8,128)S(1)}) custom-call(bf16[256,1024]{1,0:T(8,128)(2,1)S(1)} %get-tuple-element.53.refs_0_.refs_2_, bf16[256,4096]{1,0:T(8,128)(2,1)} %bitcast.12, ...), custom_call_target="tpu_custom_call" | custom-call | tf_op jit(solution)/shard_map/pallas_call | solution.py:219
  43.7 3.7 %shard_map.53 = (bf16[512,1024]{1,0:T(8,128)(2,1)S(1)}, bf16[512,1024]{1,0:T(8,128)(2,1)S(1)}, f32[256,1024]{1,0:T(8,128)S(1)}, f32[256,256]{1,0:T(8,128)S(1)}, f32[8,1024]{1,0:T(8,128)S(1)}) custom-call(bf16[256,1024]{1,0:T(8,128)(2,1)S(1)} %get-tuple-element.53.refs_0_.refs_2_, bf16[256,4096]{1,0:T(8,128)(2,1)} %bitcast.13, ...), custom_call_target="tpu_custom_call" | custom-call | tf_op jit(solution)/shard_map/pallas_call | solution.py:219
  47.5 3.7 %shard_map.55 = (bf16[512,1024]{1,0:T(8,128)(2,1)S(1)}, bf16[512,1024]{1,0:T(8,128)(2,1)S(1)}, f32[256,1024]{1,0:T(8,128)S(1)}, f32[256,256]{1,0:T(8,128)S(1)}, f32[16,8,128]{2,1,0:T(8,128)S(1)}) custom-call(bf16[256,1024]{1,0:T(8,128)(2,1)S(1)} %get-tuple-element.53.refs_0_.refs_2_, bf16[256,4096]{1,0:T(8,128)(2,1)} %bitcast.14, ...), custom_call_target="tpu_custom_call" | custom-call | tf_op jit(solution)/shard_map/pallas_call | solution.py:219
  55.2 13.5 %all_to_all.15.refs_1_.totals_ref = f32[16,8,128]{2,1,0:T(8,128)S(1)} all-to-all(f32[16,8,128]{2,1,0:T(8,128)S(1)} %get-tuple-element.64), channel_id=1, replica_groups=mesh['dp'=8,'proto'=16,'crop'=2] {'proto'}, dimensions={0} | all-to-all | bytes 131072 | tf_op jit(solution)/shard_map/all_to_all | solution.py:302
  68.7 2.8 %shard_map.56 = (bf16[512,256]{1,0:T(8,128)(2,1)S(1)}, bf16[512,256]{1,0:T(8,128)(2,1)S(1)}, bf16[256,1024]{1,0:T(8,128)(2,1)S(1)}, bf16[256,256]{1,0:T(8,128)(2,1)S(1)}) custom-call(bf16[256,4096]{1,0:T(8,128)(2,1)} %bitcast.15, f32[16,8,128]{2,1,0:T(8,128)S(1)} %all_to_all.15.refs_1_.totals_ref, bf16[256,1024]{1,0:T(8,128)(2,1)S(1)} %get-tuple-element.53.refs_0_.refs_2_, ...), custom_call_target="tpu_custom_call" | custom-call | tf_op jit(solution)/shard_map/pallas_call | solution.py:219
  72.3 2.8 %shard_map.57 = (f32[512,256]{1,0:T(8,128)S(1)}, f32[512,256]{1,0:T(8,128)S(1)}) custom-call(bf16[256,4096]{1,0:T(8,128)(2,1)} %bitcast.16, bf16[256,1024]{1,0:T(8,128)(2,1)S(1)} %get-tuple-element.71.refs_1_, bf16[256,256]{1,0:T(8,128)(2,1)S(1)} %get-tuple-element.72.refs_2_, bf16[512,1024]{1,0:T(8,128)(2,1)S(1)} %get-tuple-element.73.refs_3_, ...), custom_call_target="tpu_custom_call" | custom-call | tf_op jit(solution)/shard_map/pallas_call | solution.py:219
  77.1 4.8 %all-to-all-start.2 = ((bf16[16,4,16,256]{3,2,1,0:T(8,128)(2,1)}), bf16[16,4,16,256]{3,2,1,0:T(8,128)(2,1)S(1)}, u32[]{:S(2)}, u32[]{:S(2)}) async-start(bf16[16,4,16,256]{3,2,1,0:T(8,128)(2,1)} %shard_map.58), calls=%async_computation.2 | async-start | bytes 1048576 | tf_op jit(solution)/shard_map/all_to_all | solution.py:337
  85.8 2.8 %shard_map.61 = (bf16[512,256]{1,0:T(8,128)(2,1)S(1)}, bf16[512,256]{1,0:T(8,128)(2,1)S(1)}) custom-call(bf16[256,4096]{1,0:T(8,128)(2,1)} %bitcast.17, bf16[256,1024]{1,0:T(8,128)(2,1)S(1)} %get-tuple-element.71.refs_1_, bf16[256,256]{1,0:T(8,128)(2,1)S(1)} %get-tuple-element.72.refs_2_, bf16[512,1024]{1,0:T(8,128)(2,1)S(1)} %copy-done.1, ...), custom_call_target="tpu_custom_call" | custom-call | tf_op jit(solution)/shard_map/pallas_call | solution.py:219
  89.8 2.8 %shard_map.60 = (bf16[512,256]{1,0:T(8,128)(2,1)S(1)}, bf16[512,256]{1,0:T(8,128)(2,1)S(1)}) custom-call(bf16[256,4096]{1,0:T(8,128)(2,1)} %bitcast.18, bf16[256,1024]{1,0:T(8,128)(2,1)S(1)} %get-tuple-element.71.refs_1_, bf16[256,256]{1,0:T(8,128)(2,1)S(1)} %get-tuple-element.72.refs_2_, bf16[512,1024]{1,0:T(8,128)(2,1)S(1)} %get-tuple-element.84.refs_3_, ...), custom_call_target="tpu_custom_call" | custom-call | tf_op jit(solution)/shard_map/pallas_call | solution.py:219
  93.5 2.9 %collective-permute-start.17 = (bf16[512,256]{1,0:T(8,128)(2,1)S(1)}, bf16[512,256]{1,0:T(8,128)(2,1)S(1)}, u32[]{:S(2)}, u32[]{:S(2)}) collective-permute-start(bf16[512,256]{1,0:T(8,128)(2,1)S(1)} %get-tuple-element.95), channel_id=1, source_target_pairs={{0,128},{1,129},{32,160},{33,161},{64,192},{65,193},{96,224},{97,2... | collective-permute-start | bytes 786440 | tf_op jit(solution)/shard_map/ppermute | solution.py:31
  98.0 2.5 %collective-permute-done.13.refs_1_ = bf16[512,256]{1,0:T(8,128)(2,1)S(1)} collective-permute-done((bf16[512,256]{1,0:T(8,128)(2,1)S(1)}, bf16[512,256]{1,0:T(8,128)(2,1)S(1)}, u32[]{:S(2)}, u32[]{:S(2)}) %collective-permute-start.13) | collective-permute-done | bytes 262176 | tf_op jit(solution)/shard_map/ppermute | solution.py:31
  100.6 2.3 %collective-permute-start.15 = (bf16[256,256]{1,0:T(8,128)(2,1)S(1)}, bf16[256,256]{1,0:T(8,128)(2,1)S(1)}, u32[]{:S(2)}, u32[]{:S(2)}) collective-permute-start(bf16[256,256]{1,0:T(8,128)(2,1)S(1)} %get-tuple-element.91), channel_id=1, source_target_pairs={{0,192},{1,193},{32,224},{33,225},{64,128},{65,129},{96,160},{97,1... | collective-permute-start | bytes 393224 | tf_op jit(solution)/shard_map/ppermute | solution.py:31
  104.2 4.1 %collective-permute-done.19.refs_2_ = bf16[512,256]{1,0:T(8,128)(2,1)S(1)} collective-permute-done((bf16[512,256]{1,0:T(8,128)(2,1)S(1)}, bf16[512,256]{1,0:T(8,128)(2,1)S(1)}, u32[]{:S(2)}, u32[]{:S(2)}) %collective-permute-start.19) | collective-permute-done | bytes 262176 | tf_op jit(solution)/shard_map/ppermute | solution.py:31
  108.4 2.2 %collective-permute-start.20 = (bf16[256,256]{1,0:T(8,128)(2,1)S(1)}, bf16[256,256]{1,0:T(8,128)(2,1)S(1)}, u32[]{:S(2)}, u32[]{:S(2)}) collective-permute-start(bf16[256,256]{1,0:T(8,128)(2,1)S(1)} %get-tuple-element.99), channel_id=1, source_target_pairs={{0,33},{1,32},{32,1},{33,0},{64,97},{65,96},{96,65},{97,64},{128,1... | collective-permute-start | bytes 393224 | tf_op jit(solution)/shard_map/ppermute | solution.py:31
  112.0 2.9 %collective-permute-done.20.part_ref = bf16[256,256]{1,0:T(8,128)(2,1)S(1)} collective-permute-done((bf16[256,256]{1,0:T(8,128)(2,1)S(1)}, bf16[256,256]{1,0:T(8,128)(2,1)S(1)}, u32[]{:S(2)}, u32[]{:S(2)}) %collective-permute-start.20) | collective-permute-done | bytes 131104 | tf_op jit(solution)/shard_map/ppermute | solution.py:31
  115.3 3.9 %collective-permute-done.21.part_b_ref = bf16[128,256]{1,0:T(8,128)(2,1)S(1)} collective-permute-done((bf16[128,256]{1,0:T(8,128)(2,1)S(1)}, bf16[128,256]{1,0:T(8,128)(2,1)S(1)}, u32[]{:S(2)}, u32[]{:S(2)}) %collective-permute-start.21) | collective-permute-done | bytes 65568 | tf_op jit(solution)/shard_map/ppermute | solution.py:31
  (77 shorter events, 30.1 us)
Async XLA Ops:
  3.1 11.7 %collective-permute-start.3 = (bf16[128,256]{1,0:T(8,128)(2,1)S(1)}, bf16[128,256]{1,0:T(8,128)(2,1)S(1)}, u32[]{:S(2)}, u32[]{:S(2)}) collective-permute-start(bf16[128,256]{1,0:T(8,128)(2,1)S(1)} %get-tuple-element.55), channel_id=1, source_target_pairs={{0,1},{1,0},{32,33},{33,32},{64,65},{65,64},{96,97},{97,96},{128,1... | collective-permute-start | bytes 196616 | tf_op jit(solution)/shard_map/ppermute | solution.py:31
  4.5 31.4 %all-to-all-start = ((bf16[16,64,256]{2,1,0:T(8,128)(2,1)}), bf16[16,64,256]{2,1,0:T(8,128)(2,1)S(1)}, u32[]{:S(2)}, u32[]{:S(2)}) async-start(bf16[16,64,256]{2,1,0:T(8,128)(2,1)} %get-tuple-element.52), calls=%async_computation | async-start | bytes 1048576 | tf_op jit(solution)/shard_map/all_to_all | solution.py:266
  13.1 8.7 %collective-permute-start = (bf16[128,256]{1,0:T(8,128)(2,1)S(1)}, bf16[128,256]{1,0:T(8,128)(2,1)S(1)}, u32[]{:S(2)}, u32[]{:S(2)}) collective-permute-start(bf16[128,256]{1,0:T(8,128)(2,1)S(1)} %get-tuple-element.54), channel_id=1, source_target_pairs={{0,64},{1,65},{32,96},{33,97},{64,0},{65,1},{96,32},{97,33},{128,1... | collective-permute-start | bytes 196616 | tf_op jit(solution)/shard_map/ppermute | solution.py:31
  14.7 6.5 %collective-permute-start.4 = (bf16[256,256]{1,0:T(8,128)(2,1)S(1)}, bf16[256,256]{1,0:T(8,128)(2,1)S(1)}, u32[]{:S(2)}, u32[]{:S(2)}) collective-permute-start(bf16[256,256]{1,0:T(8,128)(2,1)S(1)} %pad_maximum_fusion.1), channel_id=1, source_target_pairs={{0,33},{1,32},{32,1},{33,0},{64,97},{65,96},{96,65},{97,64},{128,1... | collective-permute-start | bytes 393224 | tf_op jit(solution)/shard_map/ppermute | solution.py:31
  21.3 13.5 %collective-permute-start.9 = (bf16[512,256]{1,0:T(8,128)(2,1)S(1)}, bf16[512,256]{1,0:T(8,128)(2,1)S(1)}, u32[]{:S(2)}, u32[]{:S(2)}) collective-permute-start(bf16[512,256]{1,0:T(8,128)(2,1)S(1)} %constant_dynamic-update-slice_fusion.3.refs_3_), channel_id=1, source_target_pairs={{0,64},{1,65},{32,96},{33,97},{64,0},{65,1},{96,32},{97,33},{128,1... | collective-permute-start | bytes 786440 | tf_op jit(solution)/shard_map/ppermute | solution.py:31
  21.8 6.3 %collective-permute-start.1 = (bf16[256,256]{1,0:T(8,128)(2,1)S(1)}, bf16[256,256]{1,0:T(8,128)(2,1)S(1)}, u32[]{:S(2)}, u32[]{:S(2)}) collective-permute-start(bf16[256,256]{1,0:T(8,128)(2,1)S(1)} %pad_maximum_fusion), channel_id=1, source_target_pairs={{0,192},{1,193},{32,224},{33,225},{64,128},{65,129},{96,160},{97,1... | collective-permute-start | bytes 393224 | tf_op jit(solution)/shard_map/ppermute | solution.py:31
  28.1 11.2 %collective-permute-start.8 = (bf16[512,256]{1,0:T(8,128)(2,1)S(1)}, bf16[512,256]{1,0:T(8,128)(2,1)S(1)}, u32[]{:S(2)}, u32[]{:S(2)}) collective-permute-start(bf16[512,256]{1,0:T(8,128)(2,1)S(1)} %constant_dynamic-update-slice_fusion.refs_2_), channel_id=1, source_target_pairs={{0,1},{1,0},{32,33},{33,32},{64,65},{65,64},{96,97},{97,96},{128,1... | collective-permute-start | bytes 786440 | tf_op jit(solution)/shard_map/ppermute | solution.py:31
  28.2 15.5 %collective-permute-start.7 = (bf16[512,256]{1,0:T(8,128)(2,1)S(1)}, bf16[512,256]{1,0:T(8,128)(2,1)}, u32[]{:S(2)}, u32[]{:S(2)}) collective-permute-start(bf16[512,256]{1,0:T(8,128)(2,1)S(1)} %constant_dynamic-update-slice_fusion.3.refs_3_), channel_id=1, source_target_pairs={{0,128},{1,129},{32,160},{33,161},{64,192},{65,193},{96,224},{97,2... | collective-permute-start | bytes 786440 | tf_op jit(solution)/shard_map/ppermute | solution.py:31
  30.3 13.4 %collective-permute-start.6 = (bf16[512,256]{1,0:T(8,128)(2,1)S(1)}, bf16[512,256]{1,0:T(8,128)(2,1)}, u32[]{:S(2)}, u32[]{:S(2)}) collective-permute-start(bf16[512,256]{1,0:T(8,128)(2,1)S(1)} %constant_dynamic-update-slice_fusion.refs_2_), channel_id=1, source_target_pairs={{0,32},{1,33},{32,0},{33,1},{64,96},{65,97},{96,64},{97,65},{128,1... | collective-permute-start | bytes 786440 | tf_op jit(solution)/shard_map/ppermute | solution.py:31
  33.7 13.7 %collective-permute-start.5 = (bf16[512,256]{1,0:T(8,128)(2,1)S(1)}, bf16[512,256]{1,0:T(8,128)(2,1)}, u32[]{:S(2)}, u32[]{:S(2)}) collective-permute-start(bf16[512,256]{1,0:T(8,128)(2,1)S(1)} %constant_dynamic-update-slice_fusion.3.refs_3_), channel_id=1, source_target_pairs={{0,192},{1,193},{32,224},{33,225},{64,128},{65,129},{96,160},{97,1... | collective-permute-start | bytes 786440 | tf_op jit(solution)/shard_map/ppermute | solution.py:31
  34.8 12.7 %collective-permute-start.2 = (bf16[512,256]{1,0:T(8,128)(2,1)S(1)}, bf16[512,256]{1,0:T(8,128)(2,1)}, u32[]{:S(2)}, u32[]{:S(2)}) collective-permute-start(bf16[512,256]{1,0:T(8,128)(2,1)S(1)} %constant_dynamic-update-slice_fusion.refs_2_), channel_id=1, source_target_pairs={{0,33},{1,32},{32,1},{33,0},{64,97},{65,96},{96,65},{97,64},{128,1... | collective-permute-start | bytes 786440 | tf_op jit(solution)/shard_map/ppermute | solution.py:31
  53.2 15.6 %collective-permute-start.11 = (f32[256,256]{1,0:T(8,128)S(1)}, f32[256,256]{1,0:T(8,128)S(1)}, u32[]{:S(2)}, u32[]{:S(2)}) collective-permute-start(f32[256,256]{1,0:T(8,128)S(1)} %get-tuple-element.68), channel_id=1, source_target_pairs={{0,1},{1,0},{2,3},{3,2},{4,5},{5,4},{6,7},{7,6},{8,9},{9,8},{10,11... | collective-permute-start | bytes 786440 | tf_op jit(solution)/shard_map/ppermute | solution.py:22
  53.2 22.7 %collective-permute-start.10 = (f32[256,256]{1,0:T(8,128)S(1)}, f32[256,256]{1,0:T(8,128)S(1)}, u32[]{:S(2)}, u32[]{:S(2)}) collective-permute-start(f32[256,256]{1,0:T(8,128)S(1)} %get-tuple-element.65.own_ref), channel_id=1, source_target_pairs={{0,1},{1,0},{2,3},{3,2},{4,5},{5,4},{6,7},{7,6},{8,9},{9,8},{10,11... | collective-permute-start | bytes 786440 | tf_op jit(solution)/shard_map/ppermute | solution.py:22
  77.1 43.1 %all-to-all-start.2 = ((bf16[16,4,16,256]{3,2,1,0:T(8,128)(2,1)}), bf16[16,4,16,256]{3,2,1,0:T(8,128)(2,1)S(1)}, u32[]{:S(2)}, u32[]{:S(2)}) async-start(bf16[16,4,16,256]{3,2,1,0:T(8,128)(2,1)} %shard_map.58), calls=%async_computation.2 | async-start | bytes 1048576 | tf_op jit(solution)/shard_map/all_to_all | solution.py:337
  81.8 15.2 %collective-permute-start.12 = (bf16[512,256]{1,0:T(8,128)(2,1)}, bf16[512,256]{1,0:T(8,128)(2,1)S(1)}, u32[]{:S(2)}, u32[]{:S(2)}) collective-permute-start(bf16[512,256]{1,0:T(8,128)(2,1)} %copy-done.13), channel_id=1, source_target_pairs={{0,32},{1,33},{32,0},{33,1},{64,96},{65,97},{96,64},{97,65},{128,1... | collective-permute-start | bytes 786440 | tf_op jit(solution)/shard_map/ppermute | solution.py:31
  88.6 9.3 %collective-permute-start.14 = (bf16[512,256]{1,0:T(8,128)(2,1)S(1)}, bf16[512,256]{1,0:T(8,128)(2,1)S(1)}, u32[]{:S(2)}, u32[]{:S(2)}) collective-permute-start(bf16[512,256]{1,0:T(8,128)(2,1)S(1)} %get-tuple-element.89), channel_id=1, source_target_pairs={{0,33},{1,32},{32,1},{33,0},{64,97},{65,96},{96,65},{97,64},{128,1... | collective-permute-start | bytes 786440 | tf_op jit(solution)/shard_map/ppermute | solution.py:31
  92.6 7.9 %collective-permute-start.13 = (bf16[512,256]{1,0:T(8,128)(2,1)S(1)}, bf16[512,256]{1,0:T(8,128)(2,1)S(1)}, u32[]{:S(2)}, u32[]{:S(2)}) collective-permute-start(bf16[512,256]{1,0:T(8,128)(2,1)S(1)} %get-tuple-element.86), channel_id=1, source_target_pairs={{0,1},{1,0},{32,33},{33,32},{64,65},{65,64},{96,97},{97,96},{128,1... | collective-permute-start | bytes 786440 | tf_op jit(solution)/shard_map/ppermute | solution.py:31
  93.5 10.7 %collective-permute-start.17 = (bf16[512,256]{1,0:T(8,128)(2,1)S(1)}, bf16[512,256]{1,0:T(8,128)(2,1)S(1)}, u32[]{:S(2)}, u32[]{:S(2)}) collective-permute-start(bf16[512,256]{1,0:T(8,128)(2,1)S(1)} %get-tuple-element.95), channel_id=1, source_target_pairs={{0,128},{1,129},{32,160},{33,161},{64,192},{65,193},{96,224},{97,2... | collective-permute-start | bytes 786440 | tf_op jit(solution)/shard_map/ppermute | solution.py:31
  96.4 11.9 %collective-permute-start.19 = (bf16[512,256]{1,0:T(8,128)(2,1)S(1)}, bf16[512,256]{1,0:T(8,128)(2,1)S(1)}, u32[]{:S(2)}, u32[]{:S(2)}) collective-permute-start(bf16[512,256]{1,0:T(8,128)(2,1)S(1)} %get-tuple-element.97), channel_id=1, source_target_pairs={{0,192},{1,193},{32,224},{33,225},{64,128},{65,129},{96,160},{97,1... | collective-permute-start | bytes 786440 | tf_op jit(solution)/shard_map/ppermute | solution.py:31
  97.0 11.3 %collective-permute-start.18 = (bf16[512,256]{1,0:T(8,128)(2,1)S(1)}, bf16[512,256]{1,0:T(8,128)(2,1)S(1)}, u32[]{:S(2)}, u32[]{:S(2)}) collective-permute-start(bf16[512,256]{1,0:T(8,128)(2,1)S(1)} %get-tuple-element.96), channel_id=1, source_target_pairs={{0,64},{1,65},{32,96},{33,97},{64,0},{65,1},{96,32},{97,33},{128,1... | collective-permute-start | bytes 786440 | tf_op jit(solution)/shard_map/ppermute | solution.py:31
  100.6 10.3 %collective-permute-start.15 = (bf16[256,256]{1,0:T(8,128)(2,1)S(1)}, bf16[256,256]{1,0:T(8,128)(2,1)S(1)}, u32[]{:S(2)}, u32[]{:S(2)}) collective-permute-start(bf16[256,256]{1,0:T(8,128)(2,1)S(1)} %get-tuple-element.91), channel_id=1, source_target_pairs={{0,192},{1,193},{32,224},{33,225},{64,128},{65,129},{96,160},{97,1... | collective-permute-start | bytes 393224 | tf_op jit(solution)/shard_map/ppermute | solution.py:31
  108.4 6.4 %collective-permute-start.20 = (bf16[256,256]{1,0:T(8,128)(2,1)S(1)}, bf16[256,256]{1,0:T(8,128)(2,1)S(1)}, u32[]{:S(2)}, u32[]{:S(2)}) collective-permute-start(bf16[256,256]{1,0:T(8,128)(2,1)S(1)} %get-tuple-element.99), channel_id=1, source_target_pairs={{0,33},{1,32},{32,1},{33,0},{64,97},{65,96},{96,65},{97,64},{128,1... | collective-permute-start | bytes 393224 | tf_op jit(solution)/shard_map/ppermute | solution.py:31
  111.0 4.4 %collective-permute-start.16 = (bf16[128,256]{1,0:T(8,128)(2,1)S(1)}, bf16[128,256]{1,0:T(8,128)(2,1)S(1)}, u32[]{:S(2)}, u32[]{:S(2)}) collective-permute-start(bf16[128,256]{1,0:T(8,128)(2,1)S(1)} %get-tuple-element.93), channel_id=1, source_target_pairs={{0,64},{1,65},{32,96},{33,97},{64,0},{65,1},{96,32},{97,33},{128,1... | collective-permute-start | bytes 196616 | tf_op jit(solution)/shard_map/ppermute | solution.py:31
  114.9 4.4 %collective-permute-start.21 = (bf16[128,256]{1,0:T(8,128)(2,1)S(1)}, bf16[128,256]{1,0:T(8,128)(2,1)S(1)}, u32[]{:S(2)}, u32[]{:S(2)}) collective-permute-start(bf16[128,256]{1,0:T(8,128)(2,1)S(1)} %get-tuple-element.101), channel_id=1, source_target_pairs={{0,1},{1,0},{32,33},{33,32},{64,65},{65,64},{96,97},{97,96},{128,1... | collective-permute-start | bytes 196616 | tf_op jit(solution)/shard_map/ppermute | solution.py:31
  (14 other events, 88.3 us)

commit v5 on v4

--- a/solution.py
+++ b/solution.py
@@ -5,7 +5,7 @@
 from jax import lax
 from jax.experimental import pallas as pl
 from jax.experimental.pallas import tpu as pltpu
-from jax.sharding import PartitionSpec as P
+from jax.sharding import Mesh, PartitionSpec as P
 
 
 sharpness = 10.0
@@ -16,6 +16,7 @@
 kinds = (0, 1)
 bf16, f32 = jnp.bfloat16, jnp.float32
 owners = ("dp", "crop")
+block = ("z", "core")
 
 
 def swapped(value):
@@ -51,28 +52,15 @@
     return views / flat
 
 
-def fetch_codes(code_ref, buffer, semaphores, distance):
+def code_columns(code_ref, kind, distance):
     place = lax.axis_index(owners)
     half = code_ref.shape[1] // (2 * side * side)
-    copies = [[], []]
-    for kind in kinds:
-        for index, j in enumerate(near):
-            owner = place ^ (mask_of(kind, j) + mask_of(1 - kind, distance))
-            first = pl.multiple_of((owner * 2 + kind) * half, half)
-            copy = pltpu.make_async_copy(
-                code_ref.at[:, pl.ds(first, half)],
-                buffer.at[kind, :, pl.ds(index * half, half)],
-                semaphores.at[kind * side + index],
-            )
-            copy.start()
-            copies[kind].append(copy)
-    return copies
-
-
-def fetched_code(copies, buffer, kind):
-    for copy in copies[kind]:
-        copy.wait()
-    return buffer[kind]
+    parts = []
+    for j in near:
+        owner = place ^ (mask_of(kind, j) + mask_of(1 - kind, distance))
+        first = pl.multiple_of((owner * 2 + kind) * half, half)
+        parts.append(code_ref[:, pl.ds(first, half)])
+    return jnp.concatenate(parts, axis=1)
 
 
 def split_kernel(
@@ -91,7 +79,16 @@
         spread_ref[peer] = own
 
 
-def embeddings_kernel(raw_ref, z_t_ref, local_ref, outgoing_ref):
+def embeddings_kernel(code_ref, raw_ref, z_t_ref, local_ref, outgoing_ref, near_code_ref, semaphores):
+    n = semaphores.shape[0]
+    step = code_ref.shape[0] // n
+    copies = []
+    for index in range(n):
+        here = pl.ds(index * step, step)
+        copies.append(
+            pltpu.make_async_copy(code_ref.at[here], near_code_ref.at[here], semaphores.at[index])
+        )
+        copies[-1].start()
     z = normalize_rows(raw_ref[...])[0].astype(bf16).astype(f32)
     features = z.shape[-1]
     local = z[:, 1]
@@ -100,14 +97,14 @@
     local_ref[...] = local.reshape(-1, features)
     outgoing_ref[...] = (z[:, 0] + local).reshape(-1, features)
     z_t_ref[...] = z.reshape(-1, features).T.astype(bf16)
+    for copy in copies:
+        copy.wait()
 
 
 def scores_kernel(*refs, distance, n_before):
     z_t_ref, code_ref, *raw_refs = refs[:4]
     own_before, acc_before = refs[4 : 4 + n_before], refs[4 + n_before : 4 + 2 * n_before]
     exp_a_ref, exp_b_ref, soft_ref, own_ref, total_ref = refs[4 + 2 * n_before : 9 + 2 * n_before]
-    code_buf, semaphores = refs[-2:]
-    copies = fetch_codes(code_ref, code_buf, semaphores, distance)
     rows = z_t_ref.shape[1]
     soft = own = acc = None
     add = lambda a, b: b if a is None else a + b
@@ -118,7 +115,7 @@
         exponent = exponent.astype(bf16)
         exp_ref[...] = exponent
         soft = add(soft, dot(c, exponent, 0, 0))
-        own = add(own, dot(fetched_code(copies, code_buf, kind), c, 1, 0))
+        own = add(own, dot(code_columns(code_ref, kind, distance), c, 1, 0))
     soft_ref[...] = soft
     for before in own_before:
         own = own + before[...]
@@ -135,9 +132,7 @@
 
 
 def prototypes_kernel(*refs, distance, crops, own_images, first):
-    *refs, code_buf, semaphores = refs
     code_ref, *refs = refs
-    copies = fetch_codes(code_ref, code_buf, semaphores, distance)
     if first:
         totals_ref, z_t_ref, local_ref, incoming_ref = refs[:4]
         weights = row_weights(totals_ref, crops, own_images)
@@ -152,22 +147,30 @@
     exp_a_ref, exp_b_ref, *out_refs = refs
     for kind, exp_ref, out_ref in zip(kinds, (exp_a_ref, exp_b_ref), out_refs):
         grads = dot(exp_ref[...], zw, 1, 1)
-        grads = grads - dot(fetched_code(copies, code_buf, kind), target, 0, 0)
+        grads = grads - dot(code_columns(code_ref, kind, distance), target, 0, 0)
         out_ref[...] = grads.astype(out_ref.dtype)
 
 
 def rows_kernel(totals_ref, own_ref, other_ref, *refs, crops, own_images):
-    *soft_refs, out_ref = refs
-    soft_sum = sum(ref[...] for ref in soft_refs[1:]) + soft_refs[0][...]
+    *soft_refs, kept_ref, sent_ref = refs
+    soft = soft_refs[0][...]
+    for ref in soft_refs[1:]:
+        soft = soft + ref[...]
     weights = row_weights(totals_ref, crops, own_images)
-    n_proto = out_ref.shape[0]
-    features = out_ref.shape[3]
-    soft = (soft_sum * weights).T.reshape(n_proto, crops, own_images, features)
-    own = own_ref[...].reshape(n_proto, own_images, features)
-    other = other_ref[...].reshape(n_proto, own_images, features)
+    n_z, _, _, features = kept_ref.shape
+    soft = (soft * weights).T.reshape(n_z, 2, crops, own_images, features)
+    own = own_ref[...].reshape(n_z, 2, own_images, features)
+    other = other_ref[...].reshape(n_z, 2, own_images, features)
+    first = lax.axis_index("core") == 0
     for crop in range(crops):
         assigned = other if crop == 0 else own + other
-        out_ref[:, crop] = ((soft[:, crop] - assigned) * sharpness).astype(bf16)
+        grads = (soft[:, :, crop] - assigned) * sharpness
+        kept_ref[:, crop] = jnp.where(first, grads[:, 0], grads[:, 1])
+        sent_ref[:, crop] = jnp.where(first, grads[:, 1], grads[:, 0]).astype(bf16)
+
+
+def add_kernel(kept_ref, part_ref, out_ref):
+    out_ref[...] = (kept_ref[...] + part_ref[...].astype(f32)).astype(bf16)
 
 
 def finish_rows_kernel(parts_ref, raw_ref, out_ref):
@@ -220,7 +223,7 @@
         kernel,
         out_shape=out_shape,
         in_specs=[there if i in (*fetched, *held) else kept for i in range(len(operands))],
-        out_specs=jax.tree.map(lambda _: kept, out_shape),
+        out_specs=jax.tree.map(lambda _: kept, out_shape, is_leaf=lambda x: hasattr(x, 'shape')),
         scratch_shapes=[
             *(pltpu.VMEM(operands[i].shape, operands[i].dtype) for i in fetched),
             *(pltpu.SemaphoreType.DMA(()) for _ in fetched),
@@ -238,7 +241,7 @@
 
 
 def on_device(embeddings, codes, prototypes):
-    n_proto = lax.axis_size("proto")
+    n_proto = lax.axis_size(block)
     own_images, _, crops, features = embeddings.shape
     images = own_images * n_proto
     rows = images * crops
@@ -263,23 +266,26 @@
             moved.append(exchange(halves[kind], kind, distance))
         halves = [jnp.concatenate(pair) for pair in zip(halves, moved)]
         if step == 0:
-            raw_emb = lax.all_to_all(spread_emb, "proto", 0, 0)
+            raw_emb = lax.all_to_all(spread_emb, block, 0, 0)
     gathered = {0: halves}
     for d in arrivals:
         gathered[d] = []
         for kind in kinds:
             gathered[d].append(exchange(halves[kind], 1 - kind, d))
 
-    z_t, local_sum, outgoing = call(
+    z_t, local_sum, outgoing, code = call(
         embeddings_kernel,
-        (shape(features, rows, dtype=bf16), shape(images, features), shape(images, features)),
-        raw_emb.reshape(n_proto, crops, own_images, features),
-    )
-
-    code_scratch = [
-        pltpu.VMEM((2, images, side * half), bf16),
-        pltpu.SemaphoreType.DMA((2 * side,)),
-    ]
+        (
+            shape(features, rows, dtype=bf16),
+            shape(images, features),
+            shape(images, features),
+            pltpu.VMEM(code.shape, code.dtype),
+        ),
+        code, raw_emb.reshape(n_proto, crops, own_images, features),
+        held=(0,),
+        scratch=[pltpu.SemaphoreType.DMA((8,))],
+    )
+
     exponents = {}
     soft, own_sums, sums = [], [], []
     for d in (0, *arrivals):
@@ -290,8 +296,6 @@
             [shape(side * half, rows, dtype=bf16)] * 2
             + [shape(features, rows), shape(images, features), shape(*total_dims)],
             z_t, code, *gathered[d], *before,
-            held=(1,),
-            scratch=code_scratch,
         )
         soft.append(soft_part)
         own_sums.append(own_term)
@@ -299,7 +303,7 @@
     totals, outgoing = lax.optimization_barrier((totals, outgoing))
     incoming = swapped(outgoing)
     other_term = swapped(own_term)
-    totals = lax.all_to_all(totals, "proto", 0, 0)
+    totals = lax.all_to_all(totals, block, 0, 0)
 
     arrived = [[], []]
     for d in (*arrivals, 0):
@@ -313,8 +317,6 @@
             + [shape(features, rows, dtype=bf16), shape(images, features, dtype=bf16)] * first,
             code, *((totals, z_t, local_sum, incoming) if first else (zw, target)),
             *exponents[d],
-            held=(0,),
-            scratch=code_scratch,
         )
         parts = outs[:2]
         if first:
@@ -325,16 +327,19 @@
             else:
                 arrived[kind].insert(0, parts[kind])
 
+    row_shape = (n_proto // 2, crops, own_images, features)
+    kept_rows, sent_rows = call(
+        functools.partial(rows_kernel, crops=crops, own_images=own_images),
+        [shape(*row_shape), shape(*row_shape, dtype=bf16)],
+        totals, own_term, other_term, *soft,
+    )
+    sent_rows = lax.ppermute(sent_rows, "core", [(0, 1), (1, 0)])
     held_parts = [arrived[kind][0] for kind in kinds]
-    soft[0], *held_parts = lax.optimization_barrier((soft[0], *held_parts))
+    kept_rows, *held_parts = lax.optimization_barrier((kept_rows, *held_parts))
     for kind in kinds:
         arrived[kind][0] = held_parts[kind]
-    row_parts = call(
-        functools.partial(rows_kernel, crops=crops, own_images=own_images),
-        shape(n_proto, crops, own_images, features, dtype=bf16),
-        totals, own_term, other_term, *soft,
-    )
-    row_parts = lax.all_to_all(row_parts, "proto", 0, 0)
+    row_parts = call(add_kernel, shape(*row_shape, dtype=bf16), kept_rows, sent_rows)
+    row_parts = lax.all_to_all(row_parts, "z", 0, 0)
 
     held = []
     for kind in kinds:
@@ -361,14 +366,16 @@
 
 
 def solution(mesh):
+    n_dp, n_proto, n_crop = mesh.devices.shape
+    fine = Mesh(mesh.devices.reshape(n_dp, n_proto // 2, 2, n_crop), ("dp", *block, "crop"))
     return jax.shard_map(
         on_device,
-        mesh=mesh,
+        mesh=fine,
         in_specs=(
-            P(("dp", "proto"), "crop", None, None),
-            P("dp", "crop", "proto"),
-            P("proto", ("dp", "crop"), None),
+            P(("dp", *block), "crop", None, None),
+            P("dp", "crop", block),
+            P(block, ("dp", "crop"), None),
         ),
-        out_specs=(P(("dp", "proto"), "crop", None, None), P("proto", ("dp", "crop"), None)),
+        out_specs=(P(("dp", *block), "crop", None, None), P(block, ("dp", "crop"), None)),
         check_vma=False,
     )

time: 122 us -> 99.9 us (0.82)
  Pallas kernels: 29.7 us -> 18.7 us
  local copies, waits for them, and re-layouts: 8.2 us -> 0.04 us
  waiting for transfers between devices: 23.8 us -> 21.4 us
    pallas_call x17 -> x18, Pallas kernels: 29.7 us -> 18.7 us  [call(): pl.pallas_call(kernel, out_shape=out_shape, in_specs=[there if i in (*fet...]
    unnamed x31 -> x5, local copies, waits for them, and re-layouts: 8.19 us -> 0.03 us
    ppermute x20, waiting for transfers between devices: 23.8 us -> 21.4 us  [exchange(): lax.ppermute(value, owners, [(owner, owner ^ mask) for owner in range(sid...]
  transfers between devices with their start and end apart: 24 -> 25, of which waited for: 10 -> 10; matrix products, arithmetic and copies ran while one was open for 0% -> 0% of each run, Pallas kernels for 18% -> 14%
where the time goes in v5:
time: 99.9 us; the launch traced here: 98.8 us
  starting transfers between devices  44.4 us (44%)
  waiting for transfers between devices  21.4 us (21%)
  Pallas kernels  18.7 us (19%)
  blocking collectives  13.5 us (14%)
    ppermute x20, starting transfers between devices, exchange(): lax.ppermute(value, owners, [(owner, owner ^ mask) for owner in range(sid...  28.6 us
    ppermute x20, waiting for transfers between devices, exchange(): lax.ppermute(value, owners, [(owner, owner ^ mask) for owner in range(sid...  21.4 us
    pallas_call x18, Pallas kernels, call(): pl.pallas_call(kernel, out_shape=out_shape, in_specs=[there if i in (*fet...  18.7 us
    all_to_all x1, blocking collectives, on_device(): totals = lax.all_to_all(totals, block, 0, 0)  13.5 us
    all_to_all x1, starting transfers between devices, on_device(): raw_emb = lax.all_to_all(spread_emb, block, 0, 0)  8.59 us
    all_to_all x1, starting transfers between devices, on_device(): row_parts = lax.all_to_all(row_parts, 'z', 0, 0)  4.98 us
    ppermute x2, starting transfers between devices, swapped(): return lax.ppermute(value, 'crop', [(0, 1), (1, 0)])  2.11 us
  transfers between devices with their start and end apart: 25, of which 10 were waited for; matrix products, arithmetic and copies ran while one was open for 0% of the time, Pallas kernels for 14%

profile of v5, /device:TPU:32, one launch (start us, length us, event | category | flops | bytes accessed | tf_op | source)
XLA Modules:
  0.0 98.8 jit_solution(12501724572883662666)
XLA Ops:
  0.6 1.8 %shard_map.50 = (bf16[128,256]{1,0:T(8,128)(2,1)S(1)}, bf16[128,256]{1,0:T(8,128)(2,1)S(1)}, bf16[4,16,256]{2,1,0:T(8,128)(2,1)S(1)}, bf16[16,64,256]{2,1,0:T(8,128)(2,1)}) custom-call(bf16[256,256]{1,0:T(8,128)(2,1)} %bitcast.9, bf16[16,4,256]{2,1,0:T(4,128)(2,1)} %bitcast.14), custom_call_target="tpu_custom_call" | custom-call | tf_op jit(solution)/shard_map/pallas_call | solution.py:222
  4.0 8.6 %all-to-all-start = ((bf16[16,64,256]{2,1,0:T(8,128)(2,1)}), bf16[16,64,256]{2,1,0:T(8,128)(2,1)S(1)}, u32[]{:S(2)}, u32[]{:S(2)}) async-start(bf16[16,64,256]{2,1,0:T(8,128)(2,1)} %get-tuple-element.55), calls=%async_computation | async-start | bytes 1048576 | tf_op jit(solution)/shard_map/all_to_all | solution.py:269
  14.2 2.2 %collective-permute-start.4 = (bf16[256,256]{1,0:T(8,128)(2,1)S(1)}, bf16[256,256]{1,0:T(8,128)(2,1)S(1)}, u32[]{:S(2)}, u32[]{:S(2)}) collective-permute-start(bf16[256,256]{1,0:T(8,128)(2,1)S(1)} %pad_maximum_fusion.1), channel_id=1, source_target_pairs={{0,33},{1,32},{32,1},{33,0},{64,97},{65,96},{96,65},{97,64},{128,1... | collective-permute-start | bytes 393224 | tf_op jit(solution)/shard_map/ppermute | solution.py:32
  16.4 4.3 %collective-permute-done.4 = bf16[256,256]{1,0:T(8,128)(2,1)S(1)} collective-permute-done((bf16[256,256]{1,0:T(8,128)(2,1)S(1)}, bf16[256,256]{1,0:T(8,128)(2,1)S(1)}, u32[]{:S(2)}, u32[]{:S(2)}) %collective-permute-start.4) | collective-permute-done | bytes 131104 | tf_op jit(solution)/shard_map/ppermute | solution.py:32
  21.3 3.1 %collective-permute-start.1 = (bf16[256,256]{1,0:T(8,128)(2,1)S(1)}, bf16[256,256]{1,0:T(8,128)(2,1)S(1)}, u32[]{:S(2)}, u32[]{:S(2)}) collective-permute-start(bf16[256,256]{1,0:T(8,128)(2,1)S(1)} %pad_maximum_fusion), channel_id=1, source_target_pairs={{0,192},{1,193},{32,224},{33,225},{64,128},{65,129},{96,160},{97,1... | collective-permute-start | bytes 393224 | tf_op jit(solution)/shard_map/ppermute | solution.py:32
  24.4 3.2 %collective-permute-done.1 = bf16[256,256]{1,0:T(8,128)(2,1)S(1)} collective-permute-done((bf16[256,256]{1,0:T(8,128)(2,1)S(1)}, bf16[256,256]{1,0:T(8,128)(2,1)S(1)}, u32[]{:S(2)}, u32[]{:S(2)}) %collective-permute-start.1) | collective-permute-done | bytes 131104 | tf_op jit(solution)/shard_map/ppermute | solution.py:32
  27.7 2.1 %collective-permute-start.7 = (bf16[512,256]{1,0:T(8,128)(2,1)S(1)}, bf16[512,256]{1,0:T(8,128)(2,1)S(1)}, u32[]{:S(2)}, u32[]{:S(2)}) collective-permute-start(bf16[512,256]{1,0:T(8,128)(2,1)S(1)} %constant_dynamic-update-slice_fusion.3.refs_3_), channel_id=1, source_target_pairs={{0,128},{1,129},{32,160},{33,161},{64,192},{65,193},{96,224},{97,2... | collective-permute-start | bytes 786440 | tf_op jit(solution)/shard_map/ppermute | solution.py:32
  29.7 3.5 %collective-permute-start.6 = (bf16[512,256]{1,0:T(8,128)(2,1)S(1)}, bf16[512,256]{1,0:T(8,128)(2,1)S(1)}, u32[]{:S(2)}, u32[]{:S(2)}) collective-permute-start(bf16[512,256]{1,0:T(8,128)(2,1)S(1)} %constant_dynamic-update-slice_fusion.refs_2_), channel_id=1, source_target_pairs={{0,32},{1,33},{32,0},{33,1},{64,96},{65,97},{96,64},{97,65},{128,1... | collective-permute-start | bytes 786440 | tf_op jit(solution)/shard_map/ppermute | solution.py:32
  37.0 1.8 %shard_map.52 = (bf16[512,1024]{1,0:T(8,128)(2,1)S(1)}, bf16[512,1024]{1,0:T(8,128)(2,1)S(1)}, f32[256,1024]{1,0:T(8,128)S(1)}, f32[256,256]{1,0:T(8,128)S(1)}, f32[8,1024]{1,0:T(8,128)S(1)}) custom-call(bf16[256,1024]{1,0:T(8,128)(2,1)S(1)} %get-tuple-element.56.refs_0_.refs_2_, bf16[256,4096]{1,0:T(8,128)(2,1)S(1)} %get-tuple-element.57.refs_1_.refs_0_, ...), custom_call_target="tpu_custom_call" | custom-call | tf_op jit(solution)/shard_map/pallas_call | solution.py:222
  38.7 1.8 %shard_map.54 = (bf16[512,1024]{1,0:T(8,128)(2,1)S(1)}, bf16[512,1024]{1,0:T(8,128)(2,1)S(1)}, f32[256,1024]{1,0:T(8,128)S(1)}, f32[256,256]{1,0:T(8,128)S(1)}, f32[8,1024]{1,0:T(8,128)S(1)}) custom-call(bf16[256,1024]{1,0:T(8,128)(2,1)S(1)} %get-tuple-element.56.refs_0_.refs_2_, bf16[256,4096]{1,0:T(8,128)(2,1)S(1)} %get-tuple-element.57.refs_1_.refs_0_, ...), custom_call_target="tpu_custom_call" | custom-call | tf_op jit(solution)/shard_map/pallas_call | solution.py:222
  41.0 1.8 %shard_map.53 = (bf16[512,1024]{1,0:T(8,128)(2,1)S(1)}, bf16[512,1024]{1,0:T(8,128)(2,1)S(1)}, f32[256,1024]{1,0:T(8,128)S(1)}, f32[256,256]{1,0:T(8,128)S(1)}, f32[8,1024]{1,0:T(8,128)S(1)}) custom-call(bf16[256,1024]{1,0:T(8,128)(2,1)S(1)} %get-tuple-element.56.refs_0_.refs_2_, bf16[256,4096]{1,0:T(8,128)(2,1)S(1)} %get-tuple-element.57.refs_1_.refs_0_, ...), custom_call_target="tpu_custom_call" | custom-call | tf_op jit(solution)/shard_map/pallas_call | solution.py:222
  42.8 2.1 %collective-permute-done.2.refs_2_ = bf16[512,256]{1,0:T(8,128)(2,1)S(1)} collective-permute-done((bf16[512,256]{1,0:T(8,128)(2,1)S(1)}, bf16[512,256]{1,0:T(8,128)(2,1)S(1)}, u32[]{:S(2)}, u32[]{:S(2)}) %collective-permute-start.2) | collective-permute-done | bytes 262176 | tf_op jit(solution)/shard_map/ppermute | solution.py:32
  44.9 1.8 %shard_map.55 = (bf16[512,1024]{1,0:T(8,128)(2,1)S(1)}, bf16[512,1024]{1,0:T(8,128)(2,1)S(1)}, f32[256,1024]{1,0:T(8,128)S(1)}, f32[256,256]{1,0:T(8,128)S(1)}, f32[16,8,128]{2,1,0:T(8,128)S(1)}) custom-call(bf16[256,1024]{1,0:T(8,128)(2,1)S(1)} %get-tuple-element.56.refs_0_.refs_2_, bf16[256,4096]{1,0:T(8,128)(2,1)S(1)} %get-tuple-element.57.refs_1_.refs_0_, ...), custom_call_target="tpu_custom_call" | custom-call | tf_op jit(solution)/shard_map/pallas_call | solution.py:222
  46.8 2.0 %collective-permute-start.10 = (f32[256,256]{1,0:T(8,128)S(1)}, f32[256,256]{1,0:T(8,128)S(1)}, u32[]{:S(2)}, u32[]{:S(2)}) collective-permute-start(f32[256,256]{1,0:T(8,128)S(1)} %get-tuple-element.69.own_ref), channel_id=1, source_target_pairs={{0,1},{1,0},{2,3},{3,2},{4,5},{5,4},{6,7},{7,6},{8,9},{9,8},{10,11... | collective-permute-start | bytes 786440 | tf_op jit(solution)/shard_map/ppermute | solution.py:23
  48.8 13.5 %all_to_all.15.totals_ref.refs_1_ = f32[16,8,128]{2,1,0:T(8,128)S(1)} all-to-all(f32[16,8,128]{2,1,0:T(8,128)S(1)} %get-tuple-element.68), channel_id=1, replica_groups=mesh['dp'=8,'z'=8,'core'=2,'crop'=2] {'z','core'}, dimensions={0} | all-to-all | bytes 131072 | tf_op jit(solution)/shard_map/all_to_all | solution.py:306
  64.5 1.6 %shard_map.62 = (bf16[512,256]{1,0:T(8,128)(2,1)}, bf16[512,256]{1,0:T(8,128)(2,1)}) custom-call(bf16[256,4096]{1,0:T(8,128)(2,1)S(1)} %get-tuple-element.57.refs_1_.refs_0_, bf16[256,1024]{1,0:T(8,128)(2,1)S(1)} %get-tuple-element.79.refs_1_, bf16[256,256]{1,0:T(8,128)(2,1)S(1)} %get-tuple-element.80.refs_2_, ...), custom_call_target="tpu_custom_call" | custom-call | tf_op jit(solution)/shard_map/pallas_call | solution.py:222
  66.1 2.1 %collective-permute-start.15 = (bf16[512,256]{1,0:T(8,128)(2,1)}, bf16[512,256]{1,0:T(8,128)(2,1)S(1)}, u32[]{:S(2)}, u32[]{:S(2)}) collective-permute-start(bf16[512,256]{1,0:T(8,128)(2,1)} %get-tuple-element.95), channel_id=1, source_target_pairs={{0,33},{1,32},{32,1},{33,0},{64,97},{65,96},{96,65},{97,64},{128,1... | collective-permute-start | bytes 786440 | tf_op jit(solution)/shard_map/ppermute | solution.py:32
  68.2 1.6 %shard_map.61 = (bf16[512,256]{1,0:T(8,128)(2,1)}, bf16[512,256]{1,0:T(8,128)(2,1)}) custom-call(bf16[256,4096]{1,0:T(8,128)(2,1)S(1)} %get-tuple-element.57.refs_1_.refs_0_, bf16[256,1024]{1,0:T(8,128)(2,1)S(1)} %get-tuple-element.79.refs_1_, bf16[256,256]{1,0:T(8,128)(2,1)S(1)} %get-tuple-element.80.refs_2_, ...), custom_call_target="tpu_custom_call" | custom-call | tf_op jit(solution)/shard_map/pallas_call | solution.py:222
  70.6 2.2 %collective-permute-start.18 = (bf16[512,256]{1,0:T(8,128)(2,1)S(1)}, bf16[512,256]{1,0:T(8,128)(2,1)S(1)}, u32[]{:S(2)}, u32[]{:S(2)}) collective-permute-start(bf16[512,256]{1,0:T(8,128)(2,1)S(1)} %get-tuple-element.101), channel_id=1, source_target_pairs={{0,128},{1,129},{32,160},{33,161},{64,192},{65,193},{96,224},{97,2... | collective-permute-start | bytes 786440 | tf_op jit(solution)/shard_map/ppermute | solution.py:32
  73.4 2.4 %collective-permute-start.20 = (bf16[512,256]{1,0:T(8,128)(2,1)}, bf16[512,256]{1,0:T(8,128)(2,1)S(1)}, u32[]{:S(2)}, u32[]{:S(2)}) collective-permute-start(bf16[512,256]{1,0:T(8,128)(2,1)} %get-tuple-element.103), channel_id=1, source_target_pairs={{0,192},{1,193},{32,224},{33,225},{64,128},{65,129},{96,160},{97,1... | collective-permute-start | bytes 786440 | tf_op jit(solution)/shard_map/ppermute | solution.py:32
  77.4 5.0 %all-to-all-start.2 = ((bf16[8,4,16,256]{3,2,1,0:T(8,128)(2,1)}), bf16[8,4,16,256]{3,2,1,0:T(8,128)(2,1)S(1)}, u32[]{:S(2)}, u32[]{:S(2)}) async-start(bf16[8,4,16,256]{3,2,1,0:T(8,128)(2,1)} %shard_map.59), calls=%async_computation.2 | async-start | bytes 524288 | tf_op jit(solution)/shard_map/all_to_all | solution.py:342
  83.8 2.1 %collective-permute-done.20.refs_2_ = bf16[512,256]{1,0:T(8,128)(2,1)S(1)} collective-permute-done((bf16[512,256]{1,0:T(8,128)(2,1)}, bf16[512,256]{1,0:T(8,128)(2,1)S(1)}, u32[]{:S(2)}, u32[]{:S(2)}) %collective-permute-start.20) | collective-permute-done | bytes 262176 | tf_op jit(solution)/shard_map/ppermute | solution.py:32
  89.7 2.9 %collective-permute-done.21.part_ref = bf16[256,256]{1,0:T(8,128)(2,1)S(1)} collective-permute-done((bf16[256,256]{1,0:T(8,128)(2,1)S(1)}, bf16[256,256]{1,0:T(8,128)(2,1)S(1)}, u32[]{:S(2)}, u32[]{:S(2)}) %collective-permute-start.21) | collective-permute-done | bytes 131104 | tf_op jit(solution)/shard_map/ppermute | solution.py:32
  93.2 3.8 %collective-permute-done.22.part_b_ref = bf16[128,256]{1,0:T(8,128)(2,1)S(1)} collective-permute-done((bf16[128,256]{1,0:T(8,128)(2,1)S(1)}, bf16[128,256]{1,0:T(8,128)(2,1)S(1)}, u32[]{:S(2)}, u32[]{:S(2)}) %collective-permute-start.22) | collective-permute-done | bytes 65568 | tf_op jit(solution)/shard_map/ppermute | solution.py:32
  (54 shorter events, 20.9 us)
Async XLA Ops:
  2.4 11.7 %collective-permute-start.3 = (bf16[128,256]{1,0:T(8,128)(2,1)S(1)}, bf16[128,256]{1,0:T(8,128)(2,1)S(1)}, u32[]{:S(2)}, u32[]{:S(2)}) collective-permute-start(bf16[128,256]{1,0:T(8,128)(2,1)S(1)} %get-tuple-element.59), channel_id=1, source_target_pairs={{0,1},{1,0},{32,33},{33,32},{64,65},{65,64},{96,97},{97,96},{128,1... | collective-permute-start | bytes 196616 | tf_op jit(solution)/shard_map/ppermute | solution.py:32
  4.0 31.4 %all-to-all-start = ((bf16[16,64,256]{2,1,0:T(8,128)(2,1)}), bf16[16,64,256]{2,1,0:T(8,128)(2,1)S(1)}, u32[]{:S(2)}, u32[]{:S(2)}) async-start(bf16[16,64,256]{2,1,0:T(8,128)(2,1)} %get-tuple-element.55), calls=%async_computation | async-start | bytes 1048576 | tf_op jit(solution)/shard_map/all_to_all | solution.py:269
  12.6 8.7 %collective-permute-start = (bf16[128,256]{1,0:T(8,128)(2,1)S(1)}, bf16[128,256]{1,0:T(8,128)(2,1)S(1)}, u32[]{:S(2)}, u32[]{:S(2)}) collective-permute-start(bf16[128,256]{1,0:T(8,128)(2,1)S(1)} %get-tuple-element.58), channel_id=1, source_target_pairs={{0,64},{1,65},{32,96},{33,97},{64,0},{65,1},{96,32},{97,33},{128,1... | collective-permute-start | bytes 196616 | tf_op jit(solution)/shard_map/ppermute | solution.py:32
  14.2 6.5 %collective-permute-start.4 = (bf16[256,256]{1,0:T(8,128)(2,1)S(1)}, bf16[256,256]{1,0:T(8,128)(2,1)S(1)}, u32[]{:S(2)}, u32[]{:S(2)}) collective-permute-start(bf16[256,256]{1,0:T(8,128)(2,1)S(1)} %pad_maximum_fusion.1), channel_id=1, source_target_pairs={{0,33},{1,32},{32,1},{33,0},{64,97},{65,96},{96,65},{97,64},{128,1... | collective-permute-start | bytes 393224 | tf_op jit(solution)/shard_map/ppermute | solution.py:32
  20.7 13.5 %collective-permute-start.9 = (bf16[512,256]{1,0:T(8,128)(2,1)S(1)}, bf16[512,256]{1,0:T(8,128)(2,1)S(1)}, u32[]{:S(2)}, u32[]{:S(2)}) collective-permute-start(bf16[512,256]{1,0:T(8,128)(2,1)S(1)} %constant_dynamic-update-slice_fusion.3.refs_3_), channel_id=1, source_target_pairs={{0,64},{1,65},{32,96},{33,97},{64,0},{65,1},{96,32},{97,33},{128,1... | collective-permute-start | bytes 786440 | tf_op jit(solution)/shard_map/ppermute | solution.py:32
  21.3 6.3 %collective-permute-start.1 = (bf16[256,256]{1,0:T(8,128)(2,1)S(1)}, bf16[256,256]{1,0:T(8,128)(2,1)S(1)}, u32[]{:S(2)}, u32[]{:S(2)}) collective-permute-start(bf16[256,256]{1,0:T(8,128)(2,1)S(1)} %pad_maximum_fusion), channel_id=1, source_target_pairs={{0,192},{1,193},{32,224},{33,225},{64,128},{65,129},{96,160},{97,1... | collective-permute-start | bytes 393224 | tf_op jit(solution)/shard_map/ppermute | solution.py:32
  27.6 11.2 %collective-permute-start.8 = (bf16[512,256]{1,0:T(8,128)(2,1)S(1)}, bf16[512,256]{1,0:T(8,128)(2,1)S(1)}, u32[]{:S(2)}, u32[]{:S(2)}) collective-permute-start(bf16[512,256]{1,0:T(8,128)(2,1)S(1)} %constant_dynamic-update-slice_fusion.refs_2_), channel_id=1, source_target_pairs={{0,1},{1,0},{32,33},{33,32},{64,65},{65,64},{96,97},{97,96},{128,1... | collective-permute-start | bytes 786440 | tf_op jit(solution)/shard_map/ppermute | solution.py:32
  27.7 12.8 %collective-permute-start.7 = (bf16[512,256]{1,0:T(8,128)(2,1)S(1)}, bf16[512,256]{1,0:T(8,128)(2,1)S(1)}, u32[]{:S(2)}, u32[]{:S(2)}) collective-permute-start(bf16[512,256]{1,0:T(8,128)(2,1)S(1)} %constant_dynamic-update-slice_fusion.3.refs_3_), channel_id=1, source_target_pairs={{0,128},{1,129},{32,160},{33,161},{64,192},{65,193},{96,224},{97,2... | collective-permute-start | bytes 786440 | tf_op jit(solution)/shard_map/ppermute | solution.py:32
  29.7 11.3 %collective-permute-start.6 = (bf16[512,256]{1,0:T(8,128)(2,1)S(1)}, bf16[512,256]{1,0:T(8,128)(2,1)S(1)}, u32[]{:S(2)}, u32[]{:S(2)}) collective-permute-start(bf16[512,256]{1,0:T(8,128)(2,1)S(1)} %constant_dynamic-update-slice_fusion.refs_2_), channel_id=1, source_target_pairs={{0,32},{1,33},{32,0},{33,1},{64,96},{65,97},{96,64},{97,65},{128,1... | collective-permute-start | bytes 786440 | tf_op jit(solution)/shard_map/ppermute | solution.py:32
  33.2 9.6 %collective-permute-start.5 = (bf16[512,256]{1,0:T(8,128)(2,1)S(1)}, bf16[512,256]{1,0:T(8,128)(2,1)S(1)}, u32[]{:S(2)}, u32[]{:S(2)}) collective-permute-start(bf16[512,256]{1,0:T(8,128)(2,1)S(1)} %constant_dynamic-update-slice_fusion.3.refs_3_), channel_id=1, source_target_pairs={{0,192},{1,193},{32,224},{33,225},{64,128},{65,129},{96,160},{97,1... | collective-permute-start | bytes 786440 | tf_op jit(solution)/shard_map/ppermute | solution.py:32
  34.2 10.6 %collective-permute-start.2 = (bf16[512,256]{1,0:T(8,128)(2,1)S(1)}, bf16[512,256]{1,0:T(8,128)(2,1)S(1)}, u32[]{:S(2)}, u32[]{:S(2)}) collective-permute-start(bf16[512,256]{1,0:T(8,128)(2,1)S(1)} %constant_dynamic-update-slice_fusion.refs_2_), channel_id=1, source_target_pairs={{0,33},{1,32},{32,1},{33,0},{64,97},{65,96},{96,65},{97,64},{128,1... | collective-permute-start | bytes 786440 | tf_op jit(solution)/shard_map/ppermute | solution.py:32
  46.7 15.6 %collective-permute-start.11 = (f32[256,256]{1,0:T(8,128)S(1)}, f32[256,256]{1,0:T(8,128)S(1)}, u32[]{:S(2)}, u32[]{:S(2)}) collective-permute-start(f32[256,256]{1,0:T(8,128)S(1)} %get-tuple-element.76), channel_id=1, source_target_pairs={{0,1},{1,0},{2,3},{3,2},{4,5},{5,4},{6,7},{7,6},{8,9},{9,8},{10,11... | collective-permute-start | bytes 786440 | tf_op jit(solution)/shard_map/ppermute | solution.py:23
  46.8 17.2 %collective-permute-start.10 = (f32[256,256]{1,0:T(8,128)S(1)}, f32[256,256]{1,0:T(8,128)S(1)}, u32[]{:S(2)}, u32[]{:S(2)}) collective-permute-start(f32[256,256]{1,0:T(8,128)S(1)} %get-tuple-element.69.own_ref), channel_id=1, source_target_pairs={{0,1},{1,0},{2,3},{3,2},{4,5},{5,4},{6,7},{7,6},{8,9},{9,8},{10,11... | collective-permute-start | bytes 786440 | tf_op jit(solution)/shard_map/ppermute | solution.py:23
  63.2 10.1 %collective-permute-start.13 = (bf16[512,256]{1,0:T(8,128)(2,1)S(1)}, bf16[512,256]{1,0:T(8,128)(2,1)S(1)}, u32[]{:S(2)}, u32[]{:S(2)}) collective-permute-start(bf16[512,256]{1,0:T(8,128)(2,1)S(1)} %get-tuple-element.89), channel_id=1, source_target_pairs={{0,32},{1,33},{32,0},{33,1},{64,96},{65,97},{96,64},{97,65},{128,1... | collective-permute-start | bytes 786440 | tf_op jit(solution)/shard_map/ppermute | solution.py:32
  64.4 11.4 %collective-permute-start.12 = (bf16[8,4,16,256]{3,2,1,0:T(8,128)(2,1)S(1)}, bf16[8,4,16,256]{3,2,1,0:T(8,128)(2,1)S(1)}, u32[]{:S(2)}, u32[]{:S(2)}) collective-permute-start(bf16[8,4,16,256]{3,2,1,0:T(8,128)(2,1)S(1)} %get-tuple-element.86), channel_id=1, source_target_pairs={{0,2},{2,0},{1,3},{3,1},{4,6},{6,4},{5,7},{7,5},{8,10},{10,8},{9,1... | collective-permute-start | bytes 786440 | tf_op jit(solution)/shard_map/ppermute | solution.py:336
  66.1 16.3 %collective-permute-start.15 = (bf16[512,256]{1,0:T(8,128)(2,1)}, bf16[512,256]{1,0:T(8,128)(2,1)S(1)}, u32[]{:S(2)}, u32[]{:S(2)}) collective-permute-start(bf16[512,256]{1,0:T(8,128)(2,1)} %get-tuple-element.95), channel_id=1, source_target_pairs={{0,33},{1,32},{32,1},{33,0},{64,97},{65,96},{96,65},{97,64},{128,1... | collective-permute-start | bytes 786440 | tf_op jit(solution)/shard_map/ppermute | solution.py:32
  69.8 12.6 %collective-permute-start.14 = (bf16[512,256]{1,0:T(8,128)(2,1)}, bf16[512,256]{1,0:T(8,128)(2,1)S(1)}, u32[]{:S(2)}, u32[]{:S(2)}) collective-permute-start(bf16[512,256]{1,0:T(8,128)(2,1)} %get-tuple-element.92), channel_id=1, source_target_pairs={{0,1},{1,0},{32,33},{33,32},{64,65},{65,64},{96,97},{97,96},{128,1... | collective-permute-start | bytes 786440 | tf_op jit(solution)/shard_map/ppermute | solution.py:32
  70.6 13.3 %collective-permute-start.18 = (bf16[512,256]{1,0:T(8,128)(2,1)S(1)}, bf16[512,256]{1,0:T(8,128)(2,1)S(1)}, u32[]{:S(2)}, u32[]{:S(2)}) collective-permute-start(bf16[512,256]{1,0:T(8,128)(2,1)S(1)} %get-tuple-element.101), channel_id=1, source_target_pairs={{0,128},{1,129},{32,160},{33,161},{64,192},{65,193},{96,224},{97,2... | collective-permute-start | bytes 786440 | tf_op jit(solution)/shard_map/ppermute | solution.py:32
  73.4 12.6 %collective-permute-start.20 = (bf16[512,256]{1,0:T(8,128)(2,1)}, bf16[512,256]{1,0:T(8,128)(2,1)S(1)}, u32[]{:S(2)}, u32[]{:S(2)}) collective-permute-start(bf16[512,256]{1,0:T(8,128)(2,1)} %get-tuple-element.103), channel_id=1, source_target_pairs={{0,192},{1,193},{32,224},{33,225},{64,128},{65,129},{96,160},{97,1... | collective-permute-start | bytes 786440 | tf_op jit(solution)/shard_map/ppermute | solution.py:32
  75.8 10.1 %collective-permute-start.19 = (bf16[512,256]{1,0:T(8,128)(2,1)}, bf16[512,256]{1,0:T(8,128)(2,1)S(1)}, u32[]{:S(2)}, u32[]{:S(2)}) collective-permute-start(bf16[512,256]{1,0:T(8,128)(2,1)} %get-tuple-element.102), channel_id=1, source_target_pairs={{0,64},{1,65},{32,96},{33,97},{64,0},{65,1},{96,32},{97,33},{128,1... | collective-permute-start | bytes 786440 | tf_op jit(solution)/shard_map/ppermute | solution.py:32
  77.4 20.6 %all-to-all-start.2 = ((bf16[8,4,16,256]{3,2,1,0:T(8,128)(2,1)}), bf16[8,4,16,256]{3,2,1,0:T(8,128)(2,1)S(1)}, u32[]{:S(2)}, u32[]{:S(2)}) async-start(bf16[8,4,16,256]{3,2,1,0:T(8,128)(2,1)} %shard_map.59), calls=%async_computation.2 | async-start | bytes 524288 | tf_op jit(solution)/shard_map/all_to_all | solution.py:342
  82.6 6.3 %collective-permute-start.16 = (bf16[256,256]{1,0:T(8,128)(2,1)S(1)}, bf16[256,256]{1,0:T(8,128)(2,1)S(1)}, u32[]{:S(2)}, u32[]{:S(2)}) collective-permute-start(bf16[256,256]{1,0:T(8,128)(2,1)S(1)} %get-tuple-element.97), channel_id=1, source_target_pairs={{0,192},{1,193},{32,224},{33,225},{64,128},{65,129},{96,160},{97,1... | collective-permute-start | bytes 393224 | tf_op jit(solution)/shard_map/ppermute | solution.py:32
  86.0 6.6 %collective-permute-start.21 = (bf16[256,256]{1,0:T(8,128)(2,1)S(1)}, bf16[256,256]{1,0:T(8,128)(2,1)S(1)}, u32[]{:S(2)}, u32[]{:S(2)}) collective-permute-start(bf16[256,256]{1,0:T(8,128)(2,1)S(1)} %get-tuple-element.105), channel_id=1, source_target_pairs={{0,33},{1,32},{32,1},{33,0},{64,97},{65,96},{96,65},{97,64},{128,1... | collective-permute-start | bytes 393224 | tf_op jit(solution)/shard_map/ppermute | solution.py:32
  92.7 4.4 %collective-permute-start.22 = (bf16[128,256]{1,0:T(8,128)(2,1)S(1)}, bf16[128,256]{1,0:T(8,128)(2,1)S(1)}, u32[]{:S(2)}, u32[]{:S(2)}) collective-permute-start(bf16[128,256]{1,0:T(8,128)(2,1)S(1)} %get-tuple-element.107), channel_id=1, source_target_pairs={{0,1},{1,0},{32,33},{33,32},{64,65},{65,64},{96,97},{97,96},{128,1... | collective-permute-start | bytes 196616 | tf_op jit(solution)/shard_map/ppermute | solution.py:32
  (2 other events, 24.0 us)

commit v6 on v5

--- a/solution.py
+++ b/solution.py
@@ -79,7 +79,9 @@
         spread_ref[peer] = own
 
 
-def embeddings_kernel(code_ref, raw_ref, z_t_ref, local_ref, outgoing_ref, near_code_ref, semaphores):
+def embeddings_kernel(
+    code_ref, own_ref, other_ref, z_t_ref, local_ref, outgoing_ref, near_code_ref, semaphores
+):
     n = semaphores.shape[0]
     step = code_ref.shape[0] // n
     copies = []
@@ -89,7 +91,10 @@
             pltpu.make_async_copy(code_ref.at[here], near_code_ref.at[here], semaphores.at[index])
         )
         copies[-1].start()
-    z = normalize_rows(raw_ref[...])[0].astype(bf16).astype(f32)
+    first = lax.axis_index("core") == 0
+    own, other = own_ref[...].astype(f32), other_ref[...].astype(f32)
+    raw = jnp.stack([jnp.where(first, own, other), jnp.where(first, other, own)], axis=1)
+    z = normalize_rows(raw.reshape(-1, *own.shape[1:]))[0].astype(bf16).astype(f32)
     features = z.shape[-1]
     local = z[:, 1]
     for crop in range(2, z.shape[1]):
@@ -255,18 +260,18 @@
             shape(half, features, dtype=bf16),
             shape(half, features, dtype=bf16),
             shape(crops, own_images, features, dtype=bf16),
-            shape(n_proto, own_rows, features, dtype=bf16),
+            shape(n_proto // 2, own_rows, features, dtype=bf16),
         ],
         prototypes[0], embeddings[:, 0],
         fetched=(0, 1), held=(0, 1),
     )
-    for step, distance in enumerate((1, 3)):
+    for distance in (1, 3):
         moved = []
         for kind in kinds:
             moved.append(exchange(halves[kind], kind, distance))
         halves = [jnp.concatenate(pair) for pair in zip(halves, moved)]
-        if step == 0:
-            raw_emb = lax.all_to_all(spread_emb, block, 0, 0)
+    own_core = lax.all_to_all(spread_emb, "z", 0, 0)
+    other_core = lax.ppermute(own_core, "core", [(0, 1), (1, 0)])
     gathered = {0: halves}
     for d in arrivals:
         gathered[d] = []
@@ -281,7 +286,10 @@
             shape(images, features),
             pltpu.VMEM(code.shape, code.dtype),
         ),
-        code, raw_emb.reshape(n_proto, crops, own_images, features),
+        code, *(
+            each.reshape(n_proto // 2, crops, own_images, features)
+            for each in (own_core, other_core)
+        ),
         held=(0,),
         scratch=[pltpu.SemaphoreType.DMA((8,))],
     )

time: 99.9 us -> 103 us (1.031)
  waiting for transfers between devices: 21.4 us -> 26.8 us
  blocking collectives: 13.5 us -> 11.8 us
    ppermute x20, waiting for transfers between devices: 21.4 us -> 25.1 us  [exchange(): lax.ppermute(value, owners, [(owner, owner ^ mask) for owner in range(sid...]
    all_to_all x1, blocking collectives: 13.5 us -> 11.8 us  [on_device(): totals = lax.all_to_all(totals, block, 0, 0)]
    all_to_all x1, waiting for transfers between devices: 0.01 us -> 1.73 us  [on_device(): own_core = lax.all_to_all(spread_emb, 'z', 0, 0)]
  transfers between devices with their start and end apart: 25 -> 26, of which waited for: 10 -> 11; matrix products, arithmetic and copies ran while one was open for 0% -> 0% of each run, Pallas kernels for 14% -> 14%
where the time goes in v6:
time: 103 us; the launch traced here: 102 us
  starting transfers between devices  44.1 us (43%)
  waiting for transfers between devices  26.8 us (26%)
  Pallas kernels  18.8 us (18%)
  blocking collectives  11.8 us (11%)
    ppermute x20, starting transfers between devices, exchange(): lax.ppermute(value, owners, [(owner, owner ^ mask) for owner in range(sid...  28.1 us
    ppermute x20, waiting for transfers between devices, exchange(): lax.ppermute(value, owners, [(owner, owner ^ mask) for owner in range(sid...  25.1 us
    pallas_call x18, Pallas kernels, call(): pl.pallas_call(kernel, out_shape=out_shape, in_specs=[there if i in (*fet...  18.8 us
    all_to_all x1, blocking collectives, on_device(): totals = lax.all_to_all(totals, block, 0, 0)  11.8 us
    all_to_all x1, starting transfers between devices, on_device(): own_core = lax.all_to_all(spread_emb, 'z', 0, 0)  8.57 us
    all_to_all x1, starting transfers between devices, on_device(): row_parts = lax.all_to_all(row_parts, 'z', 0, 0)  4.98 us
    ppermute x2, starting transfers between devices, swapped(): return lax.ppermute(value, 'crop', [(0, 1), (1, 0)])  2.11 us
  transfers between devices with their start and end apart: 26, of which 11 were waited for; matrix products, arithmetic and copies ran while one was open for 0% of the time, Pallas kernels for 14%

profile of v6, /device:TPU:32, one launch (start us, length us, event | category | flops | bytes accessed | tf_op | source)
XLA Modules:
  0.0 102.4 jit_solution(11967212039601475139)
XLA Ops:
  3.9 8.6 %all-to-all-start = ((bf16[8,64,256]{2,1,0:T(8,128)(2,1)}), bf16[8,64,256]{2,1,0:T(8,128)(2,1)S(1)}, u32[]{:S(2)}, u32[]{:S(2)}) async-start(bf16[8,64,256]{2,1,0:T(8,128)(2,1)} %get-tuple-element.55), calls=%async_computation | async-start | bytes 524288 | tf_op jit(solution)/shard_map/all_to_all | solution.py:273
  14.0 2.2 %collective-permute-start.5 = (bf16[256,256]{1,0:T(8,128)(2,1)S(1)}, bf16[256,256]{1,0:T(8,128)(2,1)S(1)}, u32[]{:S(2)}, u32[]{:S(2)}) collective-permute-start(bf16[256,256]{1,0:T(8,128)(2,1)S(1)} %pad_maximum_fusion.1), channel_id=1, source_target_pairs={{0,33},{1,32},{32,1},{33,0},{64,97},{65,96},{96,65},{97,64},{128,1... | collective-permute-start | bytes 393224 | tf_op jit(solution)/shard_map/ppermute | solution.py:32
  16.3 4.1 %collective-permute-done.5 = bf16[256,256]{1,0:T(8,128)(2,1)S(1)} collective-permute-done((bf16[256,256]{1,0:T(8,128)(2,1)S(1)}, bf16[256,256]{1,0:T(8,128)(2,1)S(1)}, u32[]{:S(2)}, u32[]{:S(2)}) %collective-permute-start.5) | collective-permute-done | bytes 131104 | tf_op jit(solution)/shard_map/ppermute | solution.py:32
  20.9 1.7 %all-to-all-done = bf16[8,64,256]{2,1,0:T(8,128)(2,1)S(1)} async-done(((bf16[8,64,256]{2,1,0:T(8,128)(2,1)}), bf16[8,64,256]{2,1,0:T(8,128)(2,1)S(1)}, u32[]{:S(2)}, u32[]{:S(2)}) %all-to-all-start) | async-done | bytes 262176 | tf_op jit(solution)/shard_map/all_to_all | solution.py:273
  22.6 3.1 %collective-permute-start.2 = (bf16[256,256]{1,0:T(8,128)(2,1)S(1)}, bf16[256,256]{1,0:T(8,128)(2,1)S(1)}, u32[]{:S(2)}, u32[]{:S(2)}) collective-permute-start(bf16[256,256]{1,0:T(8,128)(2,1)S(1)} %pad_maximum_fusion), channel_id=1, source_target_pairs={{0,192},{1,193},{32,224},{33,225},{64,128},{65,129},{96,160},{97,1... | collective-permute-start | bytes 393224 | tf_op jit(solution)/shard_map/ppermute | solution.py:32
  25.7 4.2 %collective-permute-done.2 = bf16[256,256]{1,0:T(8,128)(2,1)S(1)} collective-permute-done((bf16[256,256]{1,0:T(8,128)(2,1)S(1)}, bf16[256,256]{1,0:T(8,128)(2,1)S(1)}, u32[]{:S(2)}, u32[]{:S(2)}) %collective-permute-start.2) | collective-permute-done | bytes 131104 | tf_op jit(solution)/shard_map/ppermute | solution.py:32
  30.5 1.9 %collective-permute-start.8 = (bf16[512,256]{1,0:T(8,128)(2,1)S(1)}, bf16[512,256]{1,0:T(8,128)(2,1)S(1)}, u32[]{:S(2)}, u32[]{:S(2)}) collective-permute-start(bf16[512,256]{1,0:T(8,128)(2,1)S(1)} %constant_dynamic-update-slice_fusion.3.refs_3_), channel_id=1, source_target_pairs={{0,128},{1,129},{32,160},{33,161},{64,192},{65,193},{96,224},{97,2... | collective-permute-start | bytes 786440 | tf_op jit(solution)/shard_map/ppermute | solution.py:32
  32.4 3.0 %collective-permute-start.7 = (bf16[512,256]{1,0:T(8,128)(2,1)S(1)}, bf16[512,256]{1,0:T(8,128)(2,1)S(1)}, u32[]{:S(2)}, u32[]{:S(2)}) collective-permute-start(bf16[512,256]{1,0:T(8,128)(2,1)S(1)} %constant_dynamic-update-slice_fusion.refs_2_), channel_id=1, source_target_pairs={{0,32},{1,33},{32,0},{33,1},{64,96},{65,97},{96,64},{97,65},{128,1... | collective-permute-start | bytes 786440 | tf_op jit(solution)/shard_map/ppermute | solution.py:32
  37.7 1.8 %shard_map.51 = (bf16[256,1024]{1,0:T(8,128)(2,1)S(1)}, f32[256,256]{1,0:T(8,128)S(1)}, f32[256,256]{1,0:T(8,128)S(1)}, bf16[256,4096]{1,0:T(8,128)(2,1)S(1)}) custom-call(bf16[256,4096]{1,0:T(8,128)(2,1)} %bitcast.13, bf16[8,4,16,256]{3,2,1,0:T(8,128)(2,1)S(1)} %bitcast.9, bf16[8,4,16,256]{3,2,1,0:T(8,128)(2,1)S(1)} %bitcast.12), custom_call_target="tpu_custom_call" | custom-call | tf_op jit(solution)/shard_map/pallas_call | solution.py:227
  39.4 1.8 %shard_map.52 = (bf16[512,1024]{1,0:T(8,128)(2,1)S(1)}, bf16[512,1024]{1,0:T(8,128)(2,1)S(1)}, f32[256,1024]{1,0:T(8,128)S(1)}, f32[256,256]{1,0:T(8,128)S(1)}, f32[8,1024]{1,0:T(8,128)S(1)}) custom-call(bf16[256,1024]{1,0:T(8,128)(2,1)S(1)} %get-tuple-element.56.refs_0_.refs_2_, bf16[256,4096]{1,0:T(8,128)(2,1)S(1)} %get-tuple-element.57.refs_1_.refs_0_, ...), custom_call_target="tpu_custom_call" | custom-call | tf_op jit(solution)/shard_map/pallas_call | solution.py:227
  41.2 1.8 %shard_map.54 = (bf16[512,1024]{1,0:T(8,128)(2,1)S(1)}, bf16[512,1024]{1,0:T(8,128)(2,1)S(1)}, f32[256,1024]{1,0:T(8,128)S(1)}, f32[256,256]{1,0:T(8,128)S(1)}, f32[8,1024]{1,0:T(8,128)S(1)}) custom-call(bf16[256,1024]{1,0:T(8,128)(2,1)S(1)} %get-tuple-element.56.refs_0_.refs_2_, bf16[256,4096]{1,0:T(8,128)(2,1)S(1)} %get-tuple-element.57.refs_1_.refs_0_, ...), custom_call_target="tpu_custom_call" | custom-call | tf_op jit(solution)/shard_map/pallas_call | solution.py:227
  43.0 2.2 %collective-permute-done.7.refs_2_ = bf16[512,256]{1,0:T(8,128)(2,1)S(1)} collective-permute-done((bf16[512,256]{1,0:T(8,128)(2,1)S(1)}, bf16[512,256]{1,0:T(8,128)(2,1)S(1)}, u32[]{:S(2)}, u32[]{:S(2)}) %collective-permute-start.7) | collective-permute-done | bytes 262176 | tf_op jit(solution)/shard_map/ppermute | solution.py:32
  45.2 1.8 %shard_map.53 = (bf16[512,1024]{1,0:T(8,128)(2,1)S(1)}, bf16[512,1024]{1,0:T(8,128)(2,1)S(1)}, f32[256,1024]{1,0:T(8,128)S(1)}, f32[256,256]{1,0:T(8,128)S(1)}, f32[8,1024]{1,0:T(8,128)S(1)}) custom-call(bf16[256,1024]{1,0:T(8,128)(2,1)S(1)} %get-tuple-element.56.refs_0_.refs_2_, bf16[256,4096]{1,0:T(8,128)(2,1)S(1)} %get-tuple-element.57.refs_1_.refs_0_, ...), custom_call_target="tpu_custom_call" | custom-call | tf_op jit(solution)/shard_map/pallas_call | solution.py:227
  46.9 3.0 %collective-permute-done.3.refs_2_ = bf16[512,256]{1,0:T(8,128)(2,1)S(1)} collective-permute-done((bf16[512,256]{1,0:T(8,128)(2,1)S(1)}, bf16[512,256]{1,0:T(8,128)(2,1)S(1)}, u32[]{:S(2)}, u32[]{:S(2)}) %collective-permute-start.3) | collective-permute-done | bytes 262176 | tf_op jit(solution)/shard_map/ppermute | solution.py:32
  49.9 1.8 %shard_map.55 = (bf16[512,1024]{1,0:T(8,128)(2,1)S(1)}, bf16[512,1024]{1,0:T(8,128)(2,1)S(1)}, f32[256,1024]{1,0:T(8,128)S(1)}, f32[256,256]{1,0:T(8,128)S(1)}, f32[16,8,128]{2,1,0:T(8,128)S(1)}) custom-call(bf16[256,1024]{1,0:T(8,128)(2,1)S(1)} %get-tuple-element.56.refs_0_.refs_2_, bf16[256,4096]{1,0:T(8,128)(2,1)S(1)} %get-tuple-element.57.refs_1_.refs_0_, ...), custom_call_target="tpu_custom_call" | custom-call | tf_op jit(solution)/shard_map/pallas_call | solution.py:227
  51.8 2.0 %collective-permute-start.11 = (f32[256,256]{1,0:T(8,128)S(1)}, f32[256,256]{1,0:T(8,128)S(1)}, u32[]{:S(2)}, u32[]{:S(2)}) collective-permute-start(f32[256,256]{1,0:T(8,128)S(1)} %get-tuple-element.69.own_ref), channel_id=1, source_target_pairs={{0,1},{1,0},{2,3},{3,2},{4,5},{5,4},{6,7},{7,6},{8,9},{9,8},{10,11... | collective-permute-start | bytes 786440 | tf_op jit(solution)/shard_map/ppermute | solution.py:23
  53.8 11.8 %all_to_all.15.totals_ref.refs_1_ = f32[16,8,128]{2,1,0:T(8,128)S(1)} all-to-all(f32[16,8,128]{2,1,0:T(8,128)S(1)} %get-tuple-element.68), channel_id=1, replica_groups=mesh['dp'=8,'z'=8,'core'=2,'crop'=2] {'z','core'}, dimensions={0} | all-to-all | bytes 131072 | tf_op jit(solution)/shard_map/all_to_all | solution.py:314
  69.6 2.1 %collective-permute-start.16 = (bf16[512,256]{1,0:T(8,128)(2,1)}, bf16[512,256]{1,0:T(8,128)(2,1)S(1)}, u32[]{:S(2)}, u32[]{:S(2)}) collective-permute-start(bf16[512,256]{1,0:T(8,128)(2,1)} %get-tuple-element.95), channel_id=1, source_target_pairs={{0,33},{1,32},{32,1},{33,0},{64,97},{65,96},{96,65},{97,64},{128,1... | collective-permute-start | bytes 786440 | tf_op jit(solution)/shard_map/ppermute | solution.py:32
  74.1 2.2 %collective-permute-start.19 = (bf16[512,256]{1,0:T(8,128)(2,1)S(1)}, bf16[512,256]{1,0:T(8,128)(2,1)S(1)}, u32[]{:S(2)}, u32[]{:S(2)}) collective-permute-start(bf16[512,256]{1,0:T(8,128)(2,1)S(1)} %get-tuple-element.101), channel_id=1, source_target_pairs={{0,128},{1,129},{32,160},{33,161},{64,192},{65,193},{96,224},{97,2... | collective-permute-start | bytes 786440 | tf_op jit(solution)/shard_map/ppermute | solution.py:32
  76.6 2.4 %collective-permute-start.21 = (bf16[512,256]{1,0:T(8,128)(2,1)}, bf16[512,256]{1,0:T(8,128)(2,1)S(1)}, u32[]{:S(2)}, u32[]{:S(2)}) collective-permute-start(bf16[512,256]{1,0:T(8,128)(2,1)} %get-tuple-element.103), channel_id=1, source_target_pairs={{0,192},{1,193},{32,224},{33,225},{64,128},{65,129},{96,160},{97,1... | collective-permute-start | bytes 786440 | tf_op jit(solution)/shard_map/ppermute | solution.py:32
  80.7 5.0 %all-to-all-start.2 = ((bf16[8,4,16,256]{3,2,1,0:T(8,128)(2,1)}), bf16[8,4,16,256]{3,2,1,0:T(8,128)(2,1)S(1)}, u32[]{:S(2)}, u32[]{:S(2)}) async-start(bf16[8,4,16,256]{3,2,1,0:T(8,128)(2,1)} %shard_map.59), calls=%async_computation.2 | async-start | bytes 524288 | tf_op jit(solution)/shard_map/all_to_all | solution.py:350
  86.8 2.6 %collective-permute-done.21.refs_2_ = bf16[512,256]{1,0:T(8,128)(2,1)S(1)} collective-permute-done((bf16[512,256]{1,0:T(8,128)(2,1)}, bf16[512,256]{1,0:T(8,128)(2,1)S(1)}, u32[]{:S(2)}, u32[]{:S(2)}) %collective-permute-start.21) | collective-permute-done | bytes 262176 | tf_op jit(solution)/shard_map/ppermute | solution.py:32
  93.0 3.2 %collective-permute-done.22.part_ref = bf16[256,256]{1,0:T(8,128)(2,1)S(1)} collective-permute-done((bf16[256,256]{1,0:T(8,128)(2,1)S(1)}, bf16[256,256]{1,0:T(8,128)(2,1)S(1)}, u32[]{:S(2)}, u32[]{:S(2)}) %collective-permute-start.22) | collective-permute-done | bytes 131104 | tf_op jit(solution)/shard_map/ppermute | solution.py:32
  96.5 4.0 %collective-permute-done.23.part_b_ref = bf16[128,256]{1,0:T(8,128)(2,1)S(1)} collective-permute-done((bf16[128,256]{1,0:T(8,128)(2,1)S(1)}, bf16[128,256]{1,0:T(8,128)(2,1)S(1)}, u32[]{:S(2)}, u32[]{:S(2)}) %collective-permute-start.23) | collective-permute-done | bytes 65568 | tf_op jit(solution)/shard_map/ppermute | solution.py:32
  (56 shorter events, 23.5 us)
Async XLA Ops:
  2.3 11.7 %collective-permute-start.4 = (bf16[128,256]{1,0:T(8,128)(2,1)S(1)}, bf16[128,256]{1,0:T(8,128)(2,1)S(1)}, u32[]{:S(2)}, u32[]{:S(2)}) collective-permute-start(bf16[128,256]{1,0:T(8,128)(2,1)S(1)} %get-tuple-element.59), channel_id=1, source_target_pairs={{0,1},{1,0},{32,33},{33,32},{64,65},{65,64},{96,97},{97,96},{128,1... | collective-permute-start | bytes 196616 | tf_op jit(solution)/shard_map/ppermute | solution.py:32
  3.9 18.7 %all-to-all-start = ((bf16[8,64,256]{2,1,0:T(8,128)(2,1)}), bf16[8,64,256]{2,1,0:T(8,128)(2,1)S(1)}, u32[]{:S(2)}, u32[]{:S(2)}) async-start(bf16[8,64,256]{2,1,0:T(8,128)(2,1)} %get-tuple-element.55), calls=%async_computation | async-start | bytes 524288 | tf_op jit(solution)/shard_map/all_to_all | solution.py:273
  12.5 10.1 %collective-permute-start.1 = (bf16[128,256]{1,0:T(8,128)(2,1)S(1)}, bf16[128,256]{1,0:T(8,128)(2,1)S(1)}, u32[]{:S(2)}, u32[]{:S(2)}) collective-permute-start(bf16[128,256]{1,0:T(8,128)(2,1)S(1)} %get-tuple-element.58), channel_id=1, source_target_pairs={{0,64},{1,65},{32,96},{33,97},{64,0},{65,1},{96,32},{97,33},{128,1... | collective-permute-start | bytes 196616 | tf_op jit(solution)/shard_map/ppermute | solution.py:32
  14.0 6.3 %collective-permute-start.5 = (bf16[256,256]{1,0:T(8,128)(2,1)S(1)}, bf16[256,256]{1,0:T(8,128)(2,1)S(1)}, u32[]{:S(2)}, u32[]{:S(2)}) collective-permute-start(bf16[256,256]{1,0:T(8,128)(2,1)S(1)} %pad_maximum_fusion.1), channel_id=1, source_target_pairs={{0,33},{1,32},{32,1},{33,0},{64,97},{65,96},{96,65},{97,64},{128,1... | collective-permute-start | bytes 393224 | tf_op jit(solution)/shard_map/ppermute | solution.py:32
  20.3 15.1 %collective-permute-start.10 = (bf16[512,256]{1,0:T(8,128)(2,1)S(1)}, bf16[512,256]{1,0:T(8,128)(2,1)S(1)}, u32[]{:S(2)}, u32[]{:S(2)}) collective-permute-start(bf16[512,256]{1,0:T(8,128)(2,1)S(1)} %constant_dynamic-update-slice_fusion.3.refs_3_), channel_id=1, source_target_pairs={{0,64},{1,65},{32,96},{33,97},{64,0},{65,1},{96,32},{97,33},{128,1... | collective-permute-start | bytes 786440 | tf_op jit(solution)/shard_map/ppermute | solution.py:32
  22.6 13.9 %collective-permute-start = (bf16[8,64,256]{2,1,0:T(8,128)(2,1)S(1)}, bf16[8,64,256]{2,1,0:T(8,128)(2,1)S(1)}, u32[]{:S(2)}, u32[]{:S(2)}) collective-permute-start(bf16[8,64,256]{2,1,0:T(8,128)(2,1)S(1)} %all-to-all-done), channel_id=1, source_target_pairs={{0,2},{2,0},{1,3},{3,1},{4,6},{6,4},{5,7},{7,5},{8,10},{10,8},{9,1... | collective-permute-start | bytes 786440 | tf_op jit(solution)/shard_map/ppermute | solution.py:274
  22.6 7.3 %collective-permute-start.2 = (bf16[256,256]{1,0:T(8,128)(2,1)S(1)}, bf16[256,256]{1,0:T(8,128)(2,1)S(1)}, u32[]{:S(2)}, u32[]{:S(2)}) collective-permute-start(bf16[256,256]{1,0:T(8,128)(2,1)S(1)} %pad_maximum_fusion), channel_id=1, source_target_pairs={{0,192},{1,193},{32,224},{33,225},{64,128},{65,129},{96,160},{97,1... | collective-permute-start | bytes 393224 | tf_op jit(solution)/shard_map/ppermute | solution.py:32
  29.9 11.3 %collective-permute-start.9 = (bf16[512,256]{1,0:T(8,128)(2,1)S(1)}, bf16[512,256]{1,0:T(8,128)(2,1)S(1)}, u32[]{:S(2)}, u32[]{:S(2)}) collective-permute-start(bf16[512,256]{1,0:T(8,128)(2,1)S(1)} %constant_dynamic-update-slice_fusion.refs_2_), channel_id=1, source_target_pairs={{0,1},{1,0},{32,33},{33,32},{64,65},{65,64},{96,97},{97,96},{128,1... | collective-permute-start | bytes 786440 | tf_op jit(solution)/shard_map/ppermute | solution.py:32
  30.5 12.4 %collective-permute-start.8 = (bf16[512,256]{1,0:T(8,128)(2,1)S(1)}, bf16[512,256]{1,0:T(8,128)(2,1)S(1)}, u32[]{:S(2)}, u32[]{:S(2)}) collective-permute-start(bf16[512,256]{1,0:T(8,128)(2,1)S(1)} %constant_dynamic-update-slice_fusion.3.refs_3_), channel_id=1, source_target_pairs={{0,128},{1,129},{32,160},{33,161},{64,192},{65,193},{96,224},{97,2... | collective-permute-start | bytes 786440 | tf_op jit(solution)/shard_map/ppermute | solution.py:32
  32.4 12.7 %collective-permute-start.7 = (bf16[512,256]{1,0:T(8,128)(2,1)S(1)}, bf16[512,256]{1,0:T(8,128)(2,1)S(1)}, u32[]{:S(2)}, u32[]{:S(2)}) collective-permute-start(bf16[512,256]{1,0:T(8,128)(2,1)S(1)} %constant_dynamic-update-slice_fusion.refs_2_), channel_id=1, source_target_pairs={{0,32},{1,33},{32,0},{33,1},{64,96},{65,97},{96,64},{97,65},{128,1... | collective-permute-start | bytes 786440 | tf_op jit(solution)/shard_map/ppermute | solution.py:32
  35.5 11.5 %collective-permute-start.6 = (bf16[512,256]{1,0:T(8,128)(2,1)S(1)}, bf16[512,256]{1,0:T(8,128)(2,1)S(1)}, u32[]{:S(2)}, u32[]{:S(2)}) collective-permute-start(bf16[512,256]{1,0:T(8,128)(2,1)S(1)} %constant_dynamic-update-slice_fusion.3.refs_3_), channel_id=1, source_target_pairs={{0,192},{1,193},{32,224},{33,225},{64,128},{65,129},{96,160},{97,1... | collective-permute-start | bytes 786440 | tf_op jit(solution)/shard_map/ppermute | solution.py:32
  36.5 13.4 %collective-permute-start.3 = (bf16[512,256]{1,0:T(8,128)(2,1)S(1)}, bf16[512,256]{1,0:T(8,128)(2,1)S(1)}, u32[]{:S(2)}, u32[]{:S(2)}) collective-permute-start(bf16[512,256]{1,0:T(8,128)(2,1)S(1)} %constant_dynamic-update-slice_fusion.refs_2_), channel_id=1, source_target_pairs={{0,33},{1,32},{32,1},{33,0},{64,97},{65,96},{96,65},{97,64},{128,1... | collective-permute-start | bytes 786440 | tf_op jit(solution)/shard_map/ppermute | solution.py:32
  51.7 13.9 %collective-permute-start.12 = (f32[256,256]{1,0:T(8,128)S(1)}, f32[256,256]{1,0:T(8,128)S(1)}, u32[]{:S(2)}, u32[]{:S(2)}) collective-permute-start(f32[256,256]{1,0:T(8,128)S(1)} %get-tuple-element.76), channel_id=1, source_target_pairs={{0,1},{1,0},{2,3},{3,2},{4,5},{5,4},{6,7},{7,6},{8,9},{9,8},{10,11... | collective-permute-start | bytes 786440 | tf_op jit(solution)/shard_map/ppermute | solution.py:23
  51.8 15.5 %collective-permute-start.11 = (f32[256,256]{1,0:T(8,128)S(1)}, f32[256,256]{1,0:T(8,128)S(1)}, u32[]{:S(2)}, u32[]{:S(2)}) collective-permute-start(f32[256,256]{1,0:T(8,128)S(1)} %get-tuple-element.69.own_ref), channel_id=1, source_target_pairs={{0,1},{1,0},{2,3},{3,2},{4,5},{5,4},{6,7},{7,6},{8,9},{9,8},{10,11... | collective-permute-start | bytes 786440 | tf_op jit(solution)/shard_map/ppermute | solution.py:23
  66.5 10.1 %collective-permute-start.14 = (bf16[512,256]{1,0:T(8,128)(2,1)S(1)}, bf16[512,256]{1,0:T(8,128)(2,1)S(1)}, u32[]{:S(2)}, u32[]{:S(2)}) collective-permute-start(bf16[512,256]{1,0:T(8,128)(2,1)S(1)} %get-tuple-element.89), channel_id=1, source_target_pairs={{0,32},{1,33},{32,0},{33,1},{64,96},{65,97},{96,64},{97,65},{128,1... | collective-permute-start | bytes 786440 | tf_op jit(solution)/shard_map/ppermute | solution.py:32
  67.7 11.3 %collective-permute-start.13 = (bf16[8,4,16,256]{3,2,1,0:T(8,128)(2,1)S(1)}, bf16[8,4,16,256]{3,2,1,0:T(8,128)(2,1)S(1)}, u32[]{:S(2)}, u32[]{:S(2)}) collective-permute-start(bf16[8,4,16,256]{3,2,1,0:T(8,128)(2,1)S(1)} %get-tuple-element.86), channel_id=1, source_target_pairs={{0,2},{2,0},{1,3},{3,1},{4,6},{6,4},{5,7},{7,5},{8,10},{10,8},{9,1... | collective-permute-start | bytes 786440 | tf_op jit(solution)/shard_map/ppermute | solution.py:344
  69.6 16.0 %collective-permute-start.16 = (bf16[512,256]{1,0:T(8,128)(2,1)}, bf16[512,256]{1,0:T(8,128)(2,1)S(1)}, u32[]{:S(2)}, u32[]{:S(2)}) collective-permute-start(bf16[512,256]{1,0:T(8,128)(2,1)} %get-tuple-element.95), channel_id=1, source_target_pairs={{0,33},{1,32},{32,1},{33,0},{64,97},{65,96},{96,65},{97,64},{128,1... | collective-permute-start | bytes 786440 | tf_op jit(solution)/shard_map/ppermute | solution.py:32
  73.4 12.3 %collective-permute-start.15 = (bf16[512,256]{1,0:T(8,128)(2,1)}, bf16[512,256]{1,0:T(8,128)(2,1)S(1)}, u32[]{:S(2)}, u32[]{:S(2)}) collective-permute-start(bf16[512,256]{1,0:T(8,128)(2,1)} %get-tuple-element.92), channel_id=1, source_target_pairs={{0,1},{1,0},{32,33},{33,32},{64,65},{65,64},{96,97},{97,96},{128,1... | collective-permute-start | bytes 786440 | tf_op jit(solution)/shard_map/ppermute | solution.py:32
  74.1 12.7 %collective-permute-start.19 = (bf16[512,256]{1,0:T(8,128)(2,1)S(1)}, bf16[512,256]{1,0:T(8,128)(2,1)S(1)}, u32[]{:S(2)}, u32[]{:S(2)}) collective-permute-start(bf16[512,256]{1,0:T(8,128)(2,1)S(1)} %get-tuple-element.101), channel_id=1, source_target_pairs={{0,128},{1,129},{32,160},{33,161},{64,192},{65,193},{96,224},{97,2... | collective-permute-start | bytes 786440 | tf_op jit(solution)/shard_map/ppermute | solution.py:32
  76.6 12.8 %collective-permute-start.21 = (bf16[512,256]{1,0:T(8,128)(2,1)}, bf16[512,256]{1,0:T(8,128)(2,1)S(1)}, u32[]{:S(2)}, u32[]{:S(2)}) collective-permute-start(bf16[512,256]{1,0:T(8,128)(2,1)} %get-tuple-element.103), channel_id=1, source_target_pairs={{0,192},{1,193},{32,224},{33,225},{64,128},{65,129},{96,160},{97,1... | collective-permute-start | bytes 786440 | tf_op jit(solution)/shard_map/ppermute | solution.py:32
  79.0 10.4 %collective-permute-start.20 = (bf16[512,256]{1,0:T(8,128)(2,1)}, bf16[512,256]{1,0:T(8,128)(2,1)S(1)}, u32[]{:S(2)}, u32[]{:S(2)}) collective-permute-start(bf16[512,256]{1,0:T(8,128)(2,1)} %get-tuple-element.102), channel_id=1, source_target_pairs={{0,64},{1,65},{32,96},{33,97},{64,0},{65,1},{96,32},{97,33},{128,1... | collective-permute-start | bytes 786440 | tf_op jit(solution)/shard_map/ppermute | solution.py:32
  80.7 20.8 %all-to-all-start.2 = ((bf16[8,4,16,256]{3,2,1,0:T(8,128)(2,1)}), bf16[8,4,16,256]{3,2,1,0:T(8,128)(2,1)S(1)}, u32[]{:S(2)}, u32[]{:S(2)}) async-start(bf16[8,4,16,256]{3,2,1,0:T(8,128)(2,1)} %shard_map.59), calls=%async_computation.2 | async-start | bytes 524288 | tf_op jit(solution)/shard_map/all_to_all | solution.py:350
  85.8 6.4 %collective-permute-start.17 = (bf16[256,256]{1,0:T(8,128)(2,1)S(1)}, bf16[256,256]{1,0:T(8,128)(2,1)S(1)}, u32[]{:S(2)}, u32[]{:S(2)}) collective-permute-start(bf16[256,256]{1,0:T(8,128)(2,1)S(1)} %get-tuple-element.97), channel_id=1, source_target_pairs={{0,192},{1,193},{32,224},{33,225},{64,128},{65,129},{96,160},{97,1... | collective-permute-start | bytes 393224 | tf_op jit(solution)/shard_map/ppermute | solution.py:32
  89.6 6.6 %collective-permute-start.22 = (bf16[256,256]{1,0:T(8,128)(2,1)S(1)}, bf16[256,256]{1,0:T(8,128)(2,1)S(1)}, u32[]{:S(2)}, u32[]{:S(2)}) collective-permute-start(bf16[256,256]{1,0:T(8,128)(2,1)S(1)} %get-tuple-element.105), channel_id=1, source_target_pairs={{0,33},{1,32},{32,1},{33,0},{64,97},{65,96},{96,65},{97,64},{128,1... | collective-permute-start | bytes 393224 | tf_op jit(solution)/shard_map/ppermute | solution.py:32
  (3 other events, 28.6 us)

commit v7 on v6

--- a/solution.py
+++ b/solution.py
@@ -79,9 +79,7 @@
         spread_ref[peer] = own
 
 
-def embeddings_kernel(
-    code_ref, own_ref, other_ref, z_t_ref, local_ref, outgoing_ref, near_code_ref, semaphores
-):
+def stage_kernel(code_ref, near_code_ref, semaphores):
     n = semaphores.shape[0]
     step = code_ref.shape[0] // n
     copies = []
@@ -91,6 +89,11 @@
             pltpu.make_async_copy(code_ref.at[here], near_code_ref.at[here], semaphores.at[index])
         )
         copies[-1].start()
+    for copy in copies:
+        copy.wait()
+
+
+def embeddings_kernel(own_ref, other_ref, z_t_ref, local_ref, outgoing_ref):
     first = lax.axis_index("core") == 0
     own, other = own_ref[...].astype(f32), other_ref[...].astype(f32)
     raw = jnp.stack([jnp.where(first, own, other), jnp.where(first, other, own)], axis=1)
@@ -102,14 +105,12 @@
     local_ref[...] = local.reshape(-1, features)
     outgoing_ref[...] = (z[:, 0] + local).reshape(-1, features)
     z_t_ref[...] = z.reshape(-1, features).T.astype(bf16)
-    for copy in copies:
-        copy.wait()
 
 
 def scores_kernel(*refs, distance, n_before):
     z_t_ref, code_ref, *raw_refs = refs[:4]
     own_before, acc_before = refs[4 : 4 + n_before], refs[4 + n_before : 4 + 2 * n_before]
-    exp_a_ref, exp_b_ref, soft_ref, own_ref, total_ref = refs[4 + 2 * n_before : 9 + 2 * n_before]
+    exp_a_ref, exp_b_ref, soft_ref, own_ref, total_ref = refs[-5:]
     rows = z_t_ref.shape[1]
     soft = own = acc = None
     add = lambda a, b: b if a is None else a + b
@@ -124,10 +125,12 @@
     soft_ref[...] = soft
     for before in own_before:
         own = own + before[...]
-    own_ref[...] = own
     if not n_before:
+        own_ref[...] = own
         total_ref[...] = acc
         return
+    own_ref[0] = own
+    own_ref[1] = refs[4 + 2 * n_before][...]
     for before in acc_before:
         acc = acc + before[...]
     totals = jnp.sum(acc, axis=0, keepdims=True)
@@ -142,7 +145,7 @@
         totals_ref, z_t_ref, local_ref, incoming_ref = refs[:4]
         weights = row_weights(totals_ref, crops, own_images)
         zw = (z_t_ref[...].astype(f32) * weights).astype(bf16)
-        target = (local_ref[...] + incoming_ref[...]).astype(bf16)
+        target = (local_ref[...] + incoming_ref[1]).astype(bf16)
         refs[-2][...] = zw
         refs[-1][...] = target
         refs = refs[4:-2]
@@ -164,8 +167,8 @@
     weights = row_weights(totals_ref, crops, own_images)
     n_z, _, _, features = kept_ref.shape
     soft = (soft * weights).T.reshape(n_z, 2, crops, own_images, features)
-    own = own_ref[...].reshape(n_z, 2, own_images, features)
-    other = other_ref[...].reshape(n_z, 2, own_images, features)
+    own = own_ref[0].reshape(n_z, 2, own_images, features)
+    other = other_ref[0].reshape(n_z, 2, own_images, features)
     first = lax.axis_index("core") == 0
     for crop in range(crops):
         assigned = other if crop == 0 else own + other
@@ -278,38 +281,37 @@
         for kind in kinds:
             gathered[d].append(exchange(halves[kind], 1 - kind, d))
 
-    z_t, local_sum, outgoing, code = call(
+    code = call(
+        stage_kernel,
+        pltpu.VMEM(code.shape, code.dtype),
+        code,
+        held=(0,),
+        scratch=[pltpu.SemaphoreType.DMA((8,))],
+    )
+    z_t, local_sum, outgoing = call(
         embeddings_kernel,
-        (
-            shape(features, rows, dtype=bf16),
-            shape(images, features),
-            shape(images, features),
-            pltpu.VMEM(code.shape, code.dtype),
-        ),
-        code, *(
+        (shape(features, rows, dtype=bf16), shape(images, features), shape(images, features)),
+        *(
             each.reshape(n_proto // 2, crops, own_images, features)
             for each in (own_core, other_core)
         ),
-        held=(0,),
-        scratch=[pltpu.SemaphoreType.DMA((8,))],
     )
 
     exponents = {}
     soft, own_sums, sums = [], [], []
     for d in (0, *arrivals):
-        before = (*own_sums, *sums) if d == arrivals[-1] else ()
+        before = (*own_sums, *sums, outgoing) if d == arrivals[-1] else ()
         total_dims = (n_proto, rows // 128, 128) if before else (8, rows)
+        own_dims = (2, images, features) if before else (images, features)
         *exponents[d], soft_part, own_term, totals = call(
             functools.partial(scores_kernel, distance=d, n_before=len(before) // 2),
             [shape(side * half, rows, dtype=bf16)] * 2
-            + [shape(features, rows), shape(images, features), shape(*total_dims)],
+            + [shape(features, rows), shape(*own_dims), shape(*total_dims)],
             z_t, code, *gathered[d], *before,
         )
         soft.append(soft_part)
         own_sums.append(own_term)
         sums.append(totals)
-    totals, outgoing = lax.optimization_barrier((totals, outgoing))
-    incoming = swapped(outgoing)
     other_term = swapped(own_term)
     totals = lax.all_to_all(totals, block, 0, 0)
 
@@ -323,7 +325,7 @@
             ),
             [shape(side * half, features, dtype=bf16 if d else f32)] * 2
             + [shape(features, rows, dtype=bf16), shape(images, features, dtype=bf16)] * first,
-            code, *((totals, z_t, local_sum, incoming) if first else (zw, target)),
+            code, *((totals, z_t, local_sum, other_term) if first else (zw, target)),
             *exponents[d],
         )
         parts = outs[:2]

time: 103 us -> 102 us (level)
  waiting for transfers between devices: 26.8 us -> 25.5 us
    ppermute x20, waiting for transfers between devices: 25.1 us -> 22.5 us  [exchange(): lax.ppermute(value, owners, [(owner, owner ^ mask) for owner in range(sid...]
    ppermute x2 -> x1, starting transfers between devices: 2.11 us -> 0.09 us  [swapped(): return lax.ppermute(value, 'crop', [(0, 1), (1, 0)])]
    ppermute x2 -> x1, waiting for transfers between devices: 0.01 us -> 1.26 us  [swapped(): return lax.ppermute(value, 'crop', [(0, 1), (1, 0)])]
    all_to_all x1, starting transfers between devices: 4.98 us -> 6.02 us  [on_device(): row_parts = lax.all_to_all(row_parts, 'z', 0, 0)]
    pallas_call x18 -> x19, Pallas kernels: 18.8 us -> 19.3 us  [call(): pl.pallas_call(kernel, out_shape=out_shape, in_specs=[there if i in (*fet...]
  transfers between devices with their start and end apart: 26 -> 25, of which waited for: 11 -> 12; matrix products, arithmetic and copies ran while one was open for 0% -> 0% of each run, Pallas kernels for 14% -> 14%
where the time goes in v7:
time: 102 us; the launch traced here: 101 us
  starting transfers between devices  43.9 us (43%)
  waiting for transfers between devices  25.5 us (25%)
  Pallas kernels  19.3 us (19%)
  blocking collectives  11.8 us (12%)
    ppermute x20, starting transfers between devices, exchange(): lax.ppermute(value, owners, [(owner, owner ^ mask) for owner in range(sid...  29.1 us
    ppermute x20, waiting for transfers between devices, exchange(): lax.ppermute(value, owners, [(owner, owner ^ mask) for owner in range(sid...  22.5 us
    pallas_call x19, Pallas kernels, call(): pl.pallas_call(kernel, out_shape=out_shape, in_specs=[there if i in (*fet...  19.3 us
    all_to_all x1, blocking collectives, on_device(): totals = lax.all_to_all(totals, block, 0, 0)  11.8 us
    all_to_all x1, starting transfers between devices, on_device(): own_core = lax.all_to_all(spread_emb, 'z', 0, 0)  8.57 us
    all_to_all x1, starting transfers between devices, on_device(): row_parts = lax.all_to_all(row_parts, 'z', 0, 0)  6.02 us
  transfers between devices with their start and end apart: 25, of which 12 were waited for; matrix products, arithmetic and copies ran while one was open for 0% of the time, Pallas kernels for 14%

profile of v7, /device:TPU:32, one launch (start us, length us, event | category | flops | bytes accessed | tf_op | source)
XLA Modules:
  0.0 101.3 jit_solution(7350715113901414028)
XLA Ops:
  0.6 1.7 %shard_map.50 = (bf16[128,256]{1,0:T(8,128)(2,1)S(1)}, bf16[128,256]{1,0:T(8,128)(2,1)S(1)}, bf16[4,16,256]{2,1,0:T(8,128)(2,1)S(1)}, bf16[8,64,256]{2,1,0:T(8,128)(2,1)}) custom-call(bf16[256,256]{1,0:T(8,128)(2,1)} %bitcast.10, bf16[16,4,256]{2,1,0:T(4,128)(2,1)} %bitcast.16), custom_call_target="tpu_custom_call" | custom-call | tf_op jit(solution)/shard_map/pallas_call | solution.py:230
  3.9 8.6 %all-to-all-start = ((bf16[8,64,256]{2,1,0:T(8,128)(2,1)}), bf16[8,64,256]{2,1,0:T(8,128)(2,1)S(1)}, u32[]{:S(2)}, u32[]{:S(2)}) async-start(bf16[8,64,256]{2,1,0:T(8,128)(2,1)} %get-tuple-element.52), calls=%async_computation | async-start | bytes 524288 | tf_op jit(solution)/shard_map/all_to_all | solution.py:276
  14.0 2.2 %collective-permute-start.5 = (bf16[256,256]{1,0:T(8,128)(2,1)S(1)}, bf16[256,256]{1,0:T(8,128)(2,1)S(1)}, u32[]{:S(2)}, u32[]{:S(2)}) collective-permute-start(bf16[256,256]{1,0:T(8,128)(2,1)S(1)} %pad_maximum_fusion.1), channel_id=1, source_target_pairs={{0,33},{1,32},{32,1},{33,0},{64,97},{65,96},{96,65},{97,64},{128,1... | collective-permute-start | bytes 393224 | tf_op jit(solution)/shard_map/ppermute | solution.py:32
  16.3 4.1 %collective-permute-done.5 = bf16[256,256]{1,0:T(8,128)(2,1)S(1)} collective-permute-done((bf16[256,256]{1,0:T(8,128)(2,1)S(1)}, bf16[256,256]{1,0:T(8,128)(2,1)S(1)}, u32[]{:S(2)}, u32[]{:S(2)}) %collective-permute-start.5) | collective-permute-done | bytes 131104 | tf_op jit(solution)/shard_map/ppermute | solution.py:32
  20.9 1.7 %all-to-all-done = bf16[8,64,256]{2,1,0:T(8,128)(2,1)S(1)} async-done(((bf16[8,64,256]{2,1,0:T(8,128)(2,1)}), bf16[8,64,256]{2,1,0:T(8,128)(2,1)S(1)}, u32[]{:S(2)}, u32[]{:S(2)}) %all-to-all-start) | async-done | bytes 262176 | tf_op jit(solution)/shard_map/all_to_all | solution.py:276
  22.6 3.1 %collective-permute-start.2 = (bf16[256,256]{1,0:T(8,128)(2,1)S(1)}, bf16[256,256]{1,0:T(8,128)(2,1)S(1)}, u32[]{:S(2)}, u32[]{:S(2)}) collective-permute-start(bf16[256,256]{1,0:T(8,128)(2,1)S(1)} %pad_maximum_fusion), channel_id=1, source_target_pairs={{0,192},{1,193},{32,224},{33,225},{64,128},{65,129},{96,160},{97,1... | collective-permute-start | bytes 393224 | tf_op jit(solution)/shard_map/ppermute | solution.py:32
  25.7 4.2 %collective-permute-done.2 = bf16[256,256]{1,0:T(8,128)(2,1)S(1)} collective-permute-done((bf16[256,256]{1,0:T(8,128)(2,1)S(1)}, bf16[256,256]{1,0:T(8,128)(2,1)S(1)}, u32[]{:S(2)}, u32[]{:S(2)}) %collective-permute-start.2) | collective-permute-done | bytes 131104 | tf_op jit(solution)/shard_map/ppermute | solution.py:32
  30.5 1.9 %collective-permute-start.8 = (bf16[512,256]{1,0:T(8,128)(2,1)S(1)}, bf16[512,256]{1,0:T(8,128)(2,1)S(1)}, u32[]{:S(2)}, u32[]{:S(2)}) collective-permute-start(bf16[512,256]{1,0:T(8,128)(2,1)S(1)} %constant_dynamic-update-slice_fusion.3.refs_3_), channel_id=1, source_target_pairs={{0,128},{1,129},{32,160},{33,161},{64,192},{65,193},{96,224},{97,2... | collective-permute-start | bytes 786440 | tf_op jit(solution)/shard_map/ppermute | solution.py:32
  32.4 3.0 %collective-permute-start.7 = (bf16[512,256]{1,0:T(8,128)(2,1)S(1)}, bf16[512,256]{1,0:T(8,128)(2,1)S(1)}, u32[]{:S(2)}, u32[]{:S(2)}) collective-permute-start(bf16[512,256]{1,0:T(8,128)(2,1)S(1)} %constant_dynamic-update-slice_fusion.refs_2_), channel_id=1, source_target_pairs={{0,32},{1,33},{32,0},{33,1},{64,96},{65,97},{96,64},{97,65},{128,1... | collective-permute-start | bytes 786440 | tf_op jit(solution)/shard_map/ppermute | solution.py:32
  39.9 1.8 %shard_map.53 = (bf16[512,1024]{1,0:T(8,128)(2,1)S(1)}, bf16[512,1024]{1,0:T(8,128)(2,1)S(1)}, f32[256,1024]{1,0:T(8,128)S(1)}, f32[256,256]{1,0:T(8,128)S(1)}, f32[8,1024]{1,0:T(8,128)S(1)}) custom-call(bf16[256,1024]{1,0:T(8,128)(2,1)S(1)} %get-tuple-element.53.refs_0_.refs_2_, bf16[256,4096]{1,0:T(8,128)(2,1)S(1)} %shard_map.52.refs_1_.refs_0_, ...), custom_call_target="tpu_custom_call" | custom-call | tf_op jit(solution)/shard_map/pallas_call | solution.py:230
  41.7 1.8 %shard_map.55 = (bf16[512,1024]{1,0:T(8,128)(2,1)S(1)}, bf16[512,1024]{1,0:T(8,128)(2,1)S(1)}, f32[256,1024]{1,0:T(8,128)S(1)}, f32[256,256]{1,0:T(8,128)S(1)}, f32[8,1024]{1,0:T(8,128)S(1)}) custom-call(bf16[256,1024]{1,0:T(8,128)(2,1)S(1)} %get-tuple-element.53.refs_0_.refs_2_, bf16[256,4096]{1,0:T(8,128)(2,1)S(1)} %shard_map.52.refs_1_.refs_0_, ...), custom_call_target="tpu_custom_call" | custom-call | tf_op jit(solution)/shard_map/pallas_call | solution.py:230
  43.5 1.7 %collective-permute-done.7.refs_2_ = bf16[512,256]{1,0:T(8,128)(2,1)S(1)} collective-permute-done((bf16[512,256]{1,0:T(8,128)(2,1)S(1)}, bf16[512,256]{1,0:T(8,128)(2,1)S(1)}, u32[]{:S(2)}, u32[]{:S(2)}) %collective-permute-start.7) | collective-permute-done | bytes 262176 | tf_op jit(solution)/shard_map/ppermute | solution.py:32
  45.2 1.8 %shard_map.54 = (bf16[512,1024]{1,0:T(8,128)(2,1)S(1)}, bf16[512,1024]{1,0:T(8,128)(2,1)S(1)}, f32[256,1024]{1,0:T(8,128)S(1)}, f32[256,256]{1,0:T(8,128)S(1)}, f32[8,1024]{1,0:T(8,128)S(1)}) custom-call(bf16[256,1024]{1,0:T(8,128)(2,1)S(1)} %get-tuple-element.53.refs_0_.refs_2_, bf16[256,4096]{1,0:T(8,128)(2,1)S(1)} %shard_map.52.refs_1_.refs_0_, ...), custom_call_target="tpu_custom_call" | custom-call | tf_op jit(solution)/shard_map/pallas_call | solution.py:230
  46.9 3.0 %collective-permute-done.3.refs_2_ = bf16[512,256]{1,0:T(8,128)(2,1)S(1)} collective-permute-done((bf16[512,256]{1,0:T(8,128)(2,1)S(1)}, bf16[512,256]{1,0:T(8,128)(2,1)S(1)}, u32[]{:S(2)}, u32[]{:S(2)}) %collective-permute-start.3) | collective-permute-done | bytes 262176 | tf_op jit(solution)/shard_map/ppermute | solution.py:32
  49.9 1.8 %shard_map.56 = (bf16[512,1024]{1,0:T(8,128)(2,1)S(1)}, bf16[512,1024]{1,0:T(8,128)(2,1)S(1)}, f32[256,1024]{1,0:T(8,128)S(1)}, f32[2,256,256]{2,1,0:T(8,128)S(1)}, f32[16,8,128]{2,1,0:T(8,128)S(1)}) custom-call(bf16[256,1024]{1,0:T(8,128)(2,1)S(1)} %get-tuple-element.53.refs_0_.refs_2_, bf16[256,4096]{1,0:T(8,128)(2,1)S(1)} %shard_map.52.refs_1_.refs_0_, ...), custom_call_target="tpu_custom_call" | custom-call | tf_op jit(solution)/shard_map/pallas_call | solution.py:230
  51.8 11.8 %all_to_all.15.totals_ref.refs_1_ = f32[16,8,128]{2,1,0:T(8,128)S(1)} all-to-all(f32[16,8,128]{2,1,0:T(8,128)S(1)} %get-tuple-element.63), channel_id=1, replica_groups=mesh['dp'=8,'z'=8,'core'=2,'crop'=2] {'z','core'}, dimensions={0} | all-to-all | bytes 131072 | tf_op jit(solution)/shard_map/all_to_all | solution.py:316
  69.5 2.1 %collective-permute-start.15 = (bf16[512,256]{1,0:T(8,128)(2,1)}, bf16[512,256]{1,0:T(8,128)(2,1)S(1)}, u32[]{:S(2)}, u32[]{:S(2)}) collective-permute-start(bf16[512,256]{1,0:T(8,128)(2,1)} %get-tuple-element.89), channel_id=1, source_target_pairs={{0,33},{1,32},{32,1},{33,0},{64,97},{65,96},{96,65},{97,64},{128,1... | collective-permute-start | bytes 786440 | tf_op jit(solution)/shard_map/ppermute | solution.py:32
  71.6 1.6 %shard_map.62 = (bf16[512,256]{1,0:T(8,128)(2,1)}, bf16[512,256]{1,0:T(8,128)(2,1)}) custom-call(bf16[256,4096]{1,0:T(8,128)(2,1)S(1)} %shard_map.52.refs_1_.refs_0_, bf16[256,1024]{1,0:T(8,128)(2,1)S(1)} %get-tuple-element.73.refs_1_, bf16[256,256]{1,0:T(8,128)(2,1)S(1)} %get-tuple-element.74.refs_2_, bf16[512,1024]{1,0:T(8,128)(2,1)S(1)} %get-tuple-element.84.refs_3_, ...), custom_call_target="tpu_custom_call" | custom-call | tf_op jit(solution)/shard_map/pallas_call | solution.py:230
  73.2 2.4 %collective-permute-start.18 = (bf16[512,256]{1,0:T(8,128)(2,1)S(1)}, bf16[512,256]{1,0:T(8,128)(2,1)S(1)}, u32[]{:S(2)}, u32[]{:S(2)}) collective-permute-start(bf16[512,256]{1,0:T(8,128)(2,1)S(1)} %get-tuple-element.95), channel_id=1, source_target_pairs={{0,128},{1,129},{32,160},{33,161},{64,192},{65,193},{96,224},{97,2... | collective-permute-start | bytes 786440 | tf_op jit(solution)/shard_map/ppermute | solution.py:32
  79.4 6.0 %all-to-all-start.2 = ((bf16[8,4,16,256]{3,2,1,0:T(8,128)(2,1)}), bf16[8,4,16,256]{3,2,1,0:T(8,128)(2,1)S(1)}, u32[]{:S(2)}, u32[]{:S(2)}) async-start(bf16[8,4,16,256]{3,2,1,0:T(8,128)(2,1)} %shard_map.60), calls=%async_computation.2 | async-start | bytes 524288 | tf_op jit(solution)/shard_map/all_to_all | solution.py:352
  85.5 2.2 %collective-permute-start.16 = (bf16[256,256]{1,0:T(8,128)(2,1)S(1)}, bf16[256,256]{1,0:T(8,128)(2,1)S(1)}, u32[]{:S(2)}, u32[]{:S(2)}) collective-permute-start(bf16[256,256]{1,0:T(8,128)(2,1)S(1)} %get-tuple-element.91), channel_id=1, source_target_pairs={{0,192},{1,193},{32,224},{33,225},{64,128},{65,129},{96,160},{97,1... | collective-permute-start | bytes 393224 | tf_op jit(solution)/shard_map/ppermute | solution.py:32
  89.7 2.1 %collective-permute-done.16.part_ref = bf16[256,256]{1,0:T(8,128)(2,1)S(1)} collective-permute-done((bf16[256,256]{1,0:T(8,128)(2,1)S(1)}, bf16[256,256]{1,0:T(8,128)(2,1)S(1)}, u32[]{:S(2)}, u32[]{:S(2)}) %collective-permute-start.16) | collective-permute-done | bytes 131104 | tf_op jit(solution)/shard_map/ppermute | solution.py:32
  92.0 3.1 %collective-permute-done.21.part_ref = bf16[256,256]{1,0:T(8,128)(2,1)S(1)} collective-permute-done((bf16[256,256]{1,0:T(8,128)(2,1)S(1)}, bf16[256,256]{1,0:T(8,128)(2,1)S(1)}, u32[]{:S(2)}, u32[]{:S(2)}) %collective-permute-start.21) | collective-permute-done | bytes 131104 | tf_op jit(solution)/shard_map/ppermute | solution.py:32
  96.2 3.3 %collective-permute-done.22.part_b_ref = bf16[128,256]{1,0:T(8,128)(2,1)S(1)} collective-permute-done((bf16[128,256]{1,0:T(8,128)(2,1)S(1)}, bf16[128,256]{1,0:T(8,128)(2,1)S(1)}, u32[]{:S(2)}, u32[]{:S(2)}) %collective-permute-start.22) | collective-permute-done | bytes 65568 | tf_op jit(solution)/shard_map/ppermute | solution.py:32
  (55 shorter events, 23.8 us)
Async XLA Ops:
  2.3 11.7 %collective-permute-start.4 = (bf16[128,256]{1,0:T(8,128)(2,1)S(1)}, bf16[128,256]{1,0:T(8,128)(2,1)S(1)}, u32[]{:S(2)}, u32[]{:S(2)}) collective-permute-start(bf16[128,256]{1,0:T(8,128)(2,1)S(1)} %get-tuple-element.55), channel_id=1, source_target_pairs={{0,1},{1,0},{32,33},{33,32},{64,65},{65,64},{96,97},{97,96},{128,1... | collective-permute-start | bytes 196616 | tf_op jit(solution)/shard_map/ppermute | solution.py:32
  3.9 18.7 %all-to-all-start = ((bf16[8,64,256]{2,1,0:T(8,128)(2,1)}), bf16[8,64,256]{2,1,0:T(8,128)(2,1)S(1)}, u32[]{:S(2)}, u32[]{:S(2)}) async-start(bf16[8,64,256]{2,1,0:T(8,128)(2,1)} %get-tuple-element.52), calls=%async_computation | async-start | bytes 524288 | tf_op jit(solution)/shard_map/all_to_all | solution.py:276
  12.5 10.1 %collective-permute-start.1 = (bf16[128,256]{1,0:T(8,128)(2,1)S(1)}, bf16[128,256]{1,0:T(8,128)(2,1)S(1)}, u32[]{:S(2)}, u32[]{:S(2)}) collective-permute-start(bf16[128,256]{1,0:T(8,128)(2,1)S(1)} %get-tuple-element.54), channel_id=1, source_target_pairs={{0,64},{1,65},{32,96},{33,97},{64,0},{65,1},{96,32},{97,33},{128,1... | collective-permute-start | bytes 196616 | tf_op jit(solution)/shard_map/ppermute | solution.py:32
  14.0 6.3 %collective-permute-start.5 = (bf16[256,256]{1,0:T(8,128)(2,1)S(1)}, bf16[256,256]{1,0:T(8,128)(2,1)S(1)}, u32[]{:S(2)}, u32[]{:S(2)}) collective-permute-start(bf16[256,256]{1,0:T(8,128)(2,1)S(1)} %pad_maximum_fusion.1), channel_id=1, source_target_pairs={{0,33},{1,32},{32,1},{33,0},{64,97},{65,96},{96,65},{97,64},{128,1... | collective-permute-start | bytes 393224 | tf_op jit(solution)/shard_map/ppermute | solution.py:32
  20.3 15.1 %collective-permute-start.10 = (bf16[512,256]{1,0:T(8,128)(2,1)S(1)}, bf16[512,256]{1,0:T(8,128)(2,1)S(1)}, u32[]{:S(2)}, u32[]{:S(2)}) collective-permute-start(bf16[512,256]{1,0:T(8,128)(2,1)S(1)} %constant_dynamic-update-slice_fusion.3.refs_3_), channel_id=1, source_target_pairs={{0,64},{1,65},{32,96},{33,97},{64,0},{65,1},{96,32},{97,33},{128,1... | collective-permute-start | bytes 786440 | tf_op jit(solution)/shard_map/ppermute | solution.py:32
  22.6 13.9 %collective-permute-start = (bf16[8,64,256]{2,1,0:T(8,128)(2,1)S(1)}, bf16[8,64,256]{2,1,0:T(8,128)(2,1)S(1)}, u32[]{:S(2)}, u32[]{:S(2)}) collective-permute-start(bf16[8,64,256]{2,1,0:T(8,128)(2,1)S(1)} %all-to-all-done), channel_id=1, source_target_pairs={{0,2},{2,0},{1,3},{3,1},{4,6},{6,4},{5,7},{7,5},{8,10},{10,8},{9,1... | collective-permute-start | bytes 786440 | tf_op jit(solution)/shard_map/ppermute | solution.py:277
  22.6 7.3 %collective-permute-start.2 = (bf16[256,256]{1,0:T(8,128)(2,1)S(1)}, bf16[256,256]{1,0:T(8,128)(2,1)S(1)}, u32[]{:S(2)}, u32[]{:S(2)}) collective-permute-start(bf16[256,256]{1,0:T(8,128)(2,1)S(1)} %pad_maximum_fusion), channel_id=1, source_target_pairs={{0,192},{1,193},{32,224},{33,225},{64,128},{65,129},{96,160},{97,1... | collective-permute-start | bytes 393224 | tf_op jit(solution)/shard_map/ppermute | solution.py:32
  29.9 11.8 %collective-permute-start.9 = (bf16[512,256]{1,0:T(8,128)(2,1)S(1)}, bf16[512,256]{1,0:T(8,128)(2,1)S(1)}, u32[]{:S(2)}, u32[]{:S(2)}) collective-permute-start(bf16[512,256]{1,0:T(8,128)(2,1)S(1)} %constant_dynamic-update-slice_fusion.refs_2_), channel_id=1, source_target_pairs={{0,1},{1,0},{32,33},{33,32},{64,65},{65,64},{96,97},{97,96},{128,1... | collective-permute-start | bytes 786440 | tf_op jit(solution)/shard_map/ppermute | solution.py:32
  30.5 12.9 %collective-permute-start.8 = (bf16[512,256]{1,0:T(8,128)(2,1)S(1)}, bf16[512,256]{1,0:T(8,128)(2,1)S(1)}, u32[]{:S(2)}, u32[]{:S(2)}) collective-permute-start(bf16[512,256]{1,0:T(8,128)(2,1)S(1)} %constant_dynamic-update-slice_fusion.3.refs_3_), channel_id=1, source_target_pairs={{0,128},{1,129},{32,160},{33,161},{64,192},{65,193},{96,224},{97,2... | collective-permute-start | bytes 786440 | tf_op jit(solution)/shard_map/ppermute | solution.py:32
  32.4 12.7 %collective-permute-start.7 = (bf16[512,256]{1,0:T(8,128)(2,1)S(1)}, bf16[512,256]{1,0:T(8,128)(2,1)S(1)}, u32[]{:S(2)}, u32[]{:S(2)}) collective-permute-start(bf16[512,256]{1,0:T(8,128)(2,1)S(1)} %constant_dynamic-update-slice_fusion.refs_2_), channel_id=1, source_target_pairs={{0,32},{1,33},{32,0},{33,1},{64,96},{65,97},{96,64},{97,65},{128,1... | collective-permute-start | bytes 786440 | tf_op jit(solution)/shard_map/ppermute | solution.py:32
  35.5 11.5 %collective-permute-start.6 = (bf16[512,256]{1,0:T(8,128)(2,1)S(1)}, bf16[512,256]{1,0:T(8,128)(2,1)S(1)}, u32[]{:S(2)}, u32[]{:S(2)}) collective-permute-start(bf16[512,256]{1,0:T(8,128)(2,1)S(1)} %constant_dynamic-update-slice_fusion.3.refs_3_), channel_id=1, source_target_pairs={{0,192},{1,193},{32,224},{33,225},{64,128},{65,129},{96,160},{97,1... | collective-permute-start | bytes 786440 | tf_op jit(solution)/shard_map/ppermute | solution.py:32
  36.5 13.4 %collective-permute-start.3 = (bf16[512,256]{1,0:T(8,128)(2,1)S(1)}, bf16[512,256]{1,0:T(8,128)(2,1)S(1)}, u32[]{:S(2)}, u32[]{:S(2)}) collective-permute-start(bf16[512,256]{1,0:T(8,128)(2,1)S(1)} %constant_dynamic-update-slice_fusion.refs_2_), channel_id=1, source_target_pairs={{0,33},{1,32},{32,1},{33,0},{64,97},{65,96},{96,65},{97,64},{128,1... | collective-permute-start | bytes 786440 | tf_op jit(solution)/shard_map/ppermute | solution.py:32
  51.7 13.1 %collective-permute-start.11 = (f32[2,256,256]{2,1,0:T(8,128)S(1)}, f32[2,256,256]{2,1,0:T(8,128)S(1)}, u32[]{:S(2)}, u32[]{:S(2)}) collective-permute-start(f32[2,256,256]{2,1,0:T(8,128)S(1)} %get-tuple-element.64.own_ref), channel_id=1, source_target_pairs={{0,1},{1,0},{2,3},{3,2},{4,5},{5,4},{6,7},{7,6},{8,9},{9,8},{10,11... | collective-permute-start | bytes 1572872 | tf_op jit(solution)/shard_map/ppermute | solution.py:23
  65.2 10.4 %collective-permute-start.12 = (bf16[8,4,16,256]{3,2,1,0:T(8,128)(2,1)S(1)}, bf16[8,4,16,256]{3,2,1,0:T(8,128)(2,1)S(1)}, u32[]{:S(2)}, u32[]{:S(2)}) collective-permute-start(bf16[8,4,16,256]{3,2,1,0:T(8,128)(2,1)S(1)} %get-tuple-element.80), channel_id=1, source_target_pairs={{0,2},{2,0},{1,3},{3,1},{4,6},{6,4},{5,7},{7,5},{8,10},{10,8},{9,1... | collective-permute-start | bytes 786440 | tf_op jit(solution)/shard_map/ppermute | solution.py:346
  66.3 10.6 %collective-permute-start.13 = (bf16[512,256]{1,0:T(8,128)(2,1)S(1)}, bf16[512,256]{1,0:T(8,128)(2,1)S(1)}, u32[]{:S(2)}, u32[]{:S(2)}) collective-permute-start(bf16[512,256]{1,0:T(8,128)(2,1)S(1)} %get-tuple-element.83), channel_id=1, source_target_pairs={{0,32},{1,33},{32,0},{33,1},{64,96},{65,97},{96,64},{97,65},{128,1... | collective-permute-start | bytes 786440 | tf_op jit(solution)/shard_map/ppermute | solution.py:32
  69.5 15.9 %collective-permute-start.15 = (bf16[512,256]{1,0:T(8,128)(2,1)}, bf16[512,256]{1,0:T(8,128)(2,1)S(1)}, u32[]{:S(2)}, u32[]{:S(2)}) collective-permute-start(bf16[512,256]{1,0:T(8,128)(2,1)} %get-tuple-element.89), channel_id=1, source_target_pairs={{0,33},{1,32},{32,1},{33,0},{64,97},{65,96},{96,65},{97,64},{128,1... | collective-permute-start | bytes 786440 | tf_op jit(solution)/shard_map/ppermute | solution.py:32
  73.2 12.2 %collective-permute-start.14 = (bf16[512,256]{1,0:T(8,128)(2,1)}, bf16[512,256]{1,0:T(8,128)(2,1)S(1)}, u32[]{:S(2)}, u32[]{:S(2)}) collective-permute-start(bf16[512,256]{1,0:T(8,128)(2,1)} %get-tuple-element.86), channel_id=1, source_target_pairs={{0,1},{1,0},{32,33},{33,32},{64,65},{65,64},{96,97},{97,96},{128,1... | collective-permute-start | bytes 786440 | tf_op jit(solution)/shard_map/ppermute | solution.py:32
  73.2 14.5 %collective-permute-start.18 = (bf16[512,256]{1,0:T(8,128)(2,1)S(1)}, bf16[512,256]{1,0:T(8,128)(2,1)S(1)}, u32[]{:S(2)}, u32[]{:S(2)}) collective-permute-start(bf16[512,256]{1,0:T(8,128)(2,1)S(1)} %get-tuple-element.95), channel_id=1, source_target_pairs={{0,128},{1,129},{32,160},{33,161},{64,192},{65,193},{96,224},{97,2... | collective-permute-start | bytes 786440 | tf_op jit(solution)/shard_map/ppermute | solution.py:32
  75.7 12.7 %collective-permute-start.20 = (bf16[512,256]{1,0:T(8,128)(2,1)}, bf16[512,256]{1,0:T(8,128)(2,1)S(1)}, u32[]{:S(2)}, u32[]{:S(2)}) collective-permute-start(bf16[512,256]{1,0:T(8,128)(2,1)} %get-tuple-element.97), channel_id=1, source_target_pairs={{0,192},{1,193},{32,224},{33,225},{64,128},{65,129},{96,160},{97,1... | collective-permute-start | bytes 786440 | tf_op jit(solution)/shard_map/ppermute | solution.py:32
  76.9 11.5 %collective-permute-start.19 = (bf16[512,256]{1,0:T(8,128)(2,1)}, bf16[512,256]{1,0:T(8,128)(2,1)S(1)}, u32[]{:S(2)}, u32[]{:S(2)}) collective-permute-start(bf16[512,256]{1,0:T(8,128)(2,1)} %get-tuple-element.96), channel_id=1, source_target_pairs={{0,64},{1,65},{32,96},{33,97},{64,0},{65,1},{96,32},{97,33},{128,1... | collective-permute-start | bytes 786440 | tf_op jit(solution)/shard_map/ppermute | solution.py:32
  79.4 21.1 %all-to-all-start.2 = ((bf16[8,4,16,256]{3,2,1,0:T(8,128)(2,1)}), bf16[8,4,16,256]{3,2,1,0:T(8,128)(2,1)S(1)}, u32[]{:S(2)}, u32[]{:S(2)}) async-start(bf16[8,4,16,256]{3,2,1,0:T(8,128)(2,1)} %shard_map.60), calls=%async_computation.2 | async-start | bytes 524288 | tf_op jit(solution)/shard_map/all_to_all | solution.py:352
  85.5 6.3 %collective-permute-start.16 = (bf16[256,256]{1,0:T(8,128)(2,1)S(1)}, bf16[256,256]{1,0:T(8,128)(2,1)S(1)}, u32[]{:S(2)}, u32[]{:S(2)}) collective-permute-start(bf16[256,256]{1,0:T(8,128)(2,1)S(1)} %get-tuple-element.91), channel_id=1, source_target_pairs={{0,192},{1,193},{32,224},{33,225},{64,128},{65,129},{96,160},{97,1... | collective-permute-start | bytes 393224 | tf_op jit(solution)/shard_map/ppermute | solution.py:32
  88.5 6.6 %collective-permute-start.21 = (bf16[256,256]{1,0:T(8,128)(2,1)S(1)}, bf16[256,256]{1,0:T(8,128)(2,1)S(1)}, u32[]{:S(2)}, u32[]{:S(2)}) collective-permute-start(bf16[256,256]{1,0:T(8,128)(2,1)S(1)} %get-tuple-element.99), channel_id=1, source_target_pairs={{0,33},{1,32},{32,1},{33,0},{64,97},{65,96},{96,65},{97,64},{128,1... | collective-permute-start | bytes 393224 | tf_op jit(solution)/shard_map/ppermute | solution.py:32
  95.2 4.4 %collective-permute-start.22 = (bf16[128,256]{1,0:T(8,128)(2,1)S(1)}, bf16[128,256]{1,0:T(8,128)(2,1)S(1)}, u32[]{:S(2)}, u32[]{:S(2)}) collective-permute-start(bf16[128,256]{1,0:T(8,128)(2,1)S(1)} %get-tuple-element.101), channel_id=1, source_target_pairs={{0,1},{1,0},{32,33},{33,32},{64,65},{65,64},{96,97},{97,96},{128,1... | collective-permute-start | bytes 196616 | tf_op jit(solution)/shard_map/ppermute | solution.py:32
  (2 other events, 24.5 us)
